TPU v7x, 32 devices: a whole 2x2x4 slice. The times are simulated.
32 devices in a mesh: fsdp: 4 (over z), replica: 2 (over x), ctx: 4 (over y, core).
Axes of the slice: x: 2, y: 2, z: 4, core: 2. Of those that a mesh axis runs over, the one named last changes fastest.
Arguments:
- hidden_in: bfloat16 [8, 1088, 2048], P(('fsdp', 'replica'), 'ctx'), may hold values from -6 to 6
- memory_rows: bfloat16 [8, 50, 2048], P(('fsdp', 'replica')), may hold values from -6 to 6
- seg_len: int32 [8], P(('fsdp', 'replica')), may hold values from 519 to 1038, as said below
- out_grad: bfloat16 [8, 1088, 2048], P(('fsdp', 'replica'), 'ctx'), may hold values from -6 to 6
- first_gain: bfloat16 [2048], P('fsdp'), may hold values from 0.5 to 1.5
- first_shift: bfloat16 [2048], P('fsdp'), may hold values from -1 to 1
- qkv_weight: bfloat16 [2048, 6144], P('fsdp'), may hold values from -0.125 to 0.125
- query_bias: bfloat16 [2048], P('fsdp'), may hold values from -4 to 4
- value_bias: bfloat16 [2048], P('fsdp'), may hold values from -2.5 to 2.5
- out_weight: bfloat16 [2048, 2048], P('fsdp'), may hold values from -2 to 2
- out_bias: bfloat16 [2048], P('fsdp'), may hold values from -1 to 1
- second_gain: bfloat16 [2048], P('fsdp'), may hold values from 0.5 to 1.5
- second_shift: bfloat16 [2048], P('fsdp'), may hold values from -1 to 1
- up_weight: bfloat16 [2048, 8192], P('fsdp'), may hold values from -0.125 to 0.125
- up_bias: bfloat16 [8192], P('fsdp'), may hold values from -1 to 1
- down_weight: bfloat16 [8192, 2048], P('fsdp'), may hold values from -0.0625 to 0.0625
- down_bias: bfloat16 [2048], P('fsdp'), may hold values from -1 to 1
Outputs:
- output: bfloat16 [8, 1088, 2048], P(('fsdp', 'replica'), 'ctx')
- input_grad: float32 [8, 1088, 2048], P(('fsdp', 'replica'), 'ctx')
- memory_grad: float32 [8, 50, 2048], P(('fsdp', 'replica'))
- first_gain_grad: float32 [2048], P('fsdp')
- first_shift_grad: float32 [2048], P('fsdp')
- qkv_weight_grad: float32 [2048, 6144], P('fsdp')
- query_bias_grad: float32 [2048], P('fsdp')
- value_bias_grad: float32 [2048], P('fsdp')
- out_weight_grad: float32 [2048, 2048], P('fsdp')
- out_bias_grad: float32 [2048], P('fsdp')
- second_gain_grad: float32 [2048], P('fsdp')
- second_shift_grad: float32 [2048], P('fsdp')
- up_weight_grad: float32 [2048, 8192], P('fsdp')
- up_bias_grad: float32 [8192], P('fsdp')
- down_weight_grad: float32 [8192, 2048], P('fsdp')
- down_bias_grad: float32 [2048], P('fsdp')
Inputs may be any that keep to these rules, and one draw needn't show every extreme that they name: Positions seg_len to 1037 of a segment are padding that no query uses as a key.
All inputs are finite; a program needn't handle non-finite values.
Results may differ from a plain program's by a relative error of at most 0.015.
Values may be sent and summed in bfloat16 or wider, within the bound.
No kernel may reach another device: no remote copies, remote signals or barrier semaphores. Data moves between devices by JAX's collectives and lax.ppermute only.
A program may use at most 512 MiB of HBM per device.

v0:
```python
import jax
import jax.numpy as jnp
from jax import lax
from jax.sharding import PartitionSpec as P

D = 2048
HEADS = 32
HEAD_DIM = 64
SUMM = 50
SEQ_LEN = 1088
SEG = 1038


epsilon = 1e-05
masked = -1e30


def smooth_unit(values):
    return jax.nn.gelu(values, approximate=False)


def layer_norm(inputs, weight, offset):
    average = jnp.mean(inputs, axis=-1, keepdims=True)
    centred = inputs - average
    spread = jnp.mean(centred * centred, axis=-1, keepdims=True)
    inverse = lax.rsqrt(spread + epsilon)
    normal = centred * inverse
    return (normal * weight + offset, normal, inverse)


def norm_back(upstream, normal, inverse, weight):
    scaled = upstream * weight
    centre_term = jnp.mean(scaled, axis=-1, keepdims=True)
    slope_term = jnp.mean(scaled * normal, axis=-1, keepdims=True)
    return (
        inverse * (scaled - centre_term - normal * slope_term),
        jnp.sum(upstream * normal, axis=0),
        jnp.sum(upstream, axis=0),
    )


def across(left, right):
    return lax.dot_general(
        left, right, (((0,), (0,)), ((), ())), preferred_element_type=jnp.float32
    )


def against(left, right):
    return lax.dot_general(
        left, right, (((1,), (1,)), ((), ())), preferred_element_type=jnp.float32
    )


def head_slice(array, block_index, block_width, head_group):
    piece = lax.dynamic_slice_in_dim(array, block_index * block_width, block_width, 2)
    return piece.reshape(piece.shape[0], piece.shape[1], head_group, block_width // head_group)


def shards(
    hidden_in,
    memory_rows,
    seg_len,
    out_grad,
    first_gain,
    first_shift,
    qkv_weight,
    query_bias,
    value_bias,
    out_weight,
    out_bias,
    second_gain,
    second_shift,
    up_weight,
    up_bias,
    down_weight,
    down_bias,
):
    gathered = (
        lax.all_gather(first_gain, "fsdp", axis=0, tiled=True),
        lax.all_gather(first_shift, "fsdp", axis=0, tiled=True),
        lax.all_gather(qkv_weight, "fsdp", axis=0, tiled=True),
        lax.all_gather(query_bias, "fsdp", axis=0, tiled=True),
        lax.all_gather(value_bias, "fsdp", axis=0, tiled=True),
        lax.all_gather(out_weight, "fsdp", axis=0, tiled=True),
        lax.all_gather(out_bias, "fsdp", axis=0, tiled=True),
        lax.all_gather(second_gain, "fsdp", axis=0, tiled=True),
        lax.all_gather(second_shift, "fsdp", axis=0, tiled=True),
        lax.all_gather(up_weight, "fsdp", axis=0, tiled=True),
        lax.all_gather(up_bias, "fsdp", axis=0, tiled=True),
        lax.all_gather(down_weight, "fsdp", axis=0, tiled=True),
        lax.all_gather(down_bias, "fsdp", axis=0, tiled=True),
    )
    gain_one = gathered[0].astype(jnp.float32)
    shift_one = gathered[1].astype(jnp.float32)
    bias_query = gathered[3].astype(jnp.float32)
    bias_value = gathered[4].astype(jnp.float32)
    bias_out = gathered[6].astype(jnp.float32)
    gain_two = gathered[7].astype(jnp.float32)
    shift_two = gathered[8].astype(jnp.float32)
    bias_up = gathered[10].astype(jnp.float32)
    bias_down = gathered[12].astype(jnp.float32)
    weight_qkv = gathered[2]
    weight_out = gathered[5]
    weight_up = gathered[9]
    weight_down = gathered[11]
    groups = hidden_in.shape[0]
    span_rows = hidden_in.shape[1]
    row_count = groups * span_rows
    mem_count = groups * SUMM
    key_count = SUMM + SEQ_LEN
    head_group = min(8, HEADS)
    group_count = HEADS // head_group
    block_width = head_group * HEAD_DIM
    tokens = hidden_in.reshape(row_count, D).astype(jnp.float32)
    normed, normal_one, inverse_one = layer_norm(tokens, gain_one, shift_one)
    normed_low = normed.astype(jnp.bfloat16)
    memory = memory_rows.reshape(mem_count, D).astype(jnp.float32)
    mem_normed, mem_normal, mem_inverse = layer_norm(memory, gain_one, shift_one)
    mem_low = mem_normed.astype(jnp.bfloat16)
    projected = jnp.dot(normed_low, weight_qkv, preferred_element_type=jnp.float32)
    mem_projected = jnp.dot(mem_low, weight_qkv[:, D:], preferred_element_type=jnp.float32)
    query = (
        ((projected[:, :D] + bias_query) * 0.125).astype(jnp.bfloat16).reshape(groups, span_rows, D)
    )
    keys_local = projected[:, D : 2 * D].astype(jnp.bfloat16).reshape(groups, span_rows, D)
    values_local = (
        (projected[:, 2 * D :] + bias_value).astype(jnp.bfloat16).reshape(groups, span_rows, D)
    )
    mem_keys = mem_projected[:, :D].astype(jnp.bfloat16).reshape(groups, SUMM, D)
    mem_values = (mem_projected[:, D:] + bias_value).astype(jnp.bfloat16).reshape(groups, SUMM, D)
    keys_seq, values_seq = (
        lax.all_gather(keys_local, "ctx", axis=1, tiled=True),
        lax.all_gather(values_local, "ctx", axis=1, tiled=True),
    )
    keys_all = jnp.concatenate([mem_keys, keys_seq], axis=1)
    values_all = jnp.concatenate([mem_values, values_seq], axis=1)
    positions = lax.axis_index("ctx") * span_rows + jnp.arange(span_rows, dtype=jnp.int32)
    key_places = jnp.arange(SEQ_LEN, dtype=jnp.int32)
    causal = key_places[None, :] <= positions[:, None]
    present = (key_places[None, :] < seg_len[:, None]) | (key_places[None, :] >= SEG)
    allowed = jnp.concatenate(
        [jnp.ones((groups, span_rows, SUMM), dtype=bool), causal[None] & present[:, None, :]],
        axis=2,
    )[:, None]

    def attend(block_index):
        query_block = head_slice(query, block_index, block_width, head_group)
        key_block = head_slice(keys_all, block_index, block_width, head_group)
        value_block = head_slice(values_all, block_index, block_width, head_group)
        scores = jnp.einsum(
            "gqhd,gkhd->ghqk", query_block, key_block, preferred_element_type=jnp.float32
        )
        scores = jnp.where(allowed, scores, masked)
        largest = jnp.max(scores, axis=-1, keepdims=True)
        expanded = jnp.exp(scores - largest)
        totals = jnp.sum(expanded, axis=-1, keepdims=True)
        weights_low = (expanded / totals).astype(jnp.bfloat16)
        mixed_rows = jnp.einsum(
            "ghqk,gkhd->gqhd", weights_low, value_block, preferred_element_type=jnp.float32
        )
        return (mixed_rows.reshape(groups, span_rows, block_width), largest + jnp.log(totals))

    mixed_blocks, log_totals = lax.map(attend, jnp.arange(group_count))
    attended = jnp.moveaxis(mixed_blocks, 0, 2).reshape(row_count, D).astype(jnp.bfloat16)
    branch = jnp.dot(attended, weight_out, preferred_element_type=jnp.float32) + bias_out
    middle = tokens + branch
    normed_two, normal_two, inverse_two = layer_norm(middle, gain_two, shift_two)
    normed_two_low = normed_two.astype(jnp.bfloat16)
    upper = jnp.dot(normed_two_low, weight_up, preferred_element_type=jnp.float32) + bias_up
    active_float, smooth_pull = jax.vjp(smooth_unit, upper)
    active = active_float.astype(jnp.bfloat16)
    output = (
        (middle + (jnp.dot(active, weight_down, preferred_element_type=jnp.float32) + bias_down))
        .astype(jnp.bfloat16)
        .reshape(groups, span_rows, D)
    )
    again = (
        lax.all_gather(qkv_weight, "fsdp", axis=0, tiled=True),
        lax.all_gather(out_weight, "fsdp", axis=0, tiled=True),
        lax.all_gather(up_weight, "fsdp", axis=0, tiled=True),
        lax.all_gather(down_weight, "fsdp", axis=0, tiled=True),
    )
    back_qkv = again[0]
    back_out = again[1]
    back_up = again[2]
    back_down = again[3]
    cotangent = out_grad.reshape(row_count, D)
    cot_float = cotangent.astype(jnp.float32)
    down_part = lax.psum_scatter(
        across(active, cotangent).astype(jnp.bfloat16), "fsdp", scatter_dimension=0, tiled=True
    ).astype(jnp.float32)
    hidden_grad = against(cotangent, back_down)
    upper_grad = smooth_pull(hidden_grad)[0].astype(jnp.bfloat16)
    up_part = lax.psum_scatter(
        across(normed_two_low, upper_grad).astype(jnp.bfloat16),
        "fsdp",
        scatter_dimension=0,
        tiled=True,
    ).astype(jnp.float32)
    normed_two_grad = against(upper_grad, back_up)
    middle_norm_grad, gain_two_grad, shift_two_grad = norm_back(
        normed_two_grad, normal_two, inverse_two, gain_two
    )
    middle_grad = cot_float + middle_norm_grad
    branch_grad = middle_grad.astype(jnp.bfloat16)
    out_weight_grad = across(attended, branch_grad)
    mixed_grad = against(branch_grad, back_out).astype(jnp.bfloat16).reshape(groups, span_rows, D)

    def attend_back(block_index):
        query_block = head_slice(query, block_index, block_width, head_group)
        key_block = head_slice(keys_all, block_index, block_width, head_group)
        value_block = head_slice(values_all, block_index, block_width, head_group)
        grad_block = head_slice(mixed_grad, block_index, block_width, head_group)
        scores = jnp.einsum(
            "gqhd,gkhd->ghqk", query_block, key_block, preferred_element_type=jnp.float32
        )
        scores = jnp.where(allowed, scores, masked)
        weights = jnp.exp(scores - log_totals[block_index])
        value_grad = jnp.einsum(
            "ghqk,gqhd->gkhd",
            weights.astype(jnp.bfloat16),
            grad_block,
            preferred_element_type=jnp.float32,
        )
        weight_grad = jnp.einsum(
            "gqhd,gkhd->ghqk", grad_block, value_block, preferred_element_type=jnp.float32
        )
        centre = jnp.sum(weights * weight_grad, axis=-1, keepdims=True)
        score_grad = (weights * (weight_grad - centre)).astype(jnp.bfloat16)
        query_grad = jnp.einsum(
            "ghqk,gkhd->gqhd", score_grad, key_block, preferred_element_type=jnp.float32
        )
        key_grad = jnp.einsum(
            "ghqk,gqhd->gkhd", score_grad, query_block, preferred_element_type=jnp.float32
        )
        return (
            query_grad.reshape(groups, span_rows, block_width),
            key_grad.reshape(groups, key_count, block_width),
            value_grad.reshape(groups, key_count, block_width),
        )

    query_blocks, key_blocks, value_blocks = lax.map(attend_back, jnp.arange(group_count))
    query_grad_all = jnp.moveaxis(query_blocks, 0, 2).reshape(groups, span_rows, D)
    key_grad_all = jnp.moveaxis(key_blocks, 0, 2).reshape(groups, key_count, D)
    value_grad_all = jnp.moveaxis(value_blocks, 0, 2).reshape(groups, key_count, D)
    key_sums, value_sums = (
        lax.psum_scatter(key_grad_all[:, SUMM:], "ctx", scatter_dimension=1, tiled=True),
        lax.psum_scatter(value_grad_all[:, SUMM:], "ctx", scatter_dimension=1, tiled=True),
    )
    mem_key_sums, mem_value_sums = lax.psum(
        (key_grad_all[:, :SUMM], value_grad_all[:, :SUMM]), "ctx"
    )
    qkv_grad = jnp.concatenate(
        [
            query_grad_all.astype(jnp.bfloat16) * 0.125,
            key_sums.astype(jnp.bfloat16),
            value_sums.astype(jnp.bfloat16),
        ],
        axis=2,
    ).reshape(row_count, 3 * D)
    mem_kv_grad = jnp.concatenate(
        [mem_key_sums.astype(jnp.bfloat16), mem_value_sums.astype(jnp.bfloat16)], axis=2
    ).reshape(mem_count, 2 * D)
    owner_flag = lax.axis_index("ctx") == 0
    first_owner = owner_flag.astype(jnp.float32)
    owned_mem_grad = jnp.where(owner_flag, mem_kv_grad, jnp.zeros_like(mem_kv_grad))
    mem_rows_grad = jnp.concatenate(
        [jnp.zeros((mem_count, D), jnp.bfloat16), owned_mem_grad], axis=1
    )
    qkv_weight_grad = across(
        jnp.concatenate([normed_low, mem_low], axis=0),
        jnp.concatenate([qkv_grad, mem_rows_grad], axis=0),
    )
    query_bias_grad = jnp.sum(qkv_grad[:, :D].astype(jnp.float32), axis=0)
    value_bias_grad = jnp.sum(qkv_grad[:, 2 * D :].astype(jnp.float32), axis=0) + jnp.sum(
        owned_mem_grad[:, D:].astype(jnp.float32), axis=0
    )
    out_bias_grad = jnp.sum(branch_grad.astype(jnp.float32), axis=0)
    up_bias_grad = jnp.sum(upper_grad.astype(jnp.float32), axis=0)
    down_bias_grad = jnp.sum(cot_float, axis=0)
    normed_grad = against(qkv_grad, back_qkv)
    token_norm_grad, gain_one_tok, shift_one_tok = norm_back(
        normed_grad, normal_one, inverse_one, gain_one
    )
    mem_normed_grad = against(mem_kv_grad, back_qkv[:, D:])
    memory_norm_grad, gain_one_mem, shift_one_mem = norm_back(
        mem_normed_grad, mem_normal, mem_inverse, gain_one
    )
    gain_one_grad = gain_one_tok + first_owner * gain_one_mem
    shift_one_grad = shift_one_tok + first_owner * shift_one_mem
    input_grad = (middle_grad + token_norm_grad).reshape(groups, span_rows, D)
    memory_grad = memory_norm_grad.reshape(groups, SUMM, D)
    shares = (
        lax.psum_scatter(
            gain_one_grad.astype(jnp.bfloat16), "fsdp", scatter_dimension=0, tiled=True
        ).astype(jnp.float32),
        lax.psum_scatter(
            shift_one_grad.astype(jnp.bfloat16), "fsdp", scatter_dimension=0, tiled=True
        ).astype(jnp.float32),
        lax.psum_scatter(
            qkv_weight_grad.astype(jnp.bfloat16), "fsdp", scatter_dimension=0, tiled=True
        ).astype(jnp.float32),
        lax.psum_scatter(
            query_bias_grad.astype(jnp.bfloat16), "fsdp", scatter_dimension=0, tiled=True
        ).astype(jnp.float32),
        lax.psum_scatter(
            value_bias_grad.astype(jnp.bfloat16), "fsdp", scatter_dimension=0, tiled=True
        ).astype(jnp.float32),
        lax.psum_scatter(
            out_weight_grad.astype(jnp.bfloat16), "fsdp", scatter_dimension=0, tiled=True
        ).astype(jnp.float32),
        lax.psum_scatter(
            out_bias_grad.astype(jnp.bfloat16), "fsdp", scatter_dimension=0, tiled=True
        ).astype(jnp.float32),
        lax.psum_scatter(
            gain_two_grad.astype(jnp.bfloat16), "fsdp", scatter_dimension=0, tiled=True
        ).astype(jnp.float32),
        lax.psum_scatter(
            shift_two_grad.astype(jnp.bfloat16), "fsdp", scatter_dimension=0, tiled=True
        ).astype(jnp.float32),
        lax.psum_scatter(
            up_bias_grad.astype(jnp.bfloat16), "fsdp", scatter_dimension=0, tiled=True
        ).astype(jnp.float32),
        lax.psum_scatter(
            down_bias_grad.astype(jnp.bfloat16), "fsdp", scatter_dimension=0, tiled=True
        ).astype(jnp.float32),
    )
    summed = lax.psum(
        (
            shares[0],
            shares[1],
            shares[2],
            shares[3],
            shares[4],
            shares[5],
            shares[6],
            shares[7],
            shares[8],
            shares[9],
            shares[10],
            up_part,
            down_part,
        ),
        ("replica", "ctx"),
    )
    return (
        output,
        input_grad,
        memory_grad,
        summed[0],
        summed[1],
        summed[2],
        summed[3],
        summed[4],
        summed[5],
        summed[6],
        summed[7],
        summed[8],
        summed[11],
        summed[9],
        summed[12],
        summed[10],
    )


def solution(mesh):
    return jax.shard_map(
        shards,
        mesh=mesh,
        in_specs=(
            P(("fsdp", "replica"), "ctx", None),
            P(("fsdp", "replica"), None, None),
            P(("fsdp", "replica")),
            P(("fsdp", "replica"), "ctx", None),
            P("fsdp"),
            P("fsdp"),
            P("fsdp", None),
            P("fsdp"),
            P("fsdp"),
            P("fsdp", None),
            P("fsdp"),
            P("fsdp"),
            P("fsdp"),
            P("fsdp", None),
            P("fsdp"),
            P("fsdp", None),
            P("fsdp"),
        ),
        out_specs=(
            P(("fsdp", "replica"), "ctx", None),
            P(("fsdp", "replica"), "ctx", None),
            P(("fsdp", "replica"), None, None),
            P("fsdp"),
            P("fsdp"),
            P("fsdp", None),
            P("fsdp"),
            P("fsdp"),
            P("fsdp", None),
            P("fsdp"),
            P("fsdp"),
            P("fsdp"),
            P("fsdp", None),
            P("fsdp"),
            P("fsdp", None),
            P("fsdp"),
        ),
        check_vma=False,
    )
```

profile of v0, /device:TPU:0, one launch (start us, length us, event | category | flops | bytes accessed | tf_op | source)
XLA Modules:
  0.0 7138.8 jit_solution(2888771679025506342)
XLA Ops:
  8.7 13.5 all-gather.3
  22.9 12.0 all-gather.2
  35.6 35.1 all-gather.5
  71.4 28.8 all-gather.4
  101.4 336.4 %all-gather.17.cloned.1.call-done = bf16[2048,6144]{1,0:T(8,128)(2,1)} async-done(((bf16[512,6144]{1,0:T(8,128)(2,1)}), bf16[2048,6144]{1,0:T(8,128)(2,1)}) %all-gather.17.cloned.1.call-update) | async-done | bytes 25165840 | tf_op jit(solution)/shard_map/all_gather | solution.py:81
  437.8 11.9 fusion.87
  459.3 11.9 all-gather.6
  471.9 13.1 all_gather.61
  485.0 11.9 all-gather.8
  497.0 11.9 all-gather.7
  513.3 7.4 fusion.7
  526.8 6.7 copy.54
  539.9 6.8 copy.56
  548.0 59.2 while.26
  607.2 70.9 all-gather.19.cloned.1.call-done
  678.1 6.6 fusion.82
  686.5 552.7 %all-gather.21.cloned.1.call-done = bf16[2048,8192]{1,0:T(8,128)(2,1)} async-done(((bf16[512,8192]{1,0:T(8,128)(2,1)}), bf16[2048,8192]{1,0:T(8,128)(2,1)}) %all-gather.21.cloned.1.call-update) | async-done | bytes 33554448 | tf_op jit(solution)/shard_map/all_gather | solution.py:88
  1239.2 34.7 multiply_convert_fusion.1
  1273.9 526.3 %all-gather.23.cloned.1.call-done = bf16[8192,2048]{1,0:T(8,128)(2,1)} async-done(((bf16[2048,2048]{1,0:T(8,128)(2,1)}), bf16[8192,2048]{1,0:T(8,128)(2,1)}) %all-gather.23.cloned.1.call-update) | async-done | bytes 33554448 | tf_op jit(solution)/shard_map/all_gather | solution.py:90
  1800.2 36.5 fusion.83
  1836.8 17.0 multiply_reduce_fusion.1
  1855.4 6.8 convolution_convert_fusion.3
  1862.4 6.9 fusion.32
  1870.6 188.6 %while.27 = (s32[]{:T(128)}, bf16[4,1,272,512]{2,3,1,0:T(8,128)(2,1)}, f32[4,1,1138,512]{2,3,1,0:T(8,128)}, f32[4,1,1138,512]{2,3,1,0:T(8,128)}, s32[4]{0:T(128)...) while((s32[]{:T(128)}, ...), condition=%wide.region_14.15_spmd, body=%wide.region_12.14_spmd.sunk | while | flops 1604632448 | bytes 115616344 | solution.py:242
  1885.0 8.4 multiply_reduce_fusion.8
  1893.3 10.1 multiply_convert_fusion.3
  1932.1 8.3 multiply_reduce_fusion.8
  1940.4 10.1 multiply_convert_fusion.3
  1979.1 8.4 multiply_reduce_fusion.8
  1987.6 10.1 multiply_convert_fusion.3
  2026.4 8.3 multiply_reduce_fusion.8
  2034.7 10.0 multiply_convert_fusion.3
  2060.7 10.1 slice.62
  2078.2 21.4 copy.74
  2099.6 21.4 copy.73
  2121.0 2492.4 %all-reduce.20 = (bf16[1,50,2048]{2,0,1:T(2,128)(2,1)S(1)}, bf16[1,50,2048]{2,0,1:T(2,128)(2,1)S(1)}, bf16[1,1088,2048]{2,0,1:T(2,128)(2,1)}, bf16[1,1088,2048]{2,0,1:T(2,128)(2,1)}) all-reduce(f32[1,50,2048]{2,0,1:T(1,128)S(1)} %copy.76, f32[1,50,2048]{2,0,1:T(1,128)S(1)} %copy.75, ...), channel_id=1, replica_groups=mesh['fsdp'=4,'replica'=2,'ctx'=4] {'ctx'}, use_global_device_ids=true, to_apply=%region_20.21 | all-reduce | flops 4661248 | bytes 27967488 | tf_op jit(solution)/shard_map/psum | solution.py:250
  4630.1 17.2 convolution_convert_fusion.2
  4649.0 24.6 convolution_convert_fusion.1
  4674.8 24.3 convolution_convert_fusion
  4699.8 13.0 all-gather.9
  4715.0 12.3 fusion.69
  4733.9 15.0 fusion.40
  4748.9 20.1 all-reduce.17
  4774.1 17.6 fusion.31
  4791.7 269.4 %reduce-scatter.9.cloned.1.call-done = bf16[512,6144]{1,0:T(8,128)(2,1)} async-done(((bf16[2048,6144]{1,0:T(8,128)(2,1)}), bf16[512,6144]{1,0:T(8,128)(2,1)}) %reduce-scatter.9.cloned.1.call-update) | async-done | bytes 6291472 | tf_op jit(solution)/shard_map/reduce_scatter | solution.py:300
  5061.2 556.4 %reduce-scatter.13.cloned.1.call-done = bf16[512,8192]{1,0:T(8,128)(2,1)} async-done(((bf16[2048,8192]{1,0:T(8,128)(2,1)}), bf16[512,8192]{1,0:T(8,128)(2,1)}) %reduce-scatter.13.cloned.1.call-update) | async-done | bytes 8388624
  5617.6 555.0 %reduce-scatter.15.cloned.1.call-done = bf16[2048,2048]{1,0:T(8,128)(2,1)} async-done(((bf16[8192,2048]{1,0:T(8,128)(2,1)}), bf16[2048,2048]{1,0:T(8,128)(2,1)}) %reduce-scatter.15.cloned.1.call-update) | async-done | bytes 8388624
  6172.6 959.1 %all-reduce.21 = (f32[512]{0:T(512)}, f32[512]{0:T(512)}, f32[512,6144]{1,0:T(8,128)}, f32[512]{0:T(512)}, f32[512]{0:T(512)}, /*index=5*/f32[512,2048]{1,0:T(8,...) all-reduce(f32[512]{0:T(512)S(1)} %dynamic-slice_convert_fusion.8, ...), channel_id=1, replica_groups=mesh['fsdp'=4,'replica'=2,'ctx'=4] {'replica','ctx'}, use_global_device_ids=true, to_apply=%region_26.27 | all-reduce | flops 12589056 | bytes 75546624 | tf_op jit(solution)/shard_map/psum | solution.py:328
  (332 shorter events, 226.5 us)
Async XLA Ops:
  7.2 93.0 %copy-start.2 = (bf16[1,272,2048]{2,1,0:T(8,128)(2,1)S(1)}, bf16[1,272,2048]{2,1,0:T(8,128)(2,1)}, u32[]{:S(2)}) copy-start(bf16[1,272,2048]{2,1,0:T(8,128)(2,1)} %param.21) | copy-start | bytes 3342340
  7.2 430.6 %all-gather.17.cloned.1.call-start = ((), (), s32[]{:S(2)}) async-start(), calls=%async_computation.4 | async-start | bytes 31457280 | tf_op jit(solution)/shard_map/all_gather | solution.py:81
  7.9 512.9 %all-gather.25.cloned.1.call-start = ((), (), s32[]{:S(2)}) async-start(), calls=%async_computation.10 | async-start | bytes 5570560 | tf_op jit(solution)/shard_map/all_gather | solution.py:133
  34.9 476.3 %copy-start.25 = (f32[4,1,512]{2,1,0:T(1,128)}, f32[4,1,512]{2,1,0:T(1,128)S(1)}, u32[]{:S(2)}) copy-start(f32[4,1,512]{2,1,0:T(1,128)S(1)} %convert_element_type.263) | copy-start | bytes 24580
  100.4 349.3 %copy-start.29 = (f32[272]{0:T(512)}, f32[272]{0:T(512)S(1)}, u32[]{:S(2)}) copy-start(f32[272]{0:T(512)S(1)} %broadcast_multiply_fusion.5) | copy-start | bytes 3268
  100.9 348.8 %copy-start.33 = (f32[272]{0:T(512)}, f32[272]{0:T(512)S(1)}, u32[]{:S(2)}) copy-start(f32[272]{0:T(512)S(1)} %add_rsqrt_fusion.1) | copy-start | bytes 3268
  101.4 348.3 %copy-start.18 = (bf16[272,2048]{1,0:T(8,128)(2,1)}, bf16[272,2048]{1,0:T(8,128)(2,1)S(1)}, u32[]{:S(2)}) copy-start(bf16[272,2048]{1,0:T(8,128)(2,1)S(1)} %fusion.34) | copy-start | bytes 3342340
  454.6 79.0 %all-gather.27.cloned.1.call-start = ((), (), s32[]{:S(2)}) async-start(), calls=%async_computation.11 | async-start | bytes 5570560 | tf_op jit(solution)/shard_map/all_gather | solution.py:132
  457.4 220.7 %all-gather.19.cloned.1.call-start = ((), (), s32[]{:S(2)}) async-start(), calls=%async_computation.5 | async-start | bytes 10485760 | tf_op jit(solution)/shard_map/all_gather | solution.py:84
  458.0 13.9 copy-start.43
  458.0 27.0 copy-start.49
  458.0 38.9 copy-start.50
  458.0 50.8 copy-start.53
  458.1 52.1 copy-start.17
  458.1 781.1 %all-gather.21.cloned.1.call-start = ((), (), s32[]{:S(2)}) async-start(), calls=%async_computation.6 | async-start | bytes 41943040 | tf_op jit(solution)/shard_map/all_gather | solution.py:88
  458.7 1341.6 %all-gather.23.cloned.1.call-start = ((), (), s32[]{:S(2)}) async-start(), calls=%async_computation.7 | async-start | bytes 41943040 | tf_op jit(solution)/shard_map/all_gather | solution.py:90
  459.2 4332.5 %reduce-scatter.11.cloned.1.call-start = ((), (), s32[]{:S(2)}) async-start(), calls=%async_computation.9 | async-start | bytes 10485760 | tf_op jit(solution)/shard_map/reduce_scatter | solution.py:309
  496.9 742.3 %copy-start.39 = (f32[4,1,512]{2,1,0:T(1,128)}, f32[4,1,512]{2,1,0:T(1,128)S(1)}, u32[]{:S(2)}) copy-start(f32[4,1,512]{2,1,0:T(1,128)S(1)} %convert_element_type.269) | copy-start | bytes 24580
  508.8 1345.0 %copy-start.27 = (f32[4,1,512]{2,1,0:T(1,128)}, f32[4,1,512]{2,1,0:T(1,128)S(1)}, u32[]{:S(2)}) copy-start(f32[4,1,512]{2,1,0:T(1,128)S(1)} %convert_element_type.268) | copy-start | bytes 24580
  510.3 10.5 copy-start.41
  510.5 10.2 copy-start.46
  607.2 77.5 %copy-start = (pred[1,1,272,1138]{3,2,1,0:T(8,128)(4,1)}, pred[1,1,272,1138]{3,2,1,0:T(8,128)(4,1)S(1)}, u32[]{:S(2)}) copy-start(pred[1,1,272,1138]{3,2,1,0:T(8,128)(4,1)S(1)} %get-tuple-element.553) | copy-start | bytes 928612
  607.2 77.5 %copy-start.7 = (bf16[1,272,2048]{1,2,0:T(8,128)(2,1)}, bf16[1,272,2048]{1,2,0:T(8,128)(2,1)S(1)}, u32[]{:S(2)}) copy-start(bf16[1,272,2048]{1,2,0:T(8,128)(2,1)S(1)} %get-tuple-element.562) | copy-start | bytes 3342340
  684.8 1169.1 %copy-start.31 = (f32[272]{0:T(512)}, f32[272]{0:T(512)S(1)}, u32[]{:S(2)}) copy-start(f32[272]{0:T(512)S(1)} %broadcast_multiply_fusion.4) | copy-start | bytes 3268
  686.5 1167.3 %copy-start.37 = (f32[272]{0:T(512)}, f32[272]{0:T(512)S(1)}, u32[]{:S(2)}) copy-start(f32[272]{0:T(512)S(1)} %add_rsqrt_fusion) | copy-start | bytes 3268
  1239.2 561.0 %copy-start.13 = (bf16[1,272,2048]{2,1,0:T(8,128)(2,1)S(1)}, bf16[1,272,2048]{2,1,0:T(8,128)(2,1)}, u32[]{:S(2)}) copy-start(bf16[1,272,2048]{2,1,0:T(8,128)(2,1)} %param.24) | copy-start | bytes 3342340
  1800.2 36.5 copy-start.5
  1836.8 17.1 copy-start.14
  1855.4 7.1 copy-start.9
  1862.2 8.4 copy-start.1
  1862.2 3199.0 %reduce-scatter.9.cloned.1.call-start = ((), (), s32[]{:S(2)}) async-start(), calls=%async_computation.8 | async-start | bytes 31457280 | tf_op jit(solution)/shard_map/reduce_scatter | solution.py:300
  2059.2 11.6 slice-start.2
  2060.7 10.1 slice-start.3
  2060.7 10.1 slice-start.4
  4618.0 8.2 copy-start.16
  4647.4 970.2 %reduce-scatter.13.cloned.1.call-start = ((), (), s32[]{:S(2)}) async-start(), calls=%async_computation.12 | async-start | bytes 41943040
  4673.6 1499.0 %reduce-scatter.15.cloned.1.call-start = ((), (), s32[]{:S(2)}) async-start(), calls=%async_computation.13 | async-start | bytes 41943040
  4699.1 13.9 copy-start.52
  4699.1 15.8 copy-start.26
  4699.1 15.8 copy-start.42
  4699.1 15.8 copy-start.47
  4715.0 18.9 copy-start.3
  4715.0 18.9 copy-start.30
  4715.0 18.9 copy-start.34
  4733.9 15.0 copy-start.35
  4733.9 15.0 copy-start.36
  4733.9 15.0 copy-start.44
  4733.9 15.0 copy-start.45
  (27 other events, 90.5 us)
Sparse Core Ops, SparseCore 0:
  9.6 428.1 all-gather.16
  454.7 34.1 all-gather.24
  491.0 35.9 all-gather.26
  528.4 149.6 all-gather.18
  679.5 559.6 all-gather.20
  1240.6 559.5 all-gather.22
  1862.3 142.6 reduce-scatter.10
  4647.5 413.5 reduce-scatter.8
  5063.6 553.8 reduce-scatter.12
  5619.8 552.7 reduce-scatter.14
where the time goes:
time: 7170 us; the launch traced here: 7140 us
  blocking collectives  3620 us (50%)
  waiting for transfers between devices  2870 us (40%)
  matrix products  357 us (5%)
  local copies, waits for them, and re-layouts  161 us (2%)
  other arithmetic  84.9 us (1%)
    psum x1, blocking collectives, shards(): lax.psum((key_grad_all[:, :SUMM], value_grad_all[:, :SUMM]), 'ctx')  2490 us
    unnamed x12, waiting for transfers between devices  1110 us
    psum x1, blocking collectives, shards(): lax.psum((shares[0], shares[1], shares[2], shares[3], shares[4], shares[5...  959 us
    all_gather x1, waiting for transfers between devices, shards(): lax.all_gather(up_weight, 'fsdp', axis=0, tiled=True)  553 us
    all_gather x1, waiting for transfers between devices, shards(): lax.all_gather(down_weight, 'fsdp', axis=0, tiled=True)  526 us
    all_gather x1, waiting for transfers between devices, shards(): lax.all_gather(qkv_weight, 'fsdp', axis=0, tiled=True)  336 us
    reduce_scatter x1, waiting for transfers between devices, shards(): lax.psum_scatter(qkv_weight_grad.astype(jnp.bfloat16), 'fsdp', scatter_di...  269 us
  transfers between devices with their start and end apart: 10, of which 7 were waited for; matrix products, arithmetic and copies ran while one was open for 7% of the time, Pallas kernels for 0%

commit v1 on v0

v1 whole, which is shorter than its diff:
```python
import jax
import jax.numpy as jnp
from jax import lax
from jax.sharding import PartitionSpec as P

D = 2048
HEADS = 32
HEAD_DIM = 64
SUMM = 50
SEQ_LEN = 1088
SEG = 1038
MEM_ROWS = 16

epsilon = 1e-05
masked = -1e30
f32 = jnp.float32
bf16 = jnp.bfloat16
PLANE = ("replica", "ctx")


def dot(left, right):
    return jnp.dot(left, right, preferred_element_type=f32)


def across(left, right):
    return lax.dot_general(left, right, (((0,), (0,)), ((), ())), preferred_element_type=f32)


def against(left, right):
    return lax.dot_general(left, right, (((1,), (1,)), ((), ())), preferred_element_type=f32)


def normal_of(rows):
    centred = rows - jnp.mean(rows, axis=-1, keepdims=True)
    inverse = lax.rsqrt(jnp.mean(centred * centred, axis=-1, keepdims=True) + epsilon)
    return centred * inverse, inverse


def norm_input_grad(upstream, normal, inverse, weight):
    scaled = upstream * weight
    centre = jnp.mean(scaled, axis=-1, keepdims=True)
    slope = jnp.mean(scaled * normal, axis=-1, keepdims=True)
    return inverse * (scaled - centre - normal * slope)


class Plane:
    def __init__(self):
        self.replicas = lax.axis_size("replica")
        self.spans = lax.axis_size("ctx")
        self.sizes = {"replica": self.replicas, "ctx": self.spans}
        self.slow = []
        bit = 1
        while bit < self.replicas:
            self.slow.append(("replica", bit))
            bit *= 2
        bit = 2
        while bit < self.spans:
            self.slow.append(("ctx", bit))
            bit *= 2
        self.fast = ("ctx", 1)
        spans = [v for v in range(self.spans) if v % 2 == 0] + [v for v in range(self.spans) if v % 2 == 1]
        self.span_order = spans
        self.order = [(r, v) for v in spans for r in range(self.replicas)]
        self.half = len(self.order) // 2

    def swap(self, array, stage):
        axis, bit = stage
        return lax.ppermute(array, axis, [(i, i ^ bit) for i in range(self.sizes[axis])])

    def step(self, name, stage):
        axis, bit = stage
        return (name[0] ^ bit, name[1]) if axis == "replica" else (name[0], name[1] ^ bit)

    def spread(self, rows):
        cut = cut_of(rows.shape[0])
        sides = [rows[:cut], rows[cut:]]
        found = [{(0, 0): sides[0]}, {(0, 0): sides[1]}]
        plans = [self.slow, self.slow[::-1]]
        for level in range(len(self.slow)):
            for side in range(2):
                stage = plans[side][level]
                for name, value in list(found[side].items()):
                    found[side][self.step(name, stage)] = self.swap(value, stage)
        pieces = []
        for name in self.order[: self.half]:
            pieces.append((found[0][name], found[1][name]))
        for upper, lower in list(pieces):
            pieces.append((self.swap(upper, self.fast), self.swap(lower, self.fast)))
        return pieces

    def gather(self, rows):
        return jnp.concatenate([half for piece in self.spread(rows) for half in piece], axis=0)

    def scatter(self, far, near):
        count = far.shape[0] // self.half
        cut = cut_of(count)
        names = self.order[: self.half]
        held = [{}, {}]
        for index in reversed(range(self.half)):
            sent = self.swap(far[index * count : (index + 1) * count], self.fast)
            kept = near[index * count : (index + 1) * count]
            total = kept.astype(f32) + sent.astype(f32)
            for side, part in enumerate((total[:cut], total[cut:])):
                held[side][names[index]] = part if index == 0 else part.astype(bf16)
        plans = [self.slow, self.slow[::-1]]
        for level in range(len(self.slow)):
            for side in range(2):
                stage = plans[side][level]
                later = plans[side][level + 1 :]
                kept = {}
                for name, value in held[side].items():
                    if self.bit(name, stage):
                        continue
                    moved = self.swap(held[side][self.step(name, stage)], stage)
                    total = value.astype(f32) + moved.astype(f32)
                    kept[name] = total if name == (0, 0) else total.astype(bf16)
                held[side] = kept
        return jnp.concatenate([held[0][(0, 0)], held[1][(0, 0)]], axis=0)

    def bit(self, name, stage):
        axis, bit = stage
        return (name[0] if axis == "replica" else name[1]) & bit


def cut_of(count):
    return (count // 2 + 15) // 16 * 16


def columns_of(weight, groups, index, width):
    span = weight.shape[1] // groups
    return jnp.concatenate(
        [lax.dynamic_slice_in_dim(weight, g * span + index * width, width, 1) for g in range(groups)], axis=1
    )


def allowed_of(plane, span_rows, own, lengths):
    places, slots = [], []
    for value in plane.span_order:
        base = own ^ value
        rows = jnp.arange(span_rows, dtype=jnp.int32) + base * span_rows
        mem = jnp.arange(MEM_ROWS, dtype=jnp.int32) + base * MEM_ROWS
        places.append((rows, mem))
    far = jnp.int32(1 << 30)
    queries = jnp.concatenate([rows for rows, _ in places])
    keys = jnp.concatenate([jnp.concatenate([rows, jnp.where(mem < SUMM, -1, far)]) for rows, mem in places])
    causal = keys[None, :] <= queries[:, None]
    present = (keys[None, :] < lengths[:, None]) | (keys[None, :] >= SEG)
    return causal[None] & present[:, None, :]


def attend(query, key, value, allowed):
    scores = jnp.einsum("gqhd,gkhd->ghqk", query, key, preferred_element_type=f32)
    scores = jnp.where(allowed[:, None], scores, masked)
    largest = jnp.max(scores, axis=-1, keepdims=True)
    expanded = jnp.exp(scores - largest)
    totals = jnp.sum(expanded, axis=-1, keepdims=True)
    weights = (expanded / totals).astype(bf16)
    mixed = jnp.einsum("ghqk,gkhd->gqhd", weights, value, preferred_element_type=f32)
    return mixed.astype(bf16), largest + jnp.log(totals)


def attend_back(query, key, value, upstream, log_totals, allowed):
    scores = jnp.einsum("gqhd,gkhd->ghqk", query, key, preferred_element_type=f32)
    scores = jnp.where(allowed[:, None], scores, masked)
    weights = jnp.exp(scores - log_totals)
    value_grad = jnp.einsum("ghqk,gqhd->gkhd", weights.astype(bf16), upstream, preferred_element_type=f32)
    weight_grad = jnp.einsum("gqhd,gkhd->ghqk", upstream, value, preferred_element_type=f32)
    centre = jnp.sum(weights * weight_grad, axis=-1, keepdims=True)
    score_grad = (weights * (weight_grad - centre)).astype(bf16)
    query_grad = jnp.einsum("ghqk,gkhd->gqhd", score_grad, key, preferred_element_type=f32)
    key_grad = jnp.einsum("ghqk,gqhd->gkhd", score_grad, query, preferred_element_type=f32)
    return query_grad.astype(bf16) * 0.125, key_grad.astype(bf16), value_grad.astype(bf16)


def shards(
    hidden_in,
    memory_rows,
    seg_len,
    out_grad,
    first_gain,
    first_shift,
    qkv_weight,
    query_bias,
    value_bias,
    out_weight,
    out_bias,
    second_gain,
    second_shift,
    up_weight,
    up_bias,
    down_weight,
    down_bias,
):
    plane = Plane()
    owners = lax.axis_size("fsdp")
    replicas, spans = plane.replicas, plane.spans
    team = replicas * spans
    pieces = len(plane.order)
    owner = lax.axis_index("fsdp")
    own_span = lax.axis_index("ctx")
    index = lax.axis_index("replica") * spans + own_span
    share = D // owners
    span_rows = hidden_in.shape[1]
    piece_rows = span_rows + MEM_ROWS
    heads = HEADS // team
    width = heads * HEAD_DIM
    hidden = up_bias.shape[0] // team
    ff = hidden * owners

    small = jnp.concatenate(
        [first_gain, first_shift, query_bias, value_bias, out_bias, second_gain, second_shift, down_bias, up_bias]
    )
    small = lax.all_gather(small.reshape(-1, 128), "fsdp", axis=0, tiled=True).reshape(owners, -1).astype(f32)
    vectors = [small[:, i * share : (i + 1) * share].reshape(D) for i in range(8)]
    gain_one, shift_one, bias_query, bias_value, bias_out, gain_two, shift_two, bias_down = vectors
    bias_up = lax.dynamic_slice_in_dim(small[:, 8 * share :], index * hidden, hidden, 1).reshape(ff)
    if heads % owners == 0:
        block = width // owners
        groups = owners
        weight_out = lax.all_gather(
            lax.dynamic_slice_in_dim(out_weight, index * block, block, 0), "fsdp", axis=0, tiled=True
        )
    else:
        block = width
        groups = 1
        weight_out = lax.dynamic_slice_in_dim(
            lax.all_gather(out_weight, "fsdp", axis=0, tiled=True), index * width, width, 0
        )
    weight_qkv = lax.all_gather(columns_of(qkv_weight, 3 * groups, index, block), "fsdp", axis=0, tiled=True)
    weight_up = lax.all_gather(columns_of(up_weight, owners, index, hidden), "fsdp", axis=0, tiled=True)
    weight_down = lax.all_gather(
        lax.dynamic_slice_in_dim(down_weight, index * hidden, hidden, 0), "fsdp", axis=0, tiled=True
    )
    my_bias = lambda vector: columns_of(vector[None], groups, index, block)[0]

    tokens = hidden_in.reshape(span_rows, D)
    slots = jnp.pad(memory_rows.reshape(SUMM, D), ((0, spans * MEM_ROWS - SUMM), (0, 0)))
    slots = lax.dynamic_slice_in_dim(slots, own_span * MEM_ROWS, MEM_ROWS, 0)
    own_rows = jnp.concatenate([tokens, slots], axis=0)
    all_rows = plane.gather(own_rows).astype(f32)
    normal_all, _ = normal_of(all_rows)
    normed = (normal_all * gain_one + shift_one).astype(bf16)
    bias_qkv = jnp.concatenate([my_bias(bias_query), jnp.zeros((width,), f32), my_bias(bias_value)])
    scale_qkv = jnp.concatenate([jnp.full((width,), 0.125, f32), jnp.ones((2 * width,), f32)])
    projected = ((dot(normed, weight_qkv) + bias_qkv) * scale_qkv).astype(bf16)

    lengths = [seg_len]
    for axis, bit in plane.slow:
        if axis == "replica":
            lengths = lengths + [plane.swap(v, (axis, bit)) for v in lengths]
    lengths = jnp.concatenate(lengths)

    def parts_of(array):
        array = array.reshape(spans, replicas, piece_rows, 3, heads, HEAD_DIM)
        array = jnp.moveaxis(array, 1, 0)
        query = array[:, :, :span_rows, 0].reshape(replicas, SEQ_LEN, heads, HEAD_DIM)
        key = array[:, :, :, 1].reshape(replicas, -1, heads, HEAD_DIM)
        value = array[:, :, :, 2].reshape(replicas, -1, heads, HEAD_DIM)
        return query, key, value

    query, key, value = parts_of(projected)
    allowed = allowed_of(plane, span_rows, own_span, lengths)
    mixed, log_totals = attend(query, key, value, allowed)
    to_pieces = lambda a: jnp.moveaxis(a.reshape(replicas, spans, -1, a.shape[-2] * a.shape[-1]), 0, 1)
    attended = to_pieces(mixed).reshape(pieces * span_rows, width)

    cut = plane.half * span_rows
    far = dot(attended[cut:], weight_out).astype(bf16)
    near = dot(attended[:cut], weight_out).astype(bf16)
    middle = tokens.astype(f32) + (plane.scatter(far, near) + bias_out)
    normal_two, inverse_two = normal_of(middle)
    normed_two = plane.gather((normal_two * gain_two + shift_two).astype(bf16))
    cotangent = out_grad.reshape(span_rows, D)
    cot_all = plane.gather(cotangent)

    upper = dot(normed_two, weight_up) + bias_up
    phi_up = 0.5 * (1.0 + lax.erf(upper * 0.7071067811865476))
    active = (upper * phi_up).astype(bf16)
    slope = phi_up + upper * (0.3989422804014327 * jnp.exp(-0.5 * upper * upper))
    upper_grad_f = against(cot_all, weight_down) * slope
    upper_grad = upper_grad_f.astype(bf16)
    far = against(upper_grad[cut:], weight_up).astype(bf16)
    near = against(upper_grad[:cut], weight_up).astype(bf16)
    normed_two_grad = plane.scatter(far, near)
    far = dot(active[cut:], weight_down).astype(bf16)
    near = dot(active[:cut], weight_down).astype(bf16)
    output = (middle + (plane.scatter(far, near) + bias_down)).astype(bf16)
    down_grad = across(active, cot_all).astype(bf16)
    up_grad = across(normed_two, upper_grad).astype(bf16)
    up_bias_grad = jnp.sum(upper_grad.astype(f32), axis=0)

    cot_float = cotangent.astype(f32)
    middle_grad = cot_float + norm_input_grad(normed_two_grad, normal_two, inverse_two, gain_two)
    branch_grad = middle_grad.astype(bf16)
    branch_all = plane.gather(branch_grad)
    mixed_grad = against(branch_all, weight_out).astype(bf16)
    out_grad_w = across(attended, branch_all).astype(bf16)
    upstream = jnp.moveaxis(mixed_grad.reshape(spans, replicas, span_rows, heads, HEAD_DIM), 1, 0)
    upstream = upstream.reshape(replicas, SEQ_LEN, heads, HEAD_DIM)
    query_grad, key_grad, value_grad = attend_back(query, key, value, upstream, log_totals, allowed)
    query_grad = jnp.pad(to_pieces(query_grad), ((0, 0), (0, 0), (0, MEM_ROWS), (0, 0)))
    projected_grad = jnp.concatenate([query_grad, to_pieces(key_grad), to_pieces(value_grad)], axis=-1)
    projected_grad = projected_grad.reshape(pieces * piece_rows, 3 * width)
    qkv_grad = across(normed, projected_grad).astype(bf16)
    qkv_bias_grad = jnp.sum(projected_grad.astype(f32), axis=0)
    cut = plane.half * piece_rows
    far = against(projected_grad[cut:], weight_qkv).astype(bf16)
    near = against(projected_grad[:cut], weight_qkv).astype(bf16)
    normed_grad = plane.scatter(far, near)
    normal_one, inverse_one = normal_of(own_rows.astype(f32))
    rows_grad = norm_input_grad(normed_grad, normal_one, inverse_one, gain_one)
    input_grad = middle_grad + rows_grad[:span_rows]
    slots_grad = lax.all_gather(rows_grad[span_rows:], "ctx", axis=0, tiled=True)[:SUMM]

    def settle(array, axis):
        mine = lax.psum_scatter(array, "fsdp", scatter_dimension=0, tiled=True)
        return lax.all_gather(mine, PLANE, axis=axis, tiled=False)

    down_all = settle(down_grad, 0).reshape(team * hidden, D).astype(f32)
    up_all = settle(up_grad, 0).reshape(team, share, owners, hidden)
    up_all = jnp.moveaxis(up_all, 0, 2).reshape(share, -1).astype(f32)
    qkv_all = settle(qkv_grad, 0).reshape(team, share, 3 * groups, block)
    qkv_all = jnp.moveaxis(qkv_all, 0, 2).reshape(share, 3 * D).astype(f32)
    if groups == owners:
        out_all = settle(out_grad_w, 0).reshape(share, D).astype(f32)
    else:
        placed = lax.dynamic_update_slice_in_dim(jnp.zeros((D, D), bf16), out_grad_w, index * width, 0)
        out_all = lax.psum(lax.psum_scatter(placed, "fsdp", scatter_dimension=0, tiled=True), PLANE).astype(f32)

    def spot(values, full, count, size):
        base = jnp.zeros((count, full // count), f32)
        return lax.dynamic_update_slice_in_dim(base, values.reshape(count, size), index * size, 1).reshape(full)

    totals = jnp.concatenate(
        [
            jnp.sum(normed_grad * normal_one, axis=0),
            jnp.sum(normed_grad, axis=0),
            spot(qkv_bias_grad[:width], D, groups, block),
            spot(qkv_bias_grad[2 * width :], D, groups, block),
            jnp.sum(branch_grad.astype(f32), axis=0),
            jnp.sum(normed_two_grad * normal_two, axis=0),
            jnp.sum(normed_two_grad, axis=0),
            jnp.sum(cot_float, axis=0),
            spot(up_bias_grad, ff * team, owners, hidden),
        ]
    )
    totals = lax.psum(totals, ("fsdp", "replica", "ctx"))
    take = lambda i: lax.dynamic_slice_in_dim(totals, i * D + owner * share, share)
    up_share = ff * team // owners
    return (
        output.reshape(hidden_in.shape),
        input_grad.reshape(hidden_in.shape),
        slots_grad.reshape(memory_rows.shape),
        take(0),
        take(1),
        qkv_all,
        take(2),
        take(3),
        out_all,
        take(4),
        take(5),
        take(6),
        up_all,
        lax.dynamic_slice_in_dim(totals, 8 * D + owner * up_share, up_share),
        down_all,
        take(7),
    )


def solution(mesh):
    rows = P(("fsdp", "replica"), "ctx", None)
    part = P("fsdp")
    table = P("fsdp", None)
    whole = P(("fsdp", "replica"), None, None)
    return jax.shard_map(
        shards,
        mesh=mesh,
        in_specs=(
            rows,
            whole,
            P(("fsdp", "replica")),
            rows,
            part,
            part,
            table,
            part,
            part,
            table,
            part,
            part,
            part,
            table,
            part,
            table,
            part,
        ),
        out_specs=(
            rows,
            rows,
            whole,
            part,
            part,
            table,
            part,
            part,
            table,
            part,
            part,
            part,
            table,
            part,
            table,
            part,
        ),
        check_vma=False,
    )
```

time: 7170 us -> 1250 us (0.17)
  blocking collectives: 3620 us -> 20.6 us
  waiting for transfers between devices: 2870 us -> 448 us
  local copies, waits for them, and re-layouts: 161 us -> 310 us
  matrix products: 357 us -> 240 us
    psum x2 -> x0, blocking collectives: 3450 us -> none  [the longest x1 2490 us: shards(): lax.psum((key_grad_all[:, :SUMM], value_grad_all[:, :SUMM]), 'ctx')]
    all_gather x6 -> x8, waiting for transfers between devices: 1490 us -> 71.5 us  [the longest x4 71.5 us: settle(): return lax.all_gather(mine, PLANE, axis=axis, tiled=False)]
    unnamed x12 -> x13, waiting for transfers between devices: 1110 us -> 1.34 us
    ppermute x0 -> x97, waiting for transfers between devices: none -> 229 us  [swap(): lax.ppermute(array, axis, [(i, i ^ bit) for i in range(self.sizes[axis])])]
    reduce_scatter x2 -> x4, waiting for transfers between devices: 269 us -> 94.7 us  [settle(): mine = lax.psum_scatter(array, 'fsdp', scatter_dimension=0, tiled=True)]
    all_gather x9 -> x2, blocking collectives: 151 us -> 20.6 us  [the longest x1 14 us: shards(): lax.all_gather(small.reshape(-1, 128), 'fsdp', axis=0, tiled=True)]
    dot_general x33 -> x12, matrix products: 196 us -> 145 us  [the longest x6 47.4 us: dot(): return jnp.dot(left, right, preferred_element_type=f32)]
  transfers between devices with their start and end apart: 10 -> 110, of which waited for: 7 -> 38; matrix products, arithmetic and copies ran while one was open for 7% -> 41% of each run, Pallas kernels for 0% -> 0%
where the time goes in v1:
time: 1250 us
  waiting for transfers between devices  448 us (36%)
  local copies, waits for them, and re-layouts  310 us (25%)
  matrix products  240 us (19%)
  other arithmetic  152 us (12%)
  starting transfers between devices  58.2 us (5%)
  blocking collectives  20.6 us (2%)
  between operations  16.8 us (1%)
    ppermute x97, waiting for transfers between devices, swap(): lax.ppermute(array, axis, [(i, i ^ bit) for i in range(self.sizes[axis])])  229 us
    unnamed x226, local copies, waits for them, and re-layouts  119 us
    reduce_scatter x4, waiting for transfers between devices, settle(): mine = lax.psum_scatter(array, 'fsdp', scatter_dimension=0, tiled=True)  94.7 us
    all_gather x4, waiting for transfers between devices, settle(): return lax.all_gather(mine, PLANE, axis=axis, tiled=False)  71.5 us
    ppermute x97, starting transfers between devices, swap(): lax.ppermute(array, axis, [(i, i ^ bit) for i in range(self.sizes[axis])])  57.2 us
    psum x1, waiting for transfers between devices, shards(): totals = lax.psum(totals, ('fsdp', 'replica', 'ctx'))  51.1 us
    dot_general x4, matrix products, across(): lax.dot_general(left, right, (((0,), (0,)), ((), ())), preferred_element_...  50.4 us
    dot_general x6, matrix products, dot(): return jnp.dot(left, right, preferred_element_type=f32)  47.4 us
  transfers between devices with their start and end apart: 110, of which 38 were waited for; matrix products, arithmetic and copies ran while one was open for 41% of the time, Pallas kernels for 0%

profile of v1, /device:TPU:0, one launch (start us, length us, event | category | flops | bytes accessed | tf_op | source)
XLA Modules:
  0.0 1246.6 jit_solution(18444732551380461520)
XLA Ops:
  32.6 14.0 %all_gather.42 = bf16[192,128]{1,0:T(8,128)(2,1)S(1)} all-gather(bf16[48,128]{1,0:T(8,128)(2,1)S(1)} %bitcast.222), channel_id=1, replica_groups=mesh['fsdp'=4,'replica'=2,'ctx'=4] {'fsdp'}, dimensions={0}, use_global_device_ids=true | all-gather | bytes 61440 | tf_op jit(solution)/shard_map/all_gather | solution.py:213
  87.9 10.9 collective-permute-done.4
  124.1 11.2 fusion.11
  135.3 12.3 multiply_convert_fusion.2
  153.4 13.7 %reshape.430 = bf16[4,2,288,3,4,64]{2,1,0,5,4,3:T(2,128)(2,1)} reshape(bf16[2304,768]{0,1:T(8,128)(2,1)} %copy.56) | data formatting | bytes 7077888 | tf_op jit(solution)/shard_map/reshape | solution.py:254
  189.8 19.1 %fusion.87 = (f32[2,4,1088]{2,1,0:T(4,128)S(1)}, f32[2,4,1088,1152]{3,2,1,0:T(8,128)}) fusion(bf16[2,1088,4,64]{1,3,2,0:T(8,128)(2,1)S(1)} %reshape_squeeze.10, bf16[2,1152,4,64]{1,3,2,0:T(8,128)(2,1)S(1)} %reshape_squeeze.11, pred[2,1088,1152]{2,1,0:T(8,128)(4,1)} %broadcast_and_fusion), kind=kOutput, calls=%fused_computation.298 | convolution fusion | flops 1303502336 | bytes 44943360 | tf_op jit(solution)/shard_map/gqhd,gkhd->ghqk/dot_general | solution.py:152
  209.0 18.7 %fusion = f32[2,4,1088]{2,1,0:T(4,128)S(1)} fusion(f32[2,4,1088,1152]{3,2,1,0:T(8,128)} %get-tuple-element.174, f32[2,4,1088]{2,1,0:T(4,128)S(1)} %get-tuple-element.173), kind=kLoop, calls=%fused_computation.6 | loop fusion | flops 20045312 | bytes 40177664 | tf_op jit(solution)/shard_map/reduce_sum | solution.py:156
  227.8 14.9 %fusion.36 = bf16[2,1088,4,64]{1,3,2,0:T(8,128)(2,1)S(1)} fusion(bf16[2,1152,4,64]{1,3,2,0:T(8,128)(2,1)S(1)} %copy-done.25, f32[2,4,1088,1152]{3,2,1,0:T(8,128)} %get-tuple-element.174, f32[2,4,1088]{2,1,0:T(4,128)S(1)} %fusion, f32[2,4,1088]{2,1,0:T(4,128)S(1)} %get-tuple-element.173), kind=kOutput, calls=%fused_computation.65 | convolution fusion | flops 1314095104 | bytes 42471424 | tf_op jit(solution)/shard_map/ghqk,gkhd->gqhd/dot_general | solution.py:158
  276.9 8.4 collective-permute-done.23
  296.6 16.5 %collective-permute-done.24 = bf16[128,2048]{1,0:T(8,128)(2,1)S(1)} collective-permute-done((bf16[128,2048]{1,0:T(8,128)(2,1)S(1)}, bf16[128,2048]{1,0:T(8,128)(2,1)S(1)}, u32[]{:S(2)}, u32[]{:S(2)}) %collective-permute-start.24) | collective-permute-done | bytes 524320 | tf_op jit(solution)/shard_map/ppermute | solution.py:68
  324.6 9.4 collective-permute-done.25
  334.8 10.0 collective-permute-done.26
  351.1 9.7 collective-permute-done.29
  372.1 17.0 %multiply_convert_fusion.1 = (bf16[2176,1024]{1,0:T(8,128)(2,1)}, f32[2176,1024]{1,0:T(8,128)}) fusion(f32[1024]{0:T(1024)S(1)} %bitcast.225, bf16[2176,2048]{1,0:T(8,128)(2,1)} %constant_dynamic-update-slice_fusion.16, bf16[2048,1024]{1,0:T(8,128)(2,1)} %all-gather.17.cloned.1.call-done), kind=kOutput, calls=%fused_computation.30 | convolution fusion | flops 9140174848 | bytes 26480640 | tf_op jit(solution)/shard_map/dot_general | solution.py:22
  389.1 17.2 %convert_reduce_fusion.2 = (f32[1024]{0:T(1024)}, bf16[2176,1024]{1,0:T(8,128)(2,1)S(1)}) fusion(f32[2176,1024]{1,0:T(8,128)} %get-tuple-element.180, f32[1024]{0:T(1024)S(1)} %bitcast.226, bf16[2176,2048]{1,0:T(8,128)(2,1)} %constant_dynamic-update-slice_fusion.31, bf16[1024,2048]{1,0:T(8,128)(2,1)} %all-gather.19.cloned.1.call-done), kind=kOutput, calls=%fused_computation.29 | convolution fusion | flops 9155771392 | bytes 26484736 | tf_op jit(solution)/shard_map/dot_general | solution.py:30
  428.9 10.4 collective-permute-done.71
  450.5 14.7 %collective-permute-done.72 = bf16[128,2048]{1,0:T(8,128)(2,1)S(1)} collective-permute-done((bf16[128,2048]{1,0:T(8,128)(2,1)S(1)}, bf16[128,2048]{1,0:T(8,128)(2,1)S(1)}, u32[]{:S(2)}, u32[]{:S(2)}) %collective-permute-start.72) | collective-permute-done | bytes 524320 | tf_op jit(solution)/shard_map/ppermute | solution.py:68
  480.8 9.8 collective-permute-done.73
  506.8 9.5 collective-permute-done.77
  540.5 16.4 %fusion.33 = bf16[2,1152,4,64]{1,3,2,0:T(8,128)(2,1)} fusion(bf16[2,1088,4,64]{1,3,2,0:T(8,128)(2,1)S(1)} %reshape.433, f32[2,4,1088,1152]{3,2,1,0:T(8,128)} %get-tuple-element.174, f32[2,4,1088]{2,1,0:T(4,128)S(1)} %bitcast.195), kind=kOutput, calls=%fused_computation.64 | convolution fusion | flops 1304100864 | bytes 42436608 | tf_op jit(solution)/shard_map/ghqk,gqhd->gkhd/dot_general | solution.py:166
  556.9 26.1 %multiply_reduce_fusion = (f32[2,4,1088]{2,1,0:T(4,128)S(1)}, f32[2,4,1088,1152]{3,2,1,0:T(8,128)}) fusion(f32[2,4,1088,1152]{3,2,1,0:T(8,128)} %get-tuple-element.174, f32[2,4,1088]{2,1,0:T(4,128)S(1)} %bitcast.196, bf16[2,1088,4,64]{1,3,2,0:T(8,128)(2,1)S(1)} %reshape.433, bf16[2,1152,4,64]{1,3,2,0:T(8,128)(2,1)S(1)} %copy-done.26), kind=kOutput, calls=%fused_computation.2 | convolution fusion | flops 1313529344 | bytes 82579456 | tf_op jit(solution)/shard_map/gqhd,gkhd->ghqk/dot_general | solution.py:167
  583.0 32.4 %multiply_convert_fusion = bf16[2,4,1088,1152]{3,2,1,0:T(8,128)(2,1)} fusion(f32[2,4,1088,1152]{3,2,1,0:T(8,128)} %get-tuple-element.176, f32[2,4,1088,1152]{3,2,1,0:T(8,128)} %get-tuple-element.174, f32[2,4,1088]{2,1,0:T(4,128)S(1)} %get-tuple-element.175, f32[2,4,1088]{2,1,0:T(4,128)S(1)} %bitcast.197), kind=kLoop, calls=%fused_computation.1 | loop fusion | flops 40108032 | bytes 100339712 | tf_op jit(solution)/shard_map/convert_element_type | solution.py:169
  615.4 11.2 fusion.32
  626.6 9.9 fusion.31
  654.7 13.2 %convert_reduce_fusion.1 = (f32[768]{0:T(1024)S(1)}, bf16[4,2,288,768]{2,0,3,1:T(4,128)(2,1)}) fusion(bf16[4,2,288,256]{2,0,3,1:T(4,128)(2,1)} %bitcast.189, bf16[4,2,288,256]{2,0,3,1:T(4,128)(2,1)} %bitcast.190, bf16[4,2,272,256]{2,0,3,1:T(4,128)(2,1)} %bitcast.191), kind=kLoop, calls=%fused_computation.21 | loop fusion | flops 17693952 | bytes 7015424 | tf_op jit(solution)/shard_map/reduce_sum | solution.py:305
  668.0 8.2 copy.66
  676.2 12.5 %convolution_convert_fusion.11 = bf16[2048,768]{1,0:T(8,128)(2,1)} fusion(bf16[2304,2048]{1,0:T(8,128)(2,1)} %fusion.11, bf16[2304,768]{1,0:T(8,128)(2,1)} %bitcast.192), kind=kOutput, calls=%fused_computation.47 | convolution fusion | flops 7249330176 | bytes 16121856 | tf_op jit(solution)/shard_map/dot_general | solution.py:26
  688.8 15.2 %convolution_convert_fusion.10 = bf16[2048,1024]{1,0:T(8,128)(2,1)} fusion(bf16[2176,2048]{1,0:T(8,128)(2,1)} %constant_dynamic-update-slice_fusion.16, bf16[2176,1024]{1,0:T(8,128)(2,1)} %copy-done.68), kind=kOutput, calls=%fused_computation.46 | convolution fusion | flops 9128902656 | bytes 17563648 | tf_op jit(solution)/shard_map/dot_general | solution.py:26
  704.1 15.5 %convolution_convert_fusion.9 = bf16[1024,2048]{1,0:T(8,128)(2,1)} fusion(bf16[2176,1024]{1,0:T(8,128)(2,1)} %get-tuple-element.179, bf16[2176,2048]{1,0:T(8,128)(2,1)} %constant_dynamic-update-slice_fusion.31), kind=kOutput, calls=%fused_computation.45 | convolution fusion | flops 9128902656 | bytes 17563648 | tf_op jit(solution)/shard_map/dot_general | solution.py:26
  719.7 10.1 fusion.78
  769.8 9.6 collective-permute-done.92
  783.5 8.6 collective-permute-done.89
  793.5 11.9 collective-permute-done.93
  813.1 15.0 %reduce-scatter.9.cloned.1.call-done = bf16[512,1024]{1,0:T(8,128)(2,1)} async-done(((bf16[2048,1024]{1,0:T(8,128)(2,1)}), bf16[512,1024]{1,0:T(8,128)(2,1)}) %reduce-scatter.9.cloned.1.call-update) | async-done | bytes 1048592 | tf_op jit(solution)/shard_map/reduce_scatter | solution.py:316
  828.6 79.7 %reduce-scatter.11.cloned.1.call-done = bf16[256,2048]{1,0:T(8,128)(2,1)} async-done(((bf16[1024,2048]{1,0:T(8,128)(2,1)}), bf16[256,2048]{1,0:T(8,128)(2,1)}) %reduce-scatter.11.cloned.1.call-update) | async-done | bytes 1048592 | tf_op jit(solution)/shard_map/reduce_scatter | solution.py:316
  934.5 9.0 collective-permute-done.47
  955.0 14.4 %collective-permute-done.48 = bf16[128,2048]{1,0:T(8,128)(2,1)} collective-permute-done((bf16[128,2048]{1,0:T(8,128)(2,1)}, bf16[128,2048]{1,0:T(8,128)(2,1)}, u32[]{:S(2)}, u32[]{:S(2)}) %collective-permute-start.48) | collective-permute-done | bytes 524320 | tf_op jit(solution)/shard_map/ppermute | solution.py:68
  984.9 51.1 %all-reduce.4.cloned.1.call-done = f32[24576]{0:T(1024)} async-done(((f32[24576]{0:T(1024)}), f32[24576]{0:T(1024)}) %all-reduce.4.cloned.1.call-update) | async-done | bytes 98320 | tf_op jit(solution)/shard_map/psum | solution.py:347
  1038.7 28.0 %all-gather.23.cloned.1.call-done = bf16[512,2048]{1,0:T(8,128)(2,1)} async-done(((bf16[64,2048]{1,0:T(8,128)(2,1)}), bf16[512,2048]{1,0:T(8,128)(2,1)}) %all-gather.23.cloned.1.call-update) | async-done | bytes 2097168 | tf_op jit(solution)/shard_map/all_gather | solution.py:317
  1070.8 43.5 %all-gather.21.cloned.1.call-done = bf16[4096,768]{1,0:T(8,128)(2,1)} async-done(((bf16[512,768]{1,0:T(8,128)(2,1)}), bf16[4096,768]{1,0:T(8,128)(2,1)}) %all-gather.21.cloned.1.call-update) | async-done | bytes 6291472 | tf_op jit(solution)/shard_map/all_gather | solution.py:317
  1114.3 9.6 copy.67
  1123.9 23.2 %copy.85 = f32[96,8,8,512]{3,2,1,0:T(8,128)} copy(f32[96,8,8,512]{3,1,2,0:T(8,128)} %bitcast.177) | data formatting | bytes 25165824
  1147.0 18.0 %copy.68 = f32[512,12,8,64]{0,3,2,1:T(8,128)} copy(f32[512,12,8,64]{0,2,3,1:T(8,128)} %bitcast.178) | data formatting | bytes 25165824 | tf_op jit(solution)/shard_map/convert_element_type | solution.py:323
  1165.1 12.6 %copy.72 = f32[512,6144]{1,0:T(8,128)} copy(f32[512,6144]{0,1:T(8,128)} %bitcast.179) | data formatting | bytes 25165824
  1177.7 16.7 %reshape.453 = f32[8,512,4,256]{3,2,1,0:T(4,128)} reshape(bf16[4096,1024]{1,0:T(8,128)(2,1)} %all-gather.25.cloned.1.call-done) | data formatting | bytes 25165824 | tf_op jit(solution)/shard_map/convert_element_type | solution.py:321
  1194.3 15.5 %copy.70 = f32[512,4,8,256]{3,2,1,0:T(8,128)S(1)} copy(f32[512,4,8,256]{3,1,0,2:T(4,128)} %bitcast.175) | data formatting | bytes 33554432 | tf_op jit(solution)/shard_map/convert_element_type | solution.py:321
  1209.8 18.0 %copy.86 = f32[64,8,32,256]{3,1,2,0:T(8,128)} copy(f32[64,8,32,256]{3,2,1,0:T(8,128)S(1)} %bitcast.176) | data formatting | bytes 33554432
  1227.8 11.8 convert_element_type.541
  (590 shorter events, 415.6 us)
Async XLA Ops:
  7.2 128.1 %all-gather.13.cloned.1.call-start = ((), (), s32[]{:S(2)}) async-start(), calls=%async_computation.4 | async-start | bytes 3932160 | tf_op jit(solution)/shard_map/all_gather | solution.py:229
  14.3 234.4 %all-gather.15.cloned.1.call-start = ((), (), s32[]{:S(2)}) async-start(), calls=%async_computation.5 | async-start | bytes 1310720 | tf_op jit(solution)/shard_map/all_gather | solution.py:220
  15.1 357.0 %all-gather.17.cloned.1.call-start = ((), (), s32[]{:S(2)}) async-start(), calls=%async_computation.6 | async-start | bytes 5242880 | tf_op jit(solution)/shard_map/all_gather | solution.py:230
  17.7 371.4 %all-gather.19.cloned.1.call-start = ((), (), s32[]{:S(2)}) async-start(), calls=%async_computation.7 | async-start | bytes 5242880 | tf_op jit(solution)/shard_map/all_gather | solution.py:231
  18.6 39.4 %collective-permute-start = (bf16[144,2048]{1,0:T(8,128)(2,1)}, bf16[144,2048]{1,0:T(8,128)(2,1)S(1)}, u32[]{:S(2)}, u32[]{:S(2)}) collective-permute-start(bf16[144,2048]{1,0:T(8,128)(2,1)} %slice_bitcast_fusion.1), channel_id=1, source_target_pairs={{0,4},{4,0},{1,5},{5,1},{2,6},{6,2},{3,7},{7,3},{8,12},{12,8},{9,1... | collective-permute-start | bytes 1769480 | tf_op jit(solution)/shard_map/ppermute | solution.py:68
  21.5 41.3 %collective-permute-start.2 = (bf16[144,2048]{1,0:T(8,128)(2,1)}, bf16[144,2048]{1,0:T(8,128)(2,1)S(1)}, u32[]{:S(2)}, u32[]{:S(2)}) collective-permute-start(bf16[144,2048]{1,0:T(8,128)(2,1)} %slice_bitcast_fusion.1), channel_id=1, source_target_pairs={{0,2},{1,3},{2,0},{3,1},{4,6},{5,7},{6,4},{7,5},{8,10},{9,11},{10,... | collective-permute-start | bytes 1769480 | tf_op jit(solution)/shard_map/ppermute | solution.py:68
  25.2 34.2 %collective-permute-start.1 = (bf16[144,2048]{1,0:T(8,128)(2,1)}, bf16[144,2048]{1,0:T(8,128)(2,1)}, u32[]{:S(2)}, u32[]{:S(2)}) collective-permute-start(bf16[144,2048]{1,0:T(8,128)(2,1)} %get-tuple-element.88), channel_id=1, source_target_pairs={{0,4},{4,0},{1,5},{5,1},{2,6},{6,2},{3,7},{7,3},{8,12},{12,8},{9,1... | collective-permute-start | bytes 1769480 | tf_op jit(solution)/shard_map/ppermute | solution.py:68
  25.7 39.4 %collective-permute-start.3 = (bf16[144,2048]{1,0:T(8,128)(2,1)}, bf16[144,2048]{1,0:T(8,128)(2,1)S(1)}, u32[]{:S(2)}, u32[]{:S(2)}) collective-permute-start(bf16[144,2048]{1,0:T(8,128)(2,1)} %get-tuple-element.88), channel_id=1, source_target_pairs={{0,2},{1,3},{2,0},{3,1},{4,6},{5,7},{6,4},{7,5},{8,10},{9,11},{10,... | collective-permute-start | bytes 1769480 | tf_op jit(solution)/shard_map/ppermute | solution.py:68
  25.7 28.7 %collective-permute-start.14 = (s32[1]{0:T(128)}, s32[1]{0:T(128)}, u32[]{:S(2)}, u32[]{:S(2)}) collective-permute-start(s32[1]{0:T(128)} %param.19), channel_id=1, source_target_pairs={{0,4},{4,0},{1,5},{5,1},{2,6},{6,2},{3,7},{7,3},{8,12},{12,8},{9,1... | collective-permute-start | bytes 20 | tf_op jit(solution)/shard_map/ppermute | solution.py:68
  30.1 781.7 %reduce-scatter.7.cloned.1.call-start = ((), (), s32[]{:S(2)}) async-start(), calls=%async_computation.10 | async-start | bytes 1310720 | tf_op jit(solution)/shard_map/reduce_scatter | solution.py:316
  54.5 47.6 %collective-permute-start.6 = (bf16[144,2048]{1,0:T(8,128)(2,1)}, bf16[144,2048]{1,0:T(8,128)(2,1)S(1)}, u32[]{:S(2)}, u32[]{:S(2)}) collective-permute-start(bf16[144,2048]{1,0:T(8,128)(2,1)} %slice_bitcast_fusion.1), channel_id=1, source_target_pairs={{0,1},{1,0},{2,3},{3,2},{4,5},{5,4},{6,7},{7,6},{8,9},{9,8},{10,11... | collective-permute-start | bytes 1769480 | tf_op jit(solution)/shard_map/ppermute | solution.py:68
  59.3 27.1 %collective-permute-start.51 = (bf16[144,2048]{1,0:T(8,128)(2,1)}, bf16[144,2048]{1,0:T(8,128)(2,1)S(1)}, u32[]{:S(2)}, u32[]{:S(2)}) collective-permute-start(bf16[144,2048]{1,0:T(8,128)(2,1)} %slice_bitcast_fusion), channel_id=1, source_target_pairs={{0,2},{1,3},{2,0},{3,1},{4,6},{5,7},{6,4},{7,5},{8,10},{9,11},{10,... | collective-permute-start | bytes 1769480 | tf_op jit(solution)/shard_map/ppermute | solution.py:68
  74.4 24.5 %collective-permute-start.4 = (bf16[144,2048]{1,0:T(8,128)(2,1)S(1)}, bf16[144,2048]{1,0:T(8,128)(2,1)S(1)}, u32[]{:S(2)}, u32[]{:S(2)}) collective-permute-start(bf16[144,2048]{1,0:T(8,128)(2,1)S(1)} %collective-permute-done), channel_id=1, source_target_pairs={{0,2},{1,3},{2,0},{3,1},{4,6},{5,7},{6,4},{7,5},{8,10},{9,11},{10,... | collective-permute-start | bytes 1769480 | tf_op jit(solution)/shard_map/ppermute | solution.py:68
  87.5 172.7 %collective-permute-start.55 = (bf16[144,2048]{1,0:T(8,128)(2,1)}, bf16[144,2048]{1,0:T(8,128)(2,1)}, u32[]{:S(2)}, u32[]{:S(2)}) collective-permute-start(bf16[144,2048]{1,0:T(8,128)(2,1)} %slice_bitcast_fusion), channel_id=1, source_target_pairs={{0,1},{1,0},{2,3},{3,2},{4,5},{5,4},{6,7},{7,6},{8,9},{9,8},{10,11... | collective-permute-start | bytes 1769480 | tf_op jit(solution)/shard_map/ppermute | solution.py:68
  98.9 155.0 %collective-permute-start.54 = (bf16[128,2048]{1,0:T(8,128)(2,1)}, bf16[128,2048]{1,0:T(8,128)(2,1)}, u32[]{:S(2)}, u32[]{:S(2)}) collective-permute-start(bf16[128,2048]{1,0:T(8,128)(2,1)} %collective-permute-done.52), channel_id=1, source_target_pairs={{0,4},{4,0},{1,5},{5,1},{2,6},{6,2},{3,7},{7,3},{8,12},{12,8},{9,1... | collective-permute-start | bytes 1572872 | tf_op jit(solution)/shard_map/ppermute | solution.py:68
  108.0 145.9 %collective-permute-start.53 = (bf16[144,2048]{1,0:T(8,128)(2,1)}, bf16[144,2048]{1,0:T(8,128)(2,1)}, u32[]{:S(2)}, u32[]{:S(2)}) collective-permute-start(bf16[144,2048]{1,0:T(8,128)(2,1)} %collective-permute-done.49), channel_id=1, source_target_pairs={{0,2},{1,3},{2,0},{3,1},{4,6},{5,7},{6,4},{7,5},{8,10},{9,11},{10,... | collective-permute-start | bytes 1769480 | tf_op jit(solution)/shard_map/ppermute | solution.py:68
  265.3 52.9 %collective-permute-start.60 = (bf16[128,2048]{1,0:T(8,128)(2,1)}, bf16[128,2048]{1,0:T(8,128)(2,1)S(1)}, u32[]{:S(2)}, u32[]{:S(2)}) collective-permute-start(bf16[128,2048]{1,0:T(8,128)(2,1)} %collective-permute-done.52), channel_id=1, source_target_pairs={{0,1},{1,0},{2,3},{3,2},{4,5},{5,4},{6,7},{7,6},{8,9},{9,8},{10,11... | collective-permute-start | bytes 1572872 | tf_op jit(solution)/shard_map/ppermute | solution.py:68
  265.8 24.5 %collective-permute-start.59 = (bf16[144,2048]{1,0:T(8,128)(2,1)S(1)}, bf16[144,2048]{1,0:T(8,128)(2,1)S(1)}, u32[]{:S(2)}, u32[]{:S(2)}) collective-permute-start(bf16[144,2048]{1,0:T(8,128)(2,1)S(1)} %copy-done.36), channel_id=1, source_target_pairs={{0,1},{1,0},{2,3},{3,2},{4,5},{5,4},{6,7},{7,6},{8,9},{9,8},{10,11... | collective-permute-start | bytes 1769480 | tf_op jit(solution)/shard_map/ppermute | solution.py:68
  285.3 28.0 %collective-permute-start.17 = (bf16[144,2048]{1,0:T(8,128)(2,1)S(1)}, bf16[144,2048]{1,0:T(8,128)(2,1)S(1)}, u32[]{:S(2)}, u32[]{:S(2)}) collective-permute-start(bf16[144,2048]{1,0:T(8,128)(2,1)S(1)} %slice.474), channel_id=1, source_target_pairs={{0,4},{4,0},{1,5},{5,1},{2,6},{6,2},{3,7},{7,3},{8,12},{12,8},{9,1... | collective-permute-start | bytes 1769480 | tf_op jit(solution)/shard_map/ppermute | solution.py:68
  296.6 27.2 %collective-permute-start.62 = (bf16[128,2048]{1,0:T(8,128)(2,1)}, bf16[128,2048]{1,0:T(8,128)(2,1)S(1)}, u32[]{:S(2)}, u32[]{:S(2)}) collective-permute-start(bf16[128,2048]{1,0:T(8,128)(2,1)} %collective-permute-done.54), channel_id=1, source_target_pairs={{0,1},{1,0},{2,3},{3,2},{4,5},{5,4},{6,7},{7,6},{8,9},{9,8},{10,11... | collective-permute-start | bytes 1572872 | tf_op jit(solution)/shard_map/ppermute | solution.py:68
  319.0 25.8 %collective-permute-start.26 = (bf16[128,2048]{1,0:T(8,128)(2,1)S(1)}, bf16[128,2048]{1,0:T(8,128)(2,1)S(1)}, u32[]{:S(2)}, u32[]{:S(2)}) collective-permute-start(bf16[128,2048]{1,0:T(8,128)(2,1)S(1)} %slice.489), channel_id=1, source_target_pairs={{0,4},{4,0},{1,5},{5,1},{2,6},{6,2},{3,7},{7,3},{8,12},{12,8},{9,1... | collective-permute-start | bytes 1572872 | tf_op jit(solution)/shard_map/ppermute | solution.py:68
  321.7 27.3 %collective-permute-start.27 = (bf16[144,2048]{1,0:T(8,128)(2,1)S(1)}, bf16[144,2048]{1,0:T(8,128)(2,1)S(1)}, u32[]{:S(2)}, u32[]{:S(2)}) collective-permute-start(bf16[144,2048]{1,0:T(8,128)(2,1)S(1)} %slice.488), channel_id=1, source_target_pairs={{0,2},{1,3},{2,0},{3,1},{4,6},{5,7},{6,4},{7,5},{8,10},{9,11},{10,... | collective-permute-start | bytes 1769480 | tf_op jit(solution)/shard_map/ppermute | solution.py:68
  323.4 25.6 %collective-permute-start.28 = (bf16[128,2048]{1,0:T(8,128)(2,1)S(1)}, bf16[128,2048]{1,0:T(8,128)(2,1)S(1)}, u32[]{:S(2)}, u32[]{:S(2)}) collective-permute-start(bf16[128,2048]{1,0:T(8,128)(2,1)S(1)} %slice.489), channel_id=1, source_target_pairs={{0,2},{1,3},{2,0},{3,1},{4,6},{5,7},{6,4},{7,5},{8,10},{9,11},{10,... | collective-permute-start | bytes 1572872 | tf_op jit(solution)/shard_map/ppermute | solution.py:68
  324.6 39.6 %collective-permute-start.31 = (bf16[144,2048]{1,0:T(8,128)(2,1)S(1)}, bf16[144,2048]{1,0:T(8,128)(2,1)S(1)}, u32[]{:S(2)}, u32[]{:S(2)}) collective-permute-start(bf16[144,2048]{1,0:T(8,128)(2,1)S(1)} %slice.488), channel_id=1, source_target_pairs={{0,1},{1,0},{2,3},{3,2},{4,5},{5,4},{6,7},{7,6},{8,9},{9,8},{10,11... | collective-permute-start | bytes 1769480 | tf_op jit(solution)/shard_map/ppermute | solution.py:68
  334.0 31.6 %collective-permute-start.32 = (bf16[128,2048]{1,0:T(8,128)(2,1)S(1)}, bf16[128,2048]{1,0:T(8,128)(2,1)S(1)}, u32[]{:S(2)}, u32[]{:S(2)}) collective-permute-start(bf16[128,2048]{1,0:T(8,128)(2,1)S(1)} %slice.489), channel_id=1, source_target_pairs={{0,1},{1,0},{2,3},{3,2},{4,5},{5,4},{6,7},{7,6},{8,9},{9,8},{10,11... | collective-permute-start | bytes 1572872 | tf_op jit(solution)/shard_map/ppermute | solution.py:68
  426.7 23.8 %collective-permute-start.70 = (bf16[128,2048]{1,0:T(8,128)(2,1)S(1)}, bf16[128,2048]{1,0:T(8,128)(2,1)S(1)}, u32[]{:S(2)}, u32[]{:S(2)}) collective-permute-start(bf16[128,2048]{1,0:T(8,128)(2,1)S(1)} %slice.525), channel_id=1, source_target_pairs={{0,2},{1,3},{2,0},{3,1},{4,6},{5,7},{6,4},{7,5},{8,10},{9,11},{10,... | collective-permute-start | bytes 1572872 | tf_op jit(solution)/shard_map/ppermute | solution.py:68
  427.1 38.9 %collective-permute-start.65 = (bf16[144,2048]{1,0:T(8,128)(2,1)S(1)}, bf16[144,2048]{1,0:T(8,128)(2,1)S(1)}, u32[]{:S(2)}, u32[]{:S(2)}) collective-permute-start(bf16[144,2048]{1,0:T(8,128)(2,1)S(1)} %slice.517), channel_id=1, source_target_pairs={{0,4},{4,0},{1,5},{5,1},{2,6},{6,2},{3,7},{7,3},{8,12},{12,8},{9,1... | collective-permute-start | bytes 1769480 | tf_op jit(solution)/shard_map/ppermute | solution.py:68
  439.4 25.8 %collective-permute-start.72 = (bf16[128,2048]{1,0:T(8,128)(2,1)S(1)}, bf16[128,2048]{1,0:T(8,128)(2,1)S(1)}, u32[]{:S(2)}, u32[]{:S(2)}) collective-permute-start(bf16[128,2048]{1,0:T(8,128)(2,1)S(1)} %add_convert_fusion.18), channel_id=1, source_target_pairs={{0,4},{4,0},{1,5},{5,1},{2,6},{6,2},{3,7},{7,3},{8,12},{12,8},{9,1... | collective-permute-start | bytes 1572872 | tf_op jit(solution)/shard_map/ppermute | solution.py:68
  474.3 25.3 %collective-permute-start.74 = (bf16[128,2048]{1,0:T(8,128)(2,1)}, bf16[128,2048]{1,0:T(8,128)(2,1)}, u32[]{:S(2)}, u32[]{:S(2)}) collective-permute-start(bf16[128,2048]{1,0:T(8,128)(2,1)} %slice.529), channel_id=1, source_target_pairs={{0,4},{4,0},{1,5},{5,1},{2,6},{6,2},{3,7},{7,3},{8,12},{12,8},{9,1... | collective-permute-start | bytes 1572872 | tf_op jit(solution)/shard_map/ppermute | solution.py:68
  478.6 27.8 %collective-permute-start.75 = (bf16[144,2048]{1,0:T(8,128)(2,1)}, bf16[144,2048]{1,0:T(8,128)(2,1)S(1)}, u32[]{:S(2)}, u32[]{:S(2)}) collective-permute-start(bf16[144,2048]{1,0:T(8,128)(2,1)} %slice.528), channel_id=1, source_target_pairs={{0,2},{1,3},{2,0},{3,1},{4,6},{5,7},{6,4},{7,5},{8,10},{9,11},{10,... | collective-permute-start | bytes 1769480 | tf_op jit(solution)/shard_map/ppermute | solution.py:68
  479.0 27.4 %collective-permute-start.76 = (bf16[128,2048]{1,0:T(8,128)(2,1)}, bf16[128,2048]{1,0:T(8,128)(2,1)S(1)}, u32[]{:S(2)}, u32[]{:S(2)}) collective-permute-start(bf16[128,2048]{1,0:T(8,128)(2,1)} %slice.529), channel_id=1, source_target_pairs={{0,2},{1,3},{2,0},{3,1},{4,6},{5,7},{6,4},{7,5},{8,10},{9,11},{10,... | collective-permute-start | bytes 1572872 | tf_op jit(solution)/shard_map/ppermute | solution.py:68
  480.7 40.0 %collective-permute-start.79 = (bf16[144,2048]{1,0:T(8,128)(2,1)}, bf16[144,2048]{1,0:T(8,128)(2,1)S(1)}, u32[]{:S(2)}, u32[]{:S(2)}) collective-permute-start(bf16[144,2048]{1,0:T(8,128)(2,1)} %slice.528), channel_id=1, source_target_pairs={{0,1},{1,0},{2,3},{3,2},{4,5},{5,4},{6,7},{7,6},{8,9},{9,8},{10,11... | collective-permute-start | bytes 1769480 | tf_op jit(solution)/shard_map/ppermute | solution.py:68
  490.6 30.8 %collective-permute-start.80 = (bf16[128,2048]{1,0:T(8,128)(2,1)}, bf16[128,2048]{1,0:T(8,128)(2,1)S(1)}, u32[]{:S(2)}, u32[]{:S(2)}) collective-permute-start(bf16[128,2048]{1,0:T(8,128)(2,1)} %slice.529), channel_id=1, source_target_pairs={{0,1},{1,0},{2,3},{3,2},{4,5},{5,4},{6,7},{7,6},{8,9},{9,8},{10,11... | collective-permute-start | bytes 1572872 | tf_op jit(solution)/shard_map/ppermute | solution.py:68
  654.7 157.7 %reduce-scatter.5.cloned.1.call-start = ((), (), s32[]{:S(2)}) async-start(), calls=%async_computation.9 | async-start | bytes 3932160 | tf_op jit(solution)/shard_map/reduce_scatter | solution.py:316
  688.8 139.4 %reduce-scatter.9.cloned.1.call-start = ((), (), s32[]{:S(2)}) async-start(), calls=%async_computation.11 | async-start | bytes 5242880 | tf_op jit(solution)/shard_map/reduce_scatter | solution.py:316
  704.1 204.2 %reduce-scatter.11.cloned.1.call-start = ((), (), s32[]{:S(2)}) async-start(), calls=%async_computation.12 | async-start | bytes 5242880 | tf_op jit(solution)/shard_map/reduce_scatter | solution.py:316
  719.6 316.4 %all-reduce.4.cloned.1.call-start = ((), (), s32[]{:S(2)}) async-start(), calls=%async_computation.8 | async-start | bytes 196608 | tf_op jit(solution)/shard_map/psum | solution.py:347
  766.0 26.1 %collective-permute-start.89 = (bf16[144,2048]{1,0:T(8,128)(2,1)}, bf16[144,2048]{1,0:T(8,128)(2,1)S(1)}, u32[]{:S(2)}, u32[]{:S(2)}) collective-permute-start(bf16[144,2048]{1,0:T(8,128)(2,1)} %slice.537), channel_id=1, source_target_pairs={{0,4},{4,0},{1,5},{5,1},{2,6},{6,2},{3,7},{7,3},{8,12},{12,8},{9,1... | collective-permute-start | bytes 1769480 | tf_op jit(solution)/shard_map/ppermute | solution.py:68
  767.8 25.6 %collective-permute-start.94 = (bf16[144,2048]{1,0:T(8,128)(2,1)}, bf16[144,2048]{1,0:T(8,128)(2,1)S(1)}, u32[]{:S(2)}, u32[]{:S(2)}) collective-permute-start(bf16[144,2048]{1,0:T(8,128)(2,1)} %slice.545), channel_id=1, source_target_pairs={{0,2},{1,3},{2,0},{3,1},{4,6},{5,7},{6,4},{7,5},{8,10},{9,11},{10,... | collective-permute-start | bytes 1769480 | tf_op jit(solution)/shard_map/ppermute | solution.py:68
  780.4 25.0 %collective-permute-start.93 = (bf16[144,2048]{1,0:T(8,128)(2,1)}, bf16[144,2048]{1,0:T(8,128)(2,1)S(1)}, u32[]{:S(2)}, u32[]{:S(2)}) collective-permute-start(bf16[144,2048]{1,0:T(8,128)(2,1)} %add_convert_fusion.14), channel_id=1, source_target_pairs={{0,2},{1,3},{2,0},{3,1},{4,6},{5,7},{6,4},{7,5},{8,10},{9,11},{10,... | collective-permute-start | bytes 1769480 | tf_op jit(solution)/shard_map/ppermute | solution.py:68
  781.8 23.6 %collective-permute-start.96 = (bf16[144,2048]{1,0:T(8,128)(2,1)}, bf16[144,2048]{1,0:T(8,128)(2,1)}, u32[]{:S(2)}, u32[]{:S(2)}) collective-permute-start(bf16[144,2048]{1,0:T(8,128)(2,1)} %add_convert_fusion.13), channel_id=1, source_target_pairs={{0,4},{4,0},{1,5},{5,1},{2,6},{6,2},{3,7},{7,3},{8,12},{12,8},{9,1... | collective-permute-start | bytes 1769480 | tf_op jit(solution)/shard_map/ppermute | solution.py:68
  811.7 254.9 %all-gather.23.cloned.1.call-start = ((), (), s32[]{:S(2)}) async-start(), calls=%async_computation.14 | async-start | bytes 2359296 | tf_op jit(solution)/shard_map/all_gather | solution.py:317
  812.3 302.0 %all-gather.21.cloned.1.call-start = ((), (), s32[]{:S(2)}) async-start(), calls=%async_computation.13 | async-start | bytes 7077888 | tf_op jit(solution)/shard_map/all_gather | solution.py:317
  813.1 364.6 %all-gather.25.cloned.1.call-start = ((), (), s32[]{:S(2)}) async-start(), calls=%async_computation.15 | async-start | bytes 9437184 | tf_op jit(solution)/shard_map/all_gather | solution.py:317
  828.1 399.7 %all-gather.27.cloned.1.call-start = ((), (), s32[]{:S(2)}) async-start(), calls=%async_computation.16 | async-start | bytes 9437184 | tf_op jit(solution)/shard_map/all_gather | solution.py:317
  934.0 37.2 %collective-permute-start.41 = (bf16[144,2048]{1,0:T(8,128)(2,1)}, bf16[144,2048]{1,0:T(8,128)(2,1)S(1)}, u32[]{:S(2)}, u32[]{:S(2)}) collective-permute-start(bf16[144,2048]{1,0:T(8,128)(2,1)} %slice.498), channel_id=1, source_target_pairs={{0,4},{4,0},{1,5},{5,1},{2,6},{6,2},{3,7},{7,3},{8,12},{12,8},{9,1... | collective-permute-start | bytes 1769480 | tf_op jit(solution)/shard_map/ppermute | solution.py:68
  944.4 25.0 %collective-permute-start.48 = (bf16[128,2048]{1,0:T(8,128)(2,1)}, bf16[128,2048]{1,0:T(8,128)(2,1)}, u32[]{:S(2)}, u32[]{:S(2)}) collective-permute-start(bf16[128,2048]{1,0:T(8,128)(2,1)} %add_convert_fusion.19), channel_id=1, source_target_pairs={{0,4},{4,0},{1,5},{5,1},{2,6},{6,2},{3,7},{7,3},{8,12},{12,8},{9,1... | collective-permute-start | bytes 1572872 | tf_op jit(solution)/shard_map/ppermute | solution.py:68
  947.5 23.7 %collective-permute-start.45 = (bf16[144,2048]{1,0:T(8,128)(2,1)}, bf16[144,2048]{1,0:T(8,128)(2,1)}, u32[]{:S(2)}, u32[]{:S(2)}) collective-permute-start(bf16[144,2048]{1,0:T(8,128)(2,1)} %add_convert_fusion.16), channel_id=1, source_target_pairs={{0,2},{1,3},{2,0},{3,1},{4,6},{5,7},{6,4},{7,5},{8,10},{9,11},{10,... | collective-permute-start | bytes 1769480 | tf_op jit(solution)/shard_map/ppermute | solution.py:68
  (131 other events, 1269.8 us)
Sparse Core Ops, SparseCore 0:
  14.4 66.8 all-gather.12
  83.4 26.6 all-gather.14
  111.7 80.2 all-gather.16
  193.4 79.2 all-gather.18
  654.8 26.2 reduce-scatter.6
  688.9 59.3 reduce-scatter.4
  751.3 76.7 reduce-scatter.8
  831.0 77.2 reduce-scatter.10
  914.8 121.1 all-reduce.3
  1037.9 28.7 all-gather.22
  1068.7 45.5 all-gather.20
  1116.2 54.3 all-gather.24
  1172.7 54.3 all-gather.26

commit v2 on v1

v2 whole, which is shorter than its diff:
```python
import functools

import jax
import jax.numpy as jnp
import numpy as np
from jax import lax
from jax.experimental import pallas as pl
from jax.experimental.pallas import tpu as pltpu
from jax.sharding import PartitionSpec as P

D = 2048
HEADS = 32
HEAD_DIM = 64
SUMM = 50
SEQ_LEN = 1088
SEG = 1038
MEM_ROWS = 16
LANES = 128
QUERY_BLOCK = 256
ROW_BLOCK = 64

epsilon = 1e-05
masked = -1e30
f32 = jnp.float32
bf16 = jnp.bfloat16
PLANE = ("replica", "ctx")


def dot(left, right):
    return jnp.dot(left, right, preferred_element_type=f32)


def across(left, right):
    return lax.dot_general(left, right, (((0,), (0,)), ((), ())), preferred_element_type=f32)


def against(left, right):
    return lax.dot_general(left, right, (((1,), (1,)), ((), ())), preferred_element_type=f32)


def normal_of(rows):
    centred = rows - jnp.mean(rows, axis=-1, keepdims=True)
    inverse = lax.rsqrt(jnp.mean(centred * centred, axis=-1, keepdims=True) + epsilon)
    return centred * inverse, inverse


def norm_input_grad(upstream, normal, inverse, weight):
    scaled = upstream * weight
    centre = jnp.mean(scaled, axis=-1, keepdims=True)
    slope = jnp.mean(scaled * normal, axis=-1, keepdims=True)
    return inverse * (scaled - centre - normal * slope)


class Plane:
    def __init__(self):
        self.replicas = lax.axis_size("replica")
        self.spans = lax.axis_size("ctx")
        self.sizes = {"replica": self.replicas, "ctx": self.spans}
        self.slow = []
        for axis, bit in (("replica", 1), ("ctx", 2)):
            while bit < self.sizes[axis]:
                self.slow.append((axis, bit))
                bit *= 2
        self.fast = ("ctx", 1)
        self.near = [(r, v) for v in range(0, self.spans, 2) for r in range(self.replicas)]
        self.far = [(r, v + 1) for r, v in self.near]
        self.half = len(self.near)

    def swap(self, array, stage=None):
        axis, bit = stage or self.fast
        return lax.ppermute(array, axis, [(i, i ^ bit) for i in range(self.sizes[axis])])

    def step(self, name, stage):
        axis, bit = stage
        return (name[0] ^ bit, name[1]) if axis == "replica" else (name[0], name[1] ^ bit)

    def bit(self, name, stage):
        axis, bit = stage
        return (name[0] if axis == "replica" else name[1]) & bit

    def send(self, rows, cut=None):
        cut = cut or cut_of(rows.shape[0])
        sides = [rows[:cut], rows[cut:]]
        return [[self.swap(side, stage) for stage in plan] for side, plan in zip(sides, (self.slow, self.slow[::-1]))]

    def travel(self, rows, fills=(), cut=None, first=None):
        cut = cut or cut_of(rows.shape[0])
        plans = [self.slow, self.slow[::-1]]
        found = [{(0, 0): rows[:cut]}, {(0, 0): rows[cut:]}]
        first = first or self.send(rows, cut)
        results = []
        for level in range(len(self.slow)):
            arrived = []
            for side in range(2):
                stage = plans[side][level]
                for name, value in list(found[side].items()):
                    moved = first[side][level] if name == (0, 0) else self.swap(value, stage)
                    name = self.step(name, stage)
                    found[side][name] = moved
                    if level == 0 or name != self.step((0, 0), stage):
                        arrived.append((side, name))
            if level < len(fills) and fills[level] is not None:
                filled = fills[level]()
                side, name = arrived[-1]
                found[side][name], filled = lax.optimization_barrier((found[side][name], filled))
                results.append(filled)
        return found, results

    def gather(self, rows, fills=(), first=None):
        found, results = self.travel(rows, fills, None, first)
        return jnp.concatenate([found[side][name] for name in self.near for side in range(2)], axis=0), results

    def sides(self, found):
        sides = [[found[side][name] for name in self.near] for side in range(2)]
        return [side + [self.swap(value) for value in side] for side in sides]

    def spread(self, block, cut=None, first=None):
        return self.sides(self.travel(block, (), cut, first)[0])

    def scatter(self, partial, fills=(), before=()):
        count = partial.shape[0] // self.half
        cut = cut_of(count)
        held = [{}, {}]
        for index, name in enumerate(self.near):
            held[0][name] = partial[index * count : index * count + cut]
            held[1][name] = partial[index * count + cut : (index + 1) * count]
        plans = [self.slow, self.slow[::-1]]
        results = []
        for level in range(len(self.slow)):
            moves = []
            for side in range(2):
                stage = plans[side][level]
                for name in reversed(held[side]):
                    if not self.bit(name, stage):
                        moves.append((side, name, held[side][self.step(name, stage)], stage))
            filled = None
            if level < len(fills):
                filled = fills[level](moves[-1][2])
            if before and level == 0:
                moves = [(*move[:2], gate([move[2]], *before)[0], move[3]) if move[1] != (0, 0) else move for move in moves]
            kept = [{}, {}]
            for number, (side, name, value, stage) in enumerate(moves):
                moved = self.swap(value, stage)
                if filled is not None and number == len(moves) - 1:
                    moved, filled = lax.optimization_barrier((moved, filled))
                    results.append(filled)
                total = held[side][name].astype(f32) + moved.astype(f32)
                kept[side][name] = total if name == (0, 0) else total.astype(bf16)
            held = kept
        for fill in fills[len(self.slow) :]:
            results.append(fill(held[0][(0, 0)]))
        return jnp.concatenate([held[0][(0, 0)], held[1][(0, 0)]], axis=0), results

    def whole(self, block):
        found = {(0, 0): block}
        firsts = [self.step((0, 0), stage) for stage in self.slow]
        for name, stage in zip(firsts, self.slow):
            found[name] = self.swap(block, stage)
        return found

    def complete(self, found, turned, before=()):
        if before:
            names = [name for name in found if name != (0, 0)]
            held = gate([found[name] for name in names], *before)
            found = {(0, 0): found[(0, 0)], **dict(zip(names, held))}
        for stage in self.slow[::-1] if turned else self.slow:
            for name, value in list(found.items()):
                name = self.step(name, stage)
                if name not in found:
                    found[name] = self.swap(value, stage)
        near = [found[name] for name in self.near]
        return [near + [self.swap(value) for value in near]]


def cut_of(count):
    return (count // 2 + 15) // 16 * 16


def columns_of(weight, groups, index, width, order=None):
    span = weight.shape[1] // groups
    order = range(groups) if order is None else order
    return jnp.concatenate(
        [lax.dynamic_slice_in_dim(weight, g * span + index * width, width, 1) for g in order], axis=1
    )


def allowed_of(plane, span_rows, own, lengths):
    places, slots = [], []
    for value in [v for _, v in plane.near + plane.far if _ == 0]:
        base = own ^ value
        rows = jnp.arange(span_rows, dtype=jnp.int32) + base * span_rows
        mem = jnp.arange(MEM_ROWS, dtype=jnp.int32) + base * MEM_ROWS
        places.append((rows, mem))
    far = jnp.int32(1 << 30)
    queries = jnp.concatenate([rows for rows, _ in places])
    keys = jnp.concatenate([jnp.concatenate([rows, jnp.where(mem < SUMM, -1, far)]) for rows, mem in places])
    causal = keys[None, :] <= queries[:, None]
    present = (keys[None, :] < lengths[:, None]) | (keys[None, :] >= SEG)
    return causal[None] & present[:, None, :]


def attend(query, key, value, allowed):
    scores = jnp.einsum("gqhd,gkhd->ghqk", query, key, preferred_element_type=f32)
    scores = jnp.where(allowed[:, None], scores, masked)
    largest = jnp.max(scores, axis=-1, keepdims=True)
    expanded = jnp.exp(scores - largest)
    totals = jnp.sum(expanded, axis=-1, keepdims=True)
    weights = (expanded / totals).astype(bf16)
    mixed = jnp.einsum("ghqk,gkhd->gqhd", weights, value, preferred_element_type=f32)
    return mixed.astype(bf16), largest + jnp.log(totals)


def attend_back(query, key, value, upstream, log_totals, allowed):
    scores = jnp.einsum("gqhd,gkhd->ghqk", query, key, preferred_element_type=f32)
    scores = jnp.where(allowed[:, None], scores, masked)
    weights = jnp.exp(scores - log_totals)
    value_grad = jnp.einsum("ghqk,gqhd->gkhd", weights.astype(bf16), upstream, preferred_element_type=f32)
    weight_grad = jnp.einsum("gqhd,gkhd->ghqk", upstream, value, preferred_element_type=f32)
    centre = jnp.sum(weights * weight_grad, axis=-1, keepdims=True)
    score_grad = (weights * (weight_grad - centre)).astype(bf16)
    query_grad = jnp.einsum("ghqk,gkhd->gqhd", score_grad, key, preferred_element_type=f32)
    key_grad = jnp.einsum("ghqk,gqhd->gkhd", score_grad, query, preferred_element_type=f32)
    return query_grad.astype(bf16) * 0.125, key_grad.astype(bf16), value_grad.astype(bf16)


def blocks_of(count):
    starts = list(range(0, count, QUERY_BLOCK))
    return [(s, min(QUERY_BLOCK, count - s)) for s in starts]


def piece_of(own, c):
    v = jnp.bitwise_xor(own, c)
    return jnp.right_shift(v, 1), jnp.bitwise_and(v, 1) == 0


def to_sequence(spans, span_rows, own, near, far, target, with_slots=True):
    base = spans * MEM_ROWS
    for c in range(spans):
        slot, is_near = piece_of(own, c)
        rows = jnp.where(is_near, near[slot, 0, :span_rows, :], far[slot, 0, :span_rows, :])
        target[base + c * span_rows : base + (c + 1) * span_rows] = rows
        if with_slots:
            rows = jnp.where(is_near, near[slot, 0, span_rows:, :], far[slot, 0, span_rows:, :])
            target[c * MEM_ROWS : (c + 1) * MEM_ROWS] = rows
    if not with_slots:
        target[:base] = jnp.zeros((base, target.shape[1]), target.dtype)


def key_bias(length, spans, seq_len):
    base = spans * MEM_ROWS
    shape = (base + seq_len, LANES)
    row = lax.broadcasted_iota(jnp.int32, shape, 0)
    place = row - base
    good = (row < SUMM) | ((place >= 0) & ((place < length) | (place >= SEG)))
    return jnp.where(good, 0.0, masked).astype(f32)


def head_masks(count):
    lane = lax.broadcasted_iota(jnp.int32, (count, LANES), 1)
    return lane < HEAD_DIM, lane == HEAD_DIM, lane == 0


def headed(array, masks, head):
    return jnp.where(masks[0] if head == 0 else ~masks[0], array, 0.0)


def scores_of(keys, query, start, size, base):
    stop = start + size
    scores = against(keys[:stop], query[start:stop])
    tail = scores[start:stop]
    row = lax.broadcasted_iota(jnp.int32, (size, size), 0)
    column = lax.broadcasted_iota(jnp.int32, (size, size), 1)
    seen = row <= column
    if start < base:
        seen = seen | (row < base - start)
    tail = jnp.where(seen, tail, masked)
    return tail if start == 0 else jnp.concatenate([scores[:start], tail], axis=0)


def attend_kernel(spans, span_rows, info, qn, qf, kn, kf, vn, vf, on, of, lse_ref, q_all, k_all, v_all, o_all):
    count = k_all.shape[0]
    base = spans * MEM_ROWS
    own = info[0]
    to_sequence(spans, span_rows, own, qn, qf, q_all)
    to_sequence(spans, span_rows, own, kn, kf, k_all)
    to_sequence(spans, span_rows, own, vn, vf, v_all)
    masks = head_masks(count)
    bias = key_bias(info[1 + pl.program_id(0)], spans, count - base)
    query, key = q_all[...].astype(f32), k_all[...].astype(f32)
    values = v_all[...].astype(f32).T.astype(bf16)
    queries, keys = [], []
    for head in range(2):
        flag = masks[1] if head == 0 else masks[2]
        queries.append((headed(query, masks, head) + jnp.where(flag, 1.0, 0.0)).astype(bf16))
        keys.append((headed(key, masks, head) + jnp.where(flag, bias, 0.0)).astype(bf16))
    for start, size in blocks_of(count):
        tops = []
        for head in range(2):
            scores = scores_of(keys[head], queries[head], start, size, base)
            largest = jnp.max(scores, axis=0, keepdims=True)
            expanded = jnp.exp(scores - largest)
            totals = jnp.sum(expanded, axis=0, keepdims=True)
            lse_ref[0, 0, head : head + 1, start : start + size] = largest + jnp.log(totals)
            mixed = jnp.dot(values[:, : start + size], expanded.astype(bf16), preferred_element_type=f32)
            tops.append(mixed[head * HEAD_DIM : (head + 1) * HEAD_DIM] / totals)
        o_all[start : start + size] = jnp.concatenate(tops, axis=0).T.astype(bf16)
    for c in range(spans):
        slot, is_near = piece_of(own, c)
        for target, chosen in ((on, is_near), (of, jnp.logical_not(is_near))):

            @pl.when(chosen)
            def _(c=c, slot=slot, target=target):
                target[slot, 0] = o_all[base + c * span_rows : base + (c + 1) * span_rows]


def attend_back_kernel(spans, span_rows, info, qn, qf, kn, kf, vn, vf, on, of, gn, gf, lse_ref, *rest):
    d_near, d_far, q_all, k_all, v_all, o_all, g_all, dq, dk, dv = rest[-10:]
    count = k_all.shape[0]
    base = spans * MEM_ROWS
    own = info[0]
    to_sequence(spans, span_rows, own, qn, qf, q_all)
    to_sequence(spans, span_rows, own, kn, kf, k_all)
    to_sequence(spans, span_rows, own, vn, vf, v_all)
    to_sequence(spans, span_rows, own, on, of, o_all, False)
    to_sequence(spans, span_rows, own, gn, gf, g_all, False)
    masks = head_masks(count)
    bias = key_bias(info[1 + pl.program_id(0)], spans, count - base)
    query, key, grad = q_all[...].astype(f32), k_all[...].astype(f32), g_all[...].astype(f32)
    overlap = (grad * o_all[...].astype(f32)).T
    keys_t = key.T.astype(bf16)
    values = v_all[...]
    plain_q, plain_g, flag_q, flag_k, deltas = [], [], [], [], []
    for head in range(2):
        flag = masks[1] if head == 0 else masks[2]
        own_q = headed(query, masks, head)
        plain_q.append(own_q.astype(bf16))
        plain_g.append(headed(grad, masks, head).astype(bf16))
        flag_q.append((own_q + jnp.where(flag, 1.0, 0.0)).astype(bf16))
        flag_k.append((headed(key, masks, head) + jnp.where(flag, bias, 0.0)).astype(bf16))
        deltas.append(jnp.sum(overlap[head * HEAD_DIM : (head + 1) * HEAD_DIM], axis=0, keepdims=True))
    for start, size in reversed(blocks_of(count)):
        stop = start + size
        tops, weights_low, slopes = [], [], []
        for head in range(2):
            scores = scores_of(flag_k[head], flag_q[head], start, size, base)
            weights = jnp.exp(scores - lse_ref[0, 0, head : head + 1, start:stop])
            weight_grad = against(values[:stop], plain_g[head][start:stop])
            slope = (weights * (weight_grad - deltas[head][:, start:stop])).astype(bf16)
            weights_low.append(weights.astype(bf16))
            slopes.append(slope)
            turned = jnp.dot(keys_t[:, :stop], slope, preferred_element_type=f32)
            tops.append(turned[head * HEAD_DIM : (head + 1) * HEAD_DIM])
        dq[start:stop] = (jnp.concatenate(tops, axis=0).T.astype(bf16).astype(f32) * 0.125).astype(bf16)
        grads = jnp.concatenate([plain_g[0][start:stop], plain_g[1][start:stop]], axis=0)
        queries = jnp.concatenate([plain_q[0][start:stop], plain_q[1][start:stop]], axis=0)
        value_part = jnp.dot(jnp.concatenate(weights_low, axis=1), grads, preferred_element_type=f32)
        key_part = jnp.dot(jnp.concatenate(slopes, axis=1), queries, preferred_element_type=f32)
        if stop == count:
            dv[...] = value_part
            dk[...] = key_part
        else:
            dv[:stop] += value_part
            dk[:stop] += key_part
    for c in range(spans):
        slot, is_near = piece_of(own, c)
        rows = slice(base + c * span_rows, base + (c + 1) * span_rows)
        slots = slice(c * MEM_ROWS, (c + 1) * MEM_ROWS)
        for target, chosen in ((d_near, is_near), (d_far, jnp.logical_not(is_near))):

            @pl.when(chosen)
            def _(slot=slot, rows=rows, slots=slots, target=target):
                for part, source in enumerate((dq, dk, dv)):
                    lanes = slice(part * LANES, (part + 1) * LANES)
                    target[slot, 0, :span_rows, lanes] = source[rows].astype(bf16)
                    low = jnp.zeros((MEM_ROWS, LANES), bf16) if part == 0 else source[slots].astype(bf16)
                    target[slot, 0, span_rows:, lanes] = low


def attend_call(info, near, far, span_rows, heads):
    slots, replicas, rows, _ = near.shape
    spans, pairs = 2 * slots, heads // 2
    count = spans * rows
    piece = lambda part: [pl.BlockSpec((slots, 1, rows, LANES), lambda r, p, info: (0, r, 0, 3 * p + part))] * 2
    mixed = pl.BlockSpec((slots, 1, span_rows, LANES), lambda r, p, info: (0, r, 0, p))
    shape = jax.ShapeDtypeStruct((slots, replicas, span_rows, pairs * LANES), bf16)
    return pl.pallas_call(
        functools.partial(attend_kernel, spans, span_rows),
        out_shape=(shape, shape, jax.ShapeDtypeStruct((replicas, pairs, 2, count), f32)),
        grid_spec=pltpu.PrefetchScalarGridSpec(
            num_scalar_prefetch=1,
            grid=(replicas, pairs),
            in_specs=piece(0) + piece(1) + piece(2),
            out_specs=(mixed, mixed, pl.BlockSpec((1, 1, 2, count), lambda r, p, info: (r, p, 0, 0))),
            scratch_shapes=[pltpu.VMEM((count, LANES), bf16)] * 4,
        ),
        compiler_params=pltpu.CompilerParams(vmem_limit_bytes=56 << 20),
        cost_estimate=pl.CostEstimate(flops=24 * 10**9, bytes_accessed=8 * 10**6, transcendentals=10**7),
        name="attend",
    )(info, near, far, near, far, near, far)


def attend_back_call(info, projected, attended, upstream, log_totals, span_rows, heads):
    slots, replicas, rows, _ = projected[0].shape
    spans, pairs = 2 * slots, heads // 2
    count = spans * rows
    piece = lambda part: [pl.BlockSpec((slots, 1, rows, LANES), lambda r, p, info: (0, r, 0, 3 * p + part))] * 2
    plain = [pl.BlockSpec((slots, 1, span_rows, LANES), lambda r, p, info: (0, r, 0, p))] * 4
    specs = piece(0) + piece(1) + piece(2) + plain
    specs.append(pl.BlockSpec((1, 1, 2, count), lambda r, p, info: (r, p, 0, 0)))
    inputs = [*projected, *projected, *projected, *attended, *upstream, log_totals]
    shape = jax.ShapeDtypeStruct((slots, replicas, rows, 3 * pairs * LANES), bf16)
    return pl.pallas_call(
        functools.partial(attend_back_kernel, spans, span_rows),
        out_shape=(shape, shape),
        grid_spec=pltpu.PrefetchScalarGridSpec(
            num_scalar_prefetch=1,
            grid=(replicas, pairs),
            in_specs=specs,
            out_specs=[pl.BlockSpec((slots, 1, rows, 3 * LANES), lambda r, p, info: (0, r, 0, p))] * 2,
            scratch_shapes=[pltpu.VMEM((count, LANES), bf16)] * 6 + [pltpu.VMEM((count, LANES), f32)] * 2,
        ),
        compiler_params=pltpu.CompilerParams(vmem_limit_bytes=56 << 20),
        cost_estimate=pl.CostEstimate(flops=30 * 10**9, bytes_accessed=16 * 10**6, transcendentals=10**7),
        name="attend_back",
    )(info, *inputs)


def place_up_kernel(owners, table, *refs):
    target = refs[-1]
    width = refs[0].shape[1] // owners
    team = target.shape[1] // (owners * width)
    for k in range(team):
        for z in range(owners):
            lanes = pl.ds(pl.multiple_of((z * team + table[k]) * width, width), width)
            target[:, lanes] = refs[k][:, z * width : (z + 1) * width].astype(f32)


def place_heads_kernel(order, table, *refs):
    target = refs[-1]
    groups = len(order)
    width = refs[0].shape[1] // groups
    team = target.shape[1] // (groups * width)
    half = team // 2
    odd = table[0] % 2 == 1
    for k in range(half):
        mine, other = refs[k][...].astype(f32), refs[k + half][...].astype(f32)
        first = jnp.where(odd, other, mine)
        second = jnp.where(odd, mine, other)
        place = table[k] // 2
        for position, g in enumerate(order):
            cut = slice(position * width, (position + 1) * width)
            lanes = pl.ds(pl.multiple_of((g * half + place) * 2 * width, 2 * width), 2 * width)
            target[:, lanes] = jnp.concatenate([first[:, cut], second[:, cut]], axis=1)


def place_columns(kernel, table, sides, rows, columns):
    result = None
    size = rows // len(sides)
    for number, side in enumerate(sides):
        inputs = list(side)
        if side[0].ndim == 3:
            block = (None, ROW_BLOCK, side[0].shape[2])
            specs = [pl.BlockSpec(block, lambda i, t, k=k: (k, i, 0)) for k in range(len(side))]
        else:
            specs = [pl.BlockSpec((ROW_BLOCK, side[0].shape[1]), lambda i, t: (i, 0))] * len(side)
        shift = number * size // ROW_BLOCK
        result = placed(kernel, table, inputs, specs, result, (rows, columns), (ROW_BLOCK, columns), size // ROW_BLOCK, lambda i, t: (i + shift, 0))
    return result


def placed(kernel, table, inputs, specs, result, shape, block, steps, index):
    aliases = {}
    if result is not None:
        inputs.append(result)
        specs.append(pl.BlockSpec(memory_space=pl.ANY))
        aliases = {len(inputs): 0}
    return pl.pallas_call(
        kernel,
        out_shape=jax.ShapeDtypeStruct(shape, f32),
        grid_spec=pltpu.PrefetchScalarGridSpec(
            num_scalar_prefetch=1,
            grid=(steps,),
            in_specs=specs,
            out_specs=pl.BlockSpec(block, index),
        ),
        input_output_aliases=aliases,
        compiler_params=pltpu.CompilerParams(vmem_limit_bytes=40 << 20),
        cost_estimate=pl.CostEstimate(flops=0, bytes_accessed=6 * steps * block[0] * block[1], transcendentals=0),
        name="place",
    )(table, *inputs)


def place_rows_kernel(team, table, *refs):
    target = refs[-1]
    for k in range(team):

        @pl.when(pl.program_id(0) == k)
        def _(k=k):
            target[...] = refs[k][...].astype(f32)


def place_rows(table, sides, used=None):
    team = len(sides[0])
    result = None
    count = len(sides)
    for number, side in enumerate(sides):
        size, columns = (used or side[0].shape[0]), side[0].shape[1]
        specs = [pl.BlockSpec((size, columns), lambda i, t: (0, 0), pipeline_mode=pl.Buffered(1))] * team
        kernel = functools.partial(place_rows_kernel, team)
        shape = (count * size * team, columns)
        result = placed(kernel, table, list(side), specs, result, shape, (size, columns), team, lambda i, t, number=number: (count * t[i] + number, 0))
    return result


def hold(value, *others):
    return lax.optimization_barrier((value, *others))[0]


def gate(values, *others):
    values = list(values)
    anywhere = pl.BlockSpec(memory_space=pl.ANY)
    return pl.pallas_call(
        lambda *refs: None,
        out_shape=[jax.ShapeDtypeStruct(v.shape, v.dtype) for v in values],
        in_specs=[anywhere] * (len(values) + len(others)),
        out_specs=[anywhere] * len(values),
        input_output_aliases={i: i for i in range(len(values))},
        name="gate",
    )(*values, *others)


def shards(
    hidden_in,
    memory_rows,
    seg_len,
    out_grad,
    first_gain,
    first_shift,
    qkv_weight,
    query_bias,
    value_bias,
    out_weight,
    out_bias,
    second_gain,
    second_shift,
    up_weight,
    up_bias,
    down_weight,
    down_bias,
):
    plane = Plane()
    owners = lax.axis_size("fsdp")
    replicas, spans = plane.replicas, plane.spans
    team = replicas * spans
    count = plane.half
    owner = lax.axis_index("fsdp")
    own_span = lax.axis_index("ctx")
    index = lax.axis_index("replica") * spans + own_span
    mate = jnp.bitwise_xor(index, 1)
    share = D // owners
    span_rows = hidden_in.shape[1]
    piece_rows = span_rows + MEM_ROWS
    heads = HEADS // team
    width = heads * HEAD_DIM
    hidden = up_bias.shape[0] // team
    ff = hidden * owners
    low = lambda array: array.astype(bf16)

    even = heads % owners == 0
    block = width // owners if even else width
    groups = owners if even else 1
    pairs = max(heads // 2, 1)
    inner = groups // pairs if groups > 1 else 1
    order = [part * groups + pair * inner + i for pair in range(pairs) for part in range(3) for i in range(inner)]
    columns_qkv = columns_of(qkv_weight, 3 * groups, index, block, order)
    weight_qkv = lax.all_gather(columns_qkv, "fsdp", axis=0, tiled=True)
    small = jnp.concatenate(
        [first_gain, first_shift, query_bias, value_bias, out_bias, second_gain, second_shift, down_bias, up_bias]
    )
    small = lax.all_gather(hold(small, columns_qkv).reshape(-1, 128), "fsdp", axis=0, tiled=True)
    small = small.reshape(owners, -1).astype(f32)
    vectors = [small[:, i * share : (i + 1) * share].reshape(D) for i in range(8)]
    gain_one, shift_one, bias_query, bias_value, bias_out, gain_two, shift_two, bias_down = vectors
    bias_up = jnp.concatenate(
        [lax.dynamic_slice_in_dim(small[:, 8 * share :], i * hidden, hidden, 1).reshape(ff) for i in (index, mate)]
    )
    if even:
        rows_out = lax.dynamic_slice_in_dim(out_weight, index * block, block, 0)
        weight_out = lax.all_gather(rows_out, "fsdp", axis=0, tiled=True)
    else:
        weight_out = lax.dynamic_slice_in_dim(
            lax.all_gather(out_weight, "fsdp", axis=0, tiled=True), index * width, width, 0
        )
    weight_up = lax.all_gather(columns_of(up_weight, owners, index, hidden), "fsdp", axis=0, tiled=True)
    weight_down = lax.all_gather(
        lax.dynamic_slice_in_dim(down_weight, index * hidden, hidden, 0), "fsdp", axis=0, tiled=True
    )
    with_mate = lambda weight, axis: jnp.concatenate([weight, plane.swap(weight)], axis=axis)

    cotangent = out_grad.reshape(span_rows, D)
    cot_float = cotangent.astype(f32)
    cot_first = plane.send(cotangent)

    tokens = hold(hidden_in, cot_first).reshape(span_rows, D)
    slots = jnp.pad(memory_rows.reshape(SUMM, D), ((0, spans * MEM_ROWS - SUMM), (0, 0)))
    slots = lax.dynamic_slice_in_dim(slots, own_span * MEM_ROWS, MEM_ROWS, 0)
    own_rows = jnp.concatenate([tokens, slots], axis=0).astype(f32)
    normal_one, inverse_one = normal_of(own_rows)
    lengths = [seg_len]
    for axis, bit in plane.slow:
        if axis == "replica":
            lengths = lengths + [plane.swap(v, (axis, bit)) for v in lengths]
    lengths = jnp.concatenate(lengths)

    normed, _ = plane.gather(hold(low(normal_one * gain_one + shift_one), lengths))
    weight_qkv = hold(weight_qkv, normed)
    qkv_mate = plane.swap(weight_qkv)
    bias_qkv = jnp.concatenate([bias_query, jnp.zeros((D,), f32), bias_value])[None]
    scale_qkv = jnp.asarray(np.repeat([0.125 if g < groups else 1.0 for g in order], block), f32)

    def project(rows, weight, device):
        bias = columns_of(bias_qkv, 3 * groups, device, block, order)[0]
        return low((dot(rows, weight) + bias) * scale_qkv).reshape(spans // 2, replicas, piece_rows, 3 * width)

    kernels = span_rows % 16 == 0 and heads % 2 == 0 and spans % 2 == 0 and SUMM <= spans * MEM_ROWS
    info = jnp.concatenate([own_span[None].astype(jnp.int32), lengths])
    split = lambda a: jnp.moveaxis(a, 1, 0).reshape(replicas, -1, heads, HEAD_DIM)
    to_pieces = lambda a: jnp.moveaxis(a.reshape(replicas, spans, -1, pairs, width // pairs), 0, 1)

    def parts_of(near, far):
        apart = jnp.concatenate([near, far], axis=0).reshape(spans, replicas, piece_rows, pairs, 3, width // pairs)
        return split(apart[:, :, :span_rows, :, 0]), split(apart[..., 1, :]), split(apart[..., 2, :])

    def attend_all():
        near, far = projected
        if kernels:
            return attend_call(info, near, far, span_rows, heads)
        allowed = allowed_of(plane, span_rows, own_span, lengths)
        mixed, totals = attend(*parts_of(near, far), allowed)
        mixed = to_pieces(mixed).reshape(spans, replicas, span_rows, width)
        return mixed[: spans // 2], mixed[spans // 2 :], totals

    projected = [project(normed, weight_qkv, index)]
    projected.append(plane.swap(project(normed, hold(qkv_mate, projected[0]), mate)))
    cot_all, filled = plane.gather(cotangent, (None, attend_all), cot_first)
    mixed_near, mixed_far, log_totals = filled[0]
    attended = jnp.concatenate([mixed_near, plane.swap(mixed_far)], axis=-1).reshape(count * span_rows, 2 * width)
    weight_out = with_mate(hold(weight_out, projected[0]), 0)
    branch, _ = plane.scatter(low(dot(attended, weight_out)))
    bias_out = gate([bias_out[None]], cot_all)[0][0] if kernels else bias_out
    weight_up = with_mate(gate([weight_up], branch)[0] if kernels else weight_up, 1)
    middle = tokens.astype(f32) + (branch + bias_out)
    normal_two, inverse_two = normal_of(middle)
    normed_two, _ = plane.gather(low(normal_two * gain_two + shift_two))

    upper = dot(normed_two, weight_up) + bias_up
    phi_up = 0.5 * (1.0 + lax.erf(upper * 0.7071067811865476))
    active = low(upper * phi_up)
    slope = low(phi_up + upper * (0.3989422804014327 * jnp.exp(-0.5 * upper * upper)))
    down_other = plane.swap(low(across(active[:, ff:], cot_all)))
    weight_down = with_mate(gate([weight_down], down_other)[0] if kernels else weight_down, 0)
    kept = []

    def upper_back(token):
        kept.append(low(against(hold(cot_all, token), weight_down) * slope.astype(f32)))
        return kept[0]

    def normed_back(token):
        return low(against(kept[0], weight_up))

    feed = low(dot(active, weight_down))
    if kernels:
        down_other = gate([down_other], feed[:16])[0]
    down_grad = low(across(active[:, :ff], cot_all) + down_other.astype(f32))
    down_mine = lax.psum_scatter(down_grad, "fsdp", scatter_dimension=0, tiled=True)
    feed, (upper_grad, partial) = plane.scatter(feed, (upper_back, normed_back))
    output = low(middle + (feed + bias_down))
    others = []

    def mate_grads(token):
        others.append(plane.swap(low(across(normed_two, hold(upper_grad, token)[:, ff:]))))
        return others[0]

    normed_two_grad, _ = plane.scatter(partial, (mate_grads,))
    gain_back = gate([gain_two[None]], output)[0][0] if kernels else gain_two
    middle_grad = cot_float + norm_input_grad(normed_two_grad, normal_two, inverse_two, gain_back)
    branch_grad = low(middle_grad)
    up_other = gate([others[0]], branch_grad)[0] if kernels else others[0]
    up_grad = low(across(normed_two, upper_grad[:, :ff]) + up_other.astype(f32))
    if kernels:
        up_grad = gate([up_grad], down_mine)[0]
    up_mine = lax.psum_scatter(up_grad, "fsdp", scatter_dimension=0, tiled=True)
    up_bias_grad = jnp.sum(upper_grad.astype(f32), axis=0)
    branch_all, _ = plane.gather(branch_grad)

    shape = (spans // 2, replicas, span_rows, width)
    upstream_far = plane.swap(low(against(branch_all, weight_out[width:])))
    upstream_near = low(against(branch_all, weight_out[:width]))
    upstream = (upstream_near.reshape(shape), upstream_far.reshape(shape))
    fine = kernels and even and hidden % LANES == 0 and block * 2 == LANES and share % (2 * ROW_BLOCK) == 0
    if kernels:
        info = gate([info], up_grad)[0]
        known = (info, projected, (mixed_near, mixed_far), upstream, log_totals, span_rows, heads)
        grads = attend_back_call(*known)
    else:
        allowed = allowed_of(plane, span_rows, own_span, lengths)
        upstream = split(jnp.concatenate(upstream, axis=0))
        query_grad, key_grad, value_grad = attend_back(*parts_of(*projected), upstream, log_totals, allowed)
        query_grad = jnp.pad(to_pieces(query_grad), ((0, 0), (0, 0), (0, MEM_ROWS), (0, 0), (0, 0)))
        grads = jnp.stack([query_grad, to_pieces(key_grad), to_pieces(value_grad)], axis=-2)
        grads = (grads[: spans // 2], grads[spans // 2 :])
    near, far = [g.reshape(count * piece_rows, 3 * width) for g in grads]
    if fine:
        down_found = plane.whole(down_mine)
        near, far = gate([near, far], *[v for name, v in down_found.items() if name != (0, 0)])
    other = plane.swap(far)
    qkv_grad = low(across(normed, near) + across(plane.swap(normed), far))
    if fine:
        qkv_grad = gate([qkv_grad], up_mine)[0]
    qkv_mine = lax.psum_scatter(qkv_grad, "fsdp", scatter_dimension=0, tiled=True)
    both = jnp.concatenate([near, gate([other], qkv_grad)[0] if kernels else other], axis=1)
    partial = low(against(both, jnp.concatenate([weight_qkv, qkv_mate], axis=1)))
    def mate_out(token):
        others.append(low(across(attended[:, width:], hold(branch_all, token))))
        return others[-1]

    def own_out(token):
        return low(across(attended[:, :width], branch_all) + plane.swap(others[-1]).astype(f32))

    if fine:
        own_replica = lax.axis_index("replica")
        names = np.array(plane.near + plane.far, np.int32)
        table = jnp.bitwise_xor(own_replica, names[:, 0]) * spans + jnp.bitwise_xor(own_span, names[:, 1])
        table = table.astype(jnp.int32)
    normed_grad, (_, out_grad_w) = plane.scatter(partial, (mate_out, own_out))
    rows_grad = norm_input_grad(normed_grad, normal_one, inverse_one, gain_one)
    input_grad = middle_grad + rows_grad[:span_rows]
    slots_all = {0: rows_grad[span_rows:]}
    bit = 1
    while bit < spans:
        for value, rows in list(slots_all.items()):
            slots_all[value ^ bit] = plane.swap(rows, ("ctx", bit))
        bit *= 2
    slots_grad = jnp.zeros((spans * MEM_ROWS, D), f32)
    for value, rows in slots_all.items():
        start = jnp.bitwise_xor(own_span, value) * MEM_ROWS
        slots_grad = lax.dynamic_update_slice_in_dim(slots_grad, rows, start, 0)
    slots_grad = slots_grad[:SUMM]

    def spot(values, full, groups, size, device):
        base = jnp.zeros((groups, full // groups), f32)
        return lax.dynamic_update_slice_in_dim(base, values.reshape(groups, size), device * size, 1).reshape(full)

    bias_grads = (jnp.sum(near.astype(f32), axis=0) + jnp.sum(far.astype(f32), axis=0)).reshape(pairs, 3, -1)
    parts = [
        spot(bias_grads[:, 0], D, groups, block, index),
        spot(bias_grads[:, 2], D, groups, block, index),
        jnp.sum(branch_grad.astype(f32), axis=0),
        jnp.sum(normed_two_grad * normal_two, axis=0),
        jnp.sum(normed_two_grad, axis=0),
        jnp.sum(cot_float, axis=0),
        spot(up_bias_grad[:ff], ff * team, owners, hidden, index)
        + spot(up_bias_grad[ff:], ff * team, owners, hidden, mate),
    ]
    sums = jnp.sum(partial.astype(f32), axis=0)
    parts += [(jnp.sum(partial.astype(f32) * normed.astype(f32), axis=0) - shift_one * sums) / gain_one, sums]
    vector = low(jnp.concatenate([part.reshape(owners, -1) for part in parts], axis=1))
    used = vector.shape[1]
    extra = -(-used // (16 * D)) * 16
    vector = jnp.pad(vector, ((0, 0), (0, extra * D - used))).reshape(owners, extra, D)

    def columns_all(full, groups, size):
        full = full.reshape(team, share, groups, size)
        return jnp.moveaxis(full, 0, 2).reshape(share, -1).astype(f32)

    if fine:
        qkv_found = plane.whole(qkv_mine)
        down_all = place_rows(table, plane.complete(down_found, True))
        sides = plane.complete(qkv_found, True, (down_all,))
        devices = jnp.arange(team, dtype=jnp.int32)
        up_full = lax.all_gather(gate([up_mine], qkv_mine)[0], PLANE, axis=0, tiled=False)
        up_all = place_columns(
            functools.partial(place_up_kernel, owners), devices, [[up_full] * team], share, ff * team
        )
        out_rows = gate([out_grad_w], qkv_mine)[0].reshape(owners, block, D)
        joined = jnp.concatenate([out_rows, vector], axis=1).reshape(-1, D)
        out_mine = lax.psum_scatter(joined, "fsdp", scatter_dimension=0, tiled=True)
        qkv_all = place_columns(functools.partial(place_heads_kernel, order), table, sides, share, 3 * D)
        out_mine = gate([out_mine], sides[0][plane.half - 1])[0]
        out_sides = plane.complete(plane.whole(out_mine), False)
        out_all = place_rows(table, out_sides, block)
        vectors = sum(rows[block:].astype(f32) for rows in out_sides[0])
    else:
        down_all = lax.all_gather(down_mine, PLANE, axis=0, tiled=True).astype(f32)
        up_all = columns_all(lax.all_gather(up_mine, PLANE, axis=0, tiled=False), owners, hidden)
        qkv_full = lax.all_gather(qkv_mine, PLANE, axis=0, tiled=False).reshape(team, share, 3 * groups, block)
        qkv_full = jnp.concatenate([qkv_full[:, :, order.index(g)][:, :, None] for g in range(3 * groups)], axis=2)
        qkv_all = columns_all(qkv_full, 3 * groups, block)
        if even:
            out_mine = lax.psum_scatter(out_grad_w, "fsdp", scatter_dimension=0, tiled=True)
            out_all = lax.all_gather(out_mine, PLANE, axis=0, tiled=True).astype(f32)
        else:
            placed = lax.dynamic_update_slice_in_dim(jnp.zeros((D, D), bf16), out_grad_w, index * width, 0)
            out_all = lax.psum(lax.psum_scatter(placed, "fsdp", scatter_dimension=0, tiled=True), PLANE).astype(f32)
        vectors = lax.psum(lax.psum_scatter(vector, "fsdp", scatter_dimension=0, tiled=True), PLANE).astype(f32)
    vectors = vectors.reshape(-1)
    take = lambda i: vectors[i * share : (i + 1) * share]
    up_end = 6 * share + ff * team // owners
    return (
        output.reshape(hidden_in.shape),
        input_grad.reshape(hidden_in.shape),
        slots_grad.reshape(memory_rows.shape),
        vectors[up_end : up_end + share],
        vectors[up_end + share : up_end + 2 * share],
        qkv_all,
        take(0),
        take(1),
        out_all,
        take(2),
        take(3),
        take(4),
        up_all,
        vectors[6 * share : up_end],
        down_all,
        take(5),
    )


def solution(mesh):
    rows = P(("fsdp", "replica"), "ctx", None)
    part = P("fsdp")
    table = P("fsdp", None)
    whole = P(("fsdp", "replica"), None, None)
    return jax.shard_map(
        shards,
        mesh=mesh,
        in_specs=(
            rows,
            whole,
            P(("fsdp", "replica")),
            rows,
            part,
            part,
            table,
            part,
            part,
            table,
            part,
            part,
            part,
            table,
            part,
            table,
            part,
        ),
        out_specs=(
            rows,
            rows,
            whole,
            part,
            part,
            table,
            part,
            part,
            table,
            part,
            part,
            part,
            table,
            part,
            table,
            part,
        ),
        check_vma=False,
    )
```

time: 1250 us -> 778 us (0.62)
  local copies, waits for them, and re-layouts: 310 us -> 65.7 us
  waiting for transfers between devices: 448 us -> 309 us
  other arithmetic: 152 us -> 53.9 us
  Pallas kernels: 0 us -> 75.2 us
  matrix products: 240 us -> 166 us
  starting transfers between devices: 58.2 us -> 71.1 us
    dot_general x6 -> x0, matrix products: 97.6 us -> none  [the longest x1 26.1 us: attend_back(): jnp.einsum('gqhd,gkhd->ghqk', upstream, value, preferred_element_type=f32)]
    reduce_scatter x4, waiting for transfers between devices: 94.7 us -> 0.01 us  [the longest x1 0.01 us: shards(): lax.psum_scatter(down_grad, 'fsdp', scatter_dimension=0, tiled=True)]
    unnamed x226 -> x217, local copies, waits for them, and re-layouts: 119 us -> 36.9 us
    pallas_call x0 -> x21, Pallas kernels: none -> 75.2 us  [the longest x4 26.9 us: placed(): pl.pallas_call(kernel, out_shape=jax.ShapeDtypeStruct(shape, f32), grid_s...]
    all_gather x6 -> x3, waiting for transfers between devices: 71.5 us -> 1.59 us  [the longest x1 1.59 us: shards(): weight_qkv = lax.all_gather(columns_qkv, 'fsdp', axis=0, tiled=True)]
    convert_element_type x7 -> x1, local copies, waits for them, and re-layouts: 67.2 us -> 0.03 us  [shards(): small = small.reshape(owners, -1).astype(f32)]
    ppermute x97 -> x85, waiting for transfers between devices: 229 us -> 290 us  [swap(): lax.ppermute(array, axis, [(i, i ^ bit) for i in range(self.sizes[axis])])]
    convert_element_type x13 -> x10, other arithmetic: 65.5 us -> 9.54 us  [the longest x3 6.18 us: shards(): low = lambda array: array.astype(bf16)]
  transfers between devices with their start and end apart: 110 -> 94, of which waited for: 38 -> 39; matrix products, arithmetic and copies ran while one was open for 41% -> 33% of each run, Pallas kernels for 0% -> 9%
where the time goes in v2:
time: 778 us; the launch traced here: 772 us
  waiting for transfers between devices  309 us (40%)
  matrix products  166 us (21%)
  Pallas kernels  75.2 us (10%)
  starting transfers between devices  71.1 us (9%)
  local copies, waits for them, and re-layouts  65.7 us (8%)
  other arithmetic  53.9 us (7%)
  between operations  16.6 us (2%)
  blocking collectives  14.1 us (2%)
    ppermute x85, waiting for transfers between devices, swap(): lax.ppermute(array, axis, [(i, i ^ bit) for i in range(self.sizes[axis])])  290 us
    ppermute x85, starting transfers between devices, swap(): lax.ppermute(array, axis, [(i, i ^ bit) for i in range(self.sizes[axis])])  69.8 us
    dot_general x8, matrix products, across(): lax.dot_general(left, right, (((0,), (0,)), ((), ())), preferred_element_...  64.8 us
    dot_general x5, matrix products, against(): lax.dot_general(left, right, (((1,), (1,)), ((), ())), preferred_element_...  52.8 us
    dot_general x5, matrix products, dot(): return jnp.dot(left, right, preferred_element_type=f32)  48.4 us
    unnamed x217, local copies, waits for them, and re-layouts  36.9 us
    pallas_call x4, Pallas kernels, placed(): pl.pallas_call(kernel, out_shape=jax.ShapeDtypeStruct(shape, f32), grid_s...  26.9 us
    pallas_call x1, Pallas kernels, attend_back_call(): pl.pallas_call(functools.partial(attend_back_kernel, spans, span_rows), o...  26.3 us
  transfers between devices with their start and end apart: 94, of which 39 were waited for; matrix products, arithmetic and copies ran while one was open for 33% of the time, Pallas kernels for 9%

profile of v2, /device:TPU:0, one launch (start us, length us, event | category | flops | bytes accessed | tf_op | source)
XLA Modules:
  0.0 771.5 jit_solution(16249648504921494834)
XLA Ops:
  24.4 14.1 %all_gather.21 = bf16[192,128]{1,0:T(8,128)(2,1)S(1)} all-gather(bf16[48,128]{1,0:T(8,128)(2,1)S(1)} %bitcast.202), channel_id=1, replica_groups=mesh['fsdp'=4,'replica'=2,'ctx'=4] {'fsdp'}, dimensions={0}, use_global_device_ids=true | all-gather | bytes 61440 | tf_op jit(solution)/shard_map/all_gather | solution.py:580
  47.3 11.1 %collective-permute-done.6 = bf16[144,2048]{1,0:T(8,128)(2,1)S(1)} collective-permute-done((bf16[144,2048]{1,0:T(8,128)(2,1)S(1)}, bf16[144,2048]{1,0:T(8,128)(2,1)S(1)}, u32[]{:S(2)}, u32[]{:S(2)}) %collective-permute-start.6) | collective-permute-done | bytes 589856 | tf_op jit(solution)/shard_map/ppermute | solution.py:71
  62.3 8.8 %collective-permute-done.7 = bf16[144,2048]{1,0:T(8,128)(2,1)S(1)} collective-permute-done((bf16[144,2048]{1,0:T(8,128)(2,1)S(1)}, bf16[144,2048]{1,0:T(8,128)(2,1)S(1)}, u32[]{:S(2)}, u32[]{:S(2)}) %collective-permute-start.7) | collective-permute-done | bytes 589856 | tf_op jit(solution)/shard_map/ppermute | solution.py:71
  74.3 5.9 collective-permute-done.10
  85.3 8.4 %fusion.15 = bf16[1152,768]{1,0:T(8,128)(2,1)} fusion(bf16[1152,2048]{1,0:T(8,128)(2,1)} %constant_dynamic-update-slice_fusion, bf16[2048,768]{1,0:T(8,128)(2,1)} %all-gather.7.cloned.1.call-done, f32[768]{0:T(1024)S(1)} %copy-done.74, f32[768]{0:T(1024)S(1)} %reduce.5), kind=kOutput, calls=%fused_computation.38 | convolution fusion | flops 3626532864 | bytes 9639936 | tf_op jit(solution)/shard_map/dot_general | solution.py:30
  93.6 8.4 %fusion.16 = bf16[1152,768]{1,0:T(8,128)(2,1)} fusion(bf16[1152,2048]{1,0:T(8,128)(2,1)} %constant_dynamic-update-slice_fusion, bf16[2048,768]{1,0:T(8,128)(2,1)} %collective-permute-done.12, f32[768]{0:T(1024)S(1)} %reduce.6, f32[768]{0:T(1024)S(1)} %copy-done.74), kind=kOutput, calls=%fused_computation.39 | convolution fusion | flops 3626532864 | bytes 9639936 | tf_op jit(solution)/shard_map/dot_general | solution.py:30
  115.2 22.0 %attend.1 = (bf16[2,2,272,256]{3,2,1,0:T(8,128)(2,1)}, bf16[2,2,272,256]{3,2,1,0:T(8,128)(2,1)}, f32[2,2,2,1152]{3,2,1,0:T(2,128)}) custom-call(s32[3]{0:T(128)} %pad_add_fusion.info.refs_0_, bf16[2,2,288,768]{3,2,1,0:T(8,128)(2,1)} %bitcast.203, bf16[2,2,288,768]{3,2,1,0:T(8,128)(2,1)} %collective-permute-done.13.qf.kf.vf, ...), custom_call_target="tpu_custom_call" | custom-call | flops 24000000000 | bytes 8000000 | tf_op jit(solution)/shard_map/attend/pallas_call | solution.py:386
  153.0 8.9 %collective-permute-done.20 = bf16[128,2048]{1,0:T(8,128)(2,1)S(1)} collective-permute-done((bf16[128,2048]{1,0:T(8,128)(2,1)S(1)}, bf16[128,2048]{1,0:T(8,128)(2,1)S(1)}, u32[]{:S(2)}, u32[]{:S(2)}) %collective-permute-start.20) | collective-permute-done | bytes 524320 | tf_op jit(solution)/shard_map/ppermute | solution.py:71
  167.4 5.9 collective-permute-done.19
  173.3 14.5 %collective-permute-done.21 = bf16[128,2048]{1,0:T(8,128)(2,1)} collective-permute-done((bf16[128,2048]{1,0:T(8,128)(2,1)}, bf16[128,2048]{1,0:T(8,128)(2,1)}, u32[]{:S(2)}, u32[]{:S(2)}) %collective-permute-start.21) | collective-permute-done | bytes 524320 | tf_op jit(solution)/shard_map/ppermute | solution.py:71
  205.4 9.7 %collective-permute-done.26 = bf16[128,2048]{1,0:T(8,128)(2,1)S(1)} collective-permute-done((bf16[128,2048]{1,0:T(8,128)(2,1)S(1)}, bf16[128,2048]{1,0:T(8,128)(2,1)S(1)}, u32[]{:S(2)}, u32[]{:S(2)}) %collective-permute-start.26) | collective-permute-done | bytes 524320 | tf_op jit(solution)/shard_map/ppermute | solution.py:71
  218.1 8.1 %collective-permute-done.24 = bf16[128,2048]{1,0:T(8,128)(2,1)} collective-permute-done((bf16[128,2048]{1,0:T(8,128)(2,1)S(1)}, bf16[128,2048]{1,0:T(8,128)(2,1)}, u32[]{:S(2)}, u32[]{:S(2)}) %collective-permute-start.24) | collective-permute-done | bytes 524320 | tf_op jit(solution)/shard_map/ppermute | solution.py:71
  229.9 9.6 %collective-permute-done.27 = bf16[144,2048]{1,0:T(8,128)(2,1)S(1)} collective-permute-done((bf16[144,2048]{1,0:T(8,128)(2,1)S(1)}, bf16[144,2048]{1,0:T(8,128)(2,1)S(1)}, u32[]{:S(2)}, u32[]{:S(2)}) %collective-permute-start.27) | collective-permute-done | bytes 589856 | tf_op jit(solution)/shard_map/ppermute | solution.py:71
  241.1 15.2 %multiply_convert_fusion = (bf16[1088,2048]{1,0:T(8,128)(2,1)S(1)}, f32[1088,2048]{1,0:T(8,128)}) fusion(f32[2048]{0:T(1024)S(1)} %pad_maximum_fusion.13, bf16[1088,2048]{1,0:T(8,128)(2,1)} %constant_dynamic-update-slice_fusion.15, bf16[2048,1024]{1,0:T(8,128)(2,1)} %collective-permute-done.29, bf16[2048,1024]{1,0:T(8,128)(2,1)S(1)} %copy-done.38), kind=kOutput, calls=%fused_computation.11 | convolution fusion | flops 9156952064 | bytes 26222592 | tf_op jit(solution)/shard_map/dot_general | solution.py:30
  256.4 11.2 %convolution_convert_fusion.5 = bf16[1024,2048]{1,0:T(8,128)(2,1)} fusion(bf16[1088,2048]{1,0:T(8,128)(2,1)} %constant_dynamic-update-slice_fusion.7.refs_1_, bf16[1088,2048]{1,0:T(8,128)(2,1)S(1)} %get-tuple-element.178), kind=kOutput, calls=%fused_computation.32 | convolution fusion | flops 4565499904 | bytes 10878976 | tf_op jit(solution)/shard_map/dot_general | solution.py:34
  267.5 15.7 %all-gather.13.cloned.1.call-done.refs_0_ = bf16[1024,2048]{1,0:T(8,128)(2,1)} async-done(((bf16[256,2048]{1,0:T(8,128)(2,1)}), bf16[1024,2048]{1,0:T(8,128)(2,1)}) %all-gather.13.cloned.1.call-update) | async-done | bytes 4194320 | tf_op jit(solution)/shard_map/all_gather | solution.py:595
  283.2 7.4 collective-permute-done.31
  290.6 13.9 %convolution_convert_fusion.1 = bf16[1088,2048]{1,0:T(8,128)(2,1)S(1)} fusion(bf16[1088,2048]{1,0:T(8,128)(2,1)} %copy-done.75, bf16[1024,2048]{1,0:T(8,128)(2,1)S(1)} %collective-permute-done.31, bf16[1024,2048]{1,0:T(8,128)(2,1)} %gate.17), kind=kOutput, calls=%fused_computation.20 | convolution fusion | flops 9145810944 | bytes 17301504 | tf_op jit(solution)/shard_map/dot_general | solution.py:30
  310.6 10.2 %add_convert_fusion = bf16[1024,2048]{1,0:T(8,128)(2,1)} fusion(bf16[1024,2048]{1,0:T(8,128)(2,1)} %gate.20, bf16[1088,2048]{1,0:T(8,128)(2,1)} %constant_dynamic-update-slice_fusion.7.refs_1_, bf16[1088,2048]{1,0:T(8,128)(2,1)} %copy-done.75), kind=kOutput, calls=%fused_computation.16 | convolution fusion | flops 4569694208 | bytes 15073280 | tf_op jit(solution)/shard_map/dot_general | solution.py:34
  320.9 19.9 %fusion.6 = bf16[1088,2048]{1,0:T(8,128)(2,1)} fusion(bf16[1088,2048]{1,0:T(8,128)(2,1)} %constant_dynamic-update-slice_fusion.7.refs_1_, bf16[1024,2048]{1,0:T(8,128)(2,1)} %copy-done.69, bf16[1024,2048]{1,0:T(8,128)(2,1)} %gate.17, f32[1088,2048]{1,0:T(8,128)} %get-tuple-element.179), kind=kOutput, calls=%fused_computation.18 | convolution fusion | flops 9170321408 | bytes 26214400 | tf_op jit(solution)/shard_map/dot_general | solution.py:38
  341.6 14.3 %convolution_convert_fusion = bf16[1088,2048]{1,0:T(8,128)(2,1)S(1)} fusion(bf16[1088,2048]{1,0:T(8,128)(2,1)} %fusion.6, bf16[2048,1024]{1,0:T(8,128)(2,1)} %collective-permute-done.29, bf16[2048,1024]{1,0:T(8,128)(2,1)} %gate.16), kind=kOutput, calls=%fused_computation.19 | convolution fusion | flops 9145810944 | bytes 17301504 | tf_op jit(solution)/shard_map/dot_general | solution.py:38
  357.0 10.3 %convolution_convert_fusion.4 = bf16[2048,1024]{1,0:T(8,128)(2,1)} fusion(bf16[1088,2048]{1,0:T(8,128)(2,1)} %constant_dynamic-update-slice_fusion.15, bf16[1088,2048]{1,0:T(8,128)(2,1)S(1)} %bitcast.175), kind=kOutput, calls=%fused_computation.31 | convolution fusion | flops 4565499904 | bytes 10878976 | tf_op jit(solution)/shard_map/dot_general | solution.py:34
  372.6 11.5 %collective-permute-done.32 = bf16[144,2048]{1,0:T(8,128)(2,1)S(1)} collective-permute-done((bf16[144,2048]{1,0:T(8,128)(2,1)S(1)}, bf16[144,2048]{1,0:T(8,128)(2,1)S(1)}, u32[]{:S(2)}, u32[]{:S(2)}) %collective-permute-start.32) | collective-permute-done | bytes 589856 | tf_op jit(solution)/shard_map/ppermute | solution.py:71
  386.7 10.1 %collective-permute-done.39 = bf16[144,2048]{1,0:T(8,128)(2,1)S(1)} collective-permute-done((bf16[144,2048]{1,0:T(8,128)(2,1)S(1)}, bf16[144,2048]{1,0:T(8,128)(2,1)S(1)}, u32[]{:S(2)}, u32[]{:S(2)}) %collective-permute-start.39) | collective-permute-done | bytes 589856 | tf_op jit(solution)/shard_map/ppermute | solution.py:71
  397.1 11.2 %collective-permute-done.43 = bf16[128,2048]{1,0:T(8,128)(2,1)S(1)} collective-permute-done((bf16[128,2048]{1,0:T(8,128)(2,1)S(1)}, bf16[128,2048]{1,0:T(8,128)(2,1)S(1)}, u32[]{:S(2)}, u32[]{:S(2)}) %collective-permute-start.43) | collective-permute-done | bytes 524320 | tf_op jit(solution)/shard_map/ppermute | solution.py:71
  411.3 8.9 %collective-permute-done.40 = bf16[144,2048]{1,0:T(8,128)(2,1)S(1)} collective-permute-done((bf16[144,2048]{1,0:T(8,128)(2,1)S(1)}, bf16[144,2048]{1,0:T(8,128)(2,1)S(1)}, u32[]{:S(2)}, u32[]{:S(2)}) %collective-permute-start.40) | collective-permute-done | bytes 589856 | tf_op jit(solution)/shard_map/ppermute | solution.py:71
  429.4 10.2 %add_convert_fusion.1.refs_0_ = bf16[2048,1024]{1,0:T(8,128)(2,1)} fusion(bf16[2048,1024]{1,0:T(8,128)(2,1)} %gate.19, bf16[1088,2048]{1,0:T(8,128)(2,1)} %constant_dynamic-update-slice_fusion.15, bf16[1088,2048]{1,0:T(8,128)(2,1)} %fusion.6), kind=kOutput, calls=%fused_computation.17 | convolution fusion | flops 4569694208 | bytes 15073280 | tf_op jit(solution)/shard_map/dot_general | solution.py:34
  449.7 11.2 %collective-permute-done.48 = bf16[128,2048]{1,0:T(8,128)(2,1)S(1)} collective-permute-done((bf16[128,2048]{1,0:T(8,128)(2,1)}, bf16[128,2048]{1,0:T(8,128)(2,1)S(1)}, u32[]{:S(2)}, u32[]{:S(2)}) %collective-permute-start.48) | collective-permute-done | bytes 524320 | tf_op jit(solution)/shard_map/ppermute | solution.py:71
  463.1 5.4 collective-permute-done.46
  473.7 11.1 %collective-permute-done.49 = bf16[144,2048]{1,0:T(8,128)(2,1)S(1)} collective-permute-done((bf16[144,2048]{1,0:T(8,128)(2,1)S(1)}, bf16[144,2048]{1,0:T(8,128)(2,1)S(1)}, u32[]{:S(2)}, u32[]{:S(2)}) %collective-permute-start.49) | collective-permute-done | bytes 589856 | tf_op jit(solution)/shard_map/ppermute | solution.py:71
  487.2 4.5 convolution_convert_fusion.8
  494.5 26.3 %attend_back.1 = (bf16[2,2,288,768]{3,2,1,0:T(8,128)(2,1)}, bf16[2,2,288,768]{3,2,1,0:T(8,128)(2,1)}) custom-call(s32[3]{0:T(128)} %gate.22.info, bf16[2,2,288,768]{3,2,1,0:T(8,128)(2,1)} %bitcast.206, bf16[2,2,288,768]{3,2,1,0:T(8,128)(2,1)} %collective-permute-done.13.qf.kf.vf, bf16[2,2,288,768]{3,2,1,0:T(8,128)(2,1)} %bitcast.207, ...), custom_call_target="tpu_custom_call" | custom-call | flops 30000001024 | bytes 16000000 | tf_op jit(solution)/shard_map/attend_back/pallas_call | solution.py:412
  521.9 7.0 fusion.70
  528.9 8.3 %add_convert_fusion.2.refs_0_ = bf16[2048,768]{1,0:T(8,128)(2,1)} fusion(f32[2048,768]{1,0:T(8,128)S(1)} %fusion.70, bf16[1152,2048]{1,0:T(8,128)(2,1)} %constant_dynamic-update-slice_fusion, bf16[1152,768]{1,0:T(8,128)(2,1)S(1)} %copy-done.31), kind=kOutput, calls=%fused_computation.26 | convolution fusion | flops 3627024384 | bytes 15925248 | tf_op jit(solution)/shard_map/dot_general | solution.py:34
  541.7 11.9 %convert_reduce_fusion = (f32[2048]{0:T(1024)S(1)}, f32[2048]{0:T(1024)S(1)}, bf16[1152,2048]{1,0:T(8,128)(2,1)S(1)}) fusion(bf16[1152,2048]{1,0:T(8,128)(2,1)} %constant_dynamic-update-slice_fusion, bf16[2048,768]{1,0:T(8,128)(2,1)} %collective-permute-done.12, bf16[2048,768]{1,0:T(8,128)(2,1)} %all-gather.7.cloned.1.call-done, ...), kind=kOutput, calls=%fused_computation.1 | convolution fusion | flops 7281569792 | bytes 19283968 | tf_op jit(solution)/shard_map/dot_general | solution.py:38
  561.3 9.7 %collective-permute-done.57 = bf16[144,2048]{1,0:T(8,128)(2,1)S(1)} collective-permute-done((bf16[144,2048]{1,0:T(8,128)(2,1)S(1)}, bf16[144,2048]{1,0:T(8,128)(2,1)S(1)}, u32[]{:S(2)}, u32[]{:S(2)}) %collective-permute-start.57) | collective-permute-done | bytes 589856 | tf_op jit(solution)/shard_map/ppermute | solution.py:71
  574.5 8.9 %collective-permute-done.56 = bf16[144,2048]{1,0:T(8,128)(2,1)} collective-permute-done((bf16[144,2048]{1,0:T(8,128)(2,1)}, bf16[144,2048]{1,0:T(8,128)(2,1)}, u32[]{:S(2)}, u32[]{:S(2)}) %collective-permute-start.56) | collective-permute-done | bytes 589856 | tf_op jit(solution)/shard_map/ppermute | solution.py:71
  591.3 5.1 fusion.22.refs_0_
  596.4 8.2 %collective-permute-done.61 = bf16[144,2048]{1,0:T(8,128)(2,1)} collective-permute-done((bf16[144,2048]{1,0:T(8,128)(2,1)S(1)}, bf16[144,2048]{1,0:T(8,128)(2,1)}, u32[]{:S(2)}, u32[]{:S(2)}) %collective-permute-start.61) | collective-permute-done | bytes 589856 | tf_op jit(solution)/shard_map/ppermute | solution.py:71
  610.1 20.8 %collective-permute-done.68.refs_3_ = bf16[256,2048]{1,0:T(8,128)(2,1)S(1)} collective-permute-done((bf16[256,2048]{1,0:T(8,128)(2,1)S(1)}, bf16[256,2048]{1,0:T(8,128)(2,1)S(1)}, u32[]{:S(2)}, u32[]{:S(2)}) %collective-permute-start.68) | collective-permute-done | bytes 1048608 | tf_op jit(solution)/shard_map/ppermute | solution.py:71
  633.6 8.6 %place.4.refs_2_ = f32[2048,2048]{1,0:T(8,128)} custom-call(s32[8]{0:T(128)S(1)} %xor_add_fusion.table, bf16[256,2048]{1,0:T(8,128)(2,1)S(1)} %copy-done.4, bf16[256,2048]{1,0:T(8,128)(2,1)S(1)} %copy-done.6, bf16[256,2048]{1,0:T(8,128)(2,1)} %collective-permute-done.53.refs_3_.refs_2_, bf16[256,2048]{1,0:T(8,128)(2,1)S(1)} %collective-permute-done.68.refs_3_, ...), custom_call_target="tpu_custom_call" | custom-call | bytes 25165824 | tf_op jit(solution)/shard_map/place/pallas_call | solution.py:477
  642.2 4.7 collective-permute-done.59
  651.4 23.8 %collective-permute-done.66.refs_0_ = bf16[512,768]{1,0:T(8,128)(2,1)S(1)} collective-permute-done((bf16[512,768]{1,0:T(8,128)(2,1)S(1)}, bf16[512,768]{1,0:T(8,128)(2,1)S(1)}, u32[]{:S(2)}, u32[]{:S(2)}) %collective-permute-start.66) | collective-permute-done | bytes 786464 | tf_op jit(solution)/shard_map/ppermute | solution.py:71
  684.8 29.6 %collective-permute-done.73.refs_1_.refs_3_ = bf16[512,768]{1,0:T(8,128)(2,1)S(1)} collective-permute-done((bf16[512,768]{1,0:T(8,128)(2,1)}, bf16[512,768]{1,0:T(8,128)(2,1)S(1)}, u32[]{:S(2)}, u32[]{:S(2)}) %collective-permute-start.73) | collective-permute-done | bytes 786464 | tf_op jit(solution)/shard_map/ppermute | solution.py:71
  724.9 4.9 collective-permute-done.75.refs_2_
  735.3 5.1 collective-permute-done.76.refs_3_
  741.5 7.1 place.5
  757.5 7.1 place.7
  (528 shorter events, 220.4 us)
Async XLA Ops:
  7.2 76.3 %all-gather.7.cloned.1.call-start = ((), (), s32[]{:S(2)}) async-start(), calls=%async_computation.4 | async-start | bytes 3932160 | tf_op jit(solution)/shard_map/all_gather | solution.py:576
  9.3 30.8 %collective-permute-start = (bf16[144,2048]{1,0:T(8,128)(2,1)}, bf16[144,2048]{1,0:T(8,128)(2,1)}, u32[]{:S(2)}, u32[]{:S(2)}) collective-permute-start(bf16[144,2048]{1,0:T(8,128)(2,1)} %slice_bitcast_fusion), channel_id=1, source_target_pairs={{0,4},{4,0},{1,5},{5,1},{2,6},{6,2},{3,7},{7,3},{8,12},{12,8},{9,1... | collective-permute-start | bytes 1769480 | tf_op jit(solution)/shard_map/ppermute | solution.py:71
  12.3 27.9 %collective-permute-start.1 = (bf16[144,2048]{1,0:T(8,128)(2,1)}, bf16[144,2048]{1,0:T(8,128)(2,1)}, u32[]{:S(2)}, u32[]{:S(2)}) collective-permute-start(bf16[144,2048]{1,0:T(8,128)(2,1)} %slice_bitcast_fusion), channel_id=1, source_target_pairs={{0,2},{1,3},{2,0},{3,1},{4,6},{5,7},{6,4},{7,5},{8,10},{9,11},{10,... | collective-permute-start | bytes 1769480 | tf_op jit(solution)/shard_map/ppermute | solution.py:71
  20.1 95.0 %all-gather.9.cloned.1.call-start = ((), (), s32[]{:S(2)}) async-start(), calls=%async_computation.5 | async-start | bytes 1310720 | tf_op jit(solution)/shard_map/all_gather | solution.py:589
  45.2 25.9 %collective-permute-start.7 = (bf16[144,2048]{1,0:T(8,128)(2,1)S(1)}, bf16[144,2048]{1,0:T(8,128)(2,1)S(1)}, u32[]{:S(2)}, u32[]{:S(2)}) collective-permute-start(bf16[144,2048]{1,0:T(8,128)(2,1)S(1)} %get-tuple-element.131), channel_id=1, source_target_pairs={{0,4},{4,0},{1,5},{5,1},{2,6},{6,2},{3,7},{7,3},{8,12},{12,8},{9,1... | collective-permute-start | bytes 1769480 | tf_op jit(solution)/shard_map/ppermute | solution.py:71
  45.7 26.8 %collective-permute-start.8 = (bf16[144,2048]{1,0:T(8,128)(2,1)S(1)}, bf16[144,2048]{1,0:T(8,128)(2,1)S(1)}, u32[]{:S(2)}, u32[]{:S(2)}) collective-permute-start(bf16[144,2048]{1,0:T(8,128)(2,1)S(1)} %get-tuple-element.132), channel_id=1, source_target_pairs={{0,2},{1,3},{2,0},{3,1},{4,6},{5,7},{6,4},{7,5},{8,10},{9,11},{10,... | collective-permute-start | bytes 1769480 | tf_op jit(solution)/shard_map/ppermute | solution.py:71
  84.3 110.5 %all-gather.11.cloned.1.call-start = ((), (), s32[]{:S(2)}) async-start(), calls=%async_computation.6 | async-start | bytes 5242880 | tf_op jit(solution)/shard_map/all_gather | solution.py:594
  106.4 176.8 %all-gather.13.cloned.1.call-start = ((), (), s32[]{:S(2)}) async-start(), calls=%async_computation.7 | async-start | bytes 5242880 | tf_op jit(solution)/shard_map/all_gather | solution.py:595
  111.2 26.0 %collective-permute-start.4 = (bf16[128,2048]{1,0:T(8,128)(2,1)}, bf16[128,2048]{1,0:T(8,128)(2,1)S(1)}, u32[]{:S(2)}, u32[]{:S(2)}) collective-permute-start(bf16[128,2048]{1,0:T(8,128)(2,1)} %collective-permute-done.2), channel_id=1, source_target_pairs={{0,4},{4,0},{1,5},{5,1},{2,6},{6,2},{3,7},{7,3},{8,12},{12,8},{9,1... | collective-permute-start | bytes 1572872 | tf_op jit(solution)/shard_map/ppermute | solution.py:71
  111.7 38.4 %collective-permute-start.22 = (bf16[144,2048]{1,0:T(8,128)(2,1)}, bf16[144,2048]{1,0:T(8,128)(2,1)S(1)}, u32[]{:S(2)}, u32[]{:S(2)}) collective-permute-start(bf16[144,2048]{1,0:T(8,128)(2,1)} %collective-permute-done), channel_id=1, source_target_pairs={{0,2},{1,3},{2,0},{3,1},{4,6},{5,7},{6,4},{7,5},{8,10},{9,11},{10,... | collective-permute-start | bytes 1769480 | tf_op jit(solution)/shard_map/ppermute | solution.py:71
  115.2 28.5 %collective-permute-start.15 = (bf16[256,2048]{1,0:T(8,128)(2,1)}, bf16[256,2048]{1,0:T(8,128)(2,1)S(1)}, u32[]{:S(2)}, u32[]{:S(2)}) collective-permute-start(bf16[256,2048]{1,0:T(8,128)(2,1)} %all-gather.9.cloned.1.call-done), channel_id=1, source_target_pairs={{0,1},{1,0},{2,3},{3,2},{4,5},{5,4},{6,7},{7,6},{8,9},{9,8},{10,11... | collective-permute-start | bytes 3145736 | tf_op jit(solution)/shard_map/ppermute | solution.py:71
  152.5 36.9 %collective-permute-start.16 = (bf16[144,2048]{1,0:T(8,128)(2,1)}, bf16[144,2048]{1,0:T(8,128)(2,1)S(1)}, u32[]{:S(2)}, u32[]{:S(2)}) collective-permute-start(bf16[144,2048]{1,0:T(8,128)(2,1)} %get-tuple-element.124), channel_id=1, source_target_pairs={{0,4},{4,0},{1,5},{5,1},{2,6},{6,2},{3,7},{7,3},{8,12},{12,8},{9,1... | collective-permute-start | bytes 1769480 | tf_op jit(solution)/shard_map/ppermute | solution.py:71
  162.8 24.9 %collective-permute-start.21 = (bf16[128,2048]{1,0:T(8,128)(2,1)}, bf16[128,2048]{1,0:T(8,128)(2,1)}, u32[]{:S(2)}, u32[]{:S(2)}) collective-permute-start(bf16[128,2048]{1,0:T(8,128)(2,1)} %add_convert_fusion.11), channel_id=1, source_target_pairs={{0,4},{4,0},{1,5},{5,1},{2,6},{6,2},{3,7},{7,3},{8,12},{12,8},{9,1... | collective-permute-start | bytes 1572872 | tf_op jit(solution)/shard_map/ppermute | solution.py:71
  165.0 24.4 %collective-permute-start.18 = (bf16[144,2048]{1,0:T(8,128)(2,1)S(1)}, bf16[144,2048]{1,0:T(8,128)(2,1)}, u32[]{:S(2)}, u32[]{:S(2)}) collective-permute-start(bf16[144,2048]{1,0:T(8,128)(2,1)S(1)} %add_convert_fusion.8), channel_id=1, source_target_pairs={{0,2},{1,3},{2,0},{3,1},{4,6},{5,7},{6,4},{7,5},{8,10},{9,11},{10,... | collective-permute-start | bytes 1769480 | tf_op jit(solution)/shard_map/ppermute | solution.py:71
  194.8 46.3 %collective-permute-start.29 = (bf16[2048,1024]{1,0:T(8,128)(2,1)}, bf16[2048,1024]{1,0:T(8,128)(2,1)}, u32[]{:S(2)}, u32[]{:S(2)}) collective-permute-start(bf16[2048,1024]{1,0:T(8,128)(2,1)} %gate.16), channel_id=1, source_target_pairs={{0,1},{1,0},{2,3},{3,2},{4,5},{5,4},{6,7},{7,6},{8,9},{9,8},{10,11... | collective-permute-start | bytes 12582920 | tf_op jit(solution)/shard_map/ppermute | solution.py:71
  201.8 24.4 %collective-permute-start.24 = (bf16[128,2048]{1,0:T(8,128)(2,1)S(1)}, bf16[128,2048]{1,0:T(8,128)(2,1)}, u32[]{:S(2)}, u32[]{:S(2)}) collective-permute-start(bf16[128,2048]{1,0:T(8,128)(2,1)S(1)} %slice.380), channel_id=1, source_target_pairs={{0,4},{4,0},{1,5},{5,1},{2,6},{6,2},{3,7},{7,3},{8,12},{12,8},{9,1... | collective-permute-start | bytes 1572872 | tf_op jit(solution)/shard_map/ppermute | solution.py:71
  204.7 234.9 %reduce-scatter.5.cloned.1.call-start = ((), (), s32[]{:S(2)}) async-start(), calls=%async_computation.8 | async-start | bytes 5242880 | tf_op jit(solution)/shard_map/reduce_scatter | solution.py:675
  204.8 23.3 %collective-permute-start.25 = (bf16[144,2048]{1,0:T(8,128)(2,1)S(1)}, bf16[144,2048]{1,0:T(8,128)(2,1)S(1)}, u32[]{:S(2)}, u32[]{:S(2)}) collective-permute-start(bf16[144,2048]{1,0:T(8,128)(2,1)S(1)} %slice.379), channel_id=1, source_target_pairs={{0,2},{1,3},{2,0},{3,1},{4,6},{5,7},{6,4},{7,5},{8,10},{9,11},{10,... | collective-permute-start | bytes 1769480 | tf_op jit(solution)/shard_map/ppermute | solution.py:71
  215.1 25.2 %collective-permute-start.28 = (bf16[128,2048]{1,0:T(8,128)(2,1)S(1)}, bf16[128,2048]{1,0:T(8,128)(2,1)S(1)}, u32[]{:S(2)}, u32[]{:S(2)}) collective-permute-start(bf16[128,2048]{1,0:T(8,128)(2,1)S(1)} %collective-permute-done.26), channel_id=1, source_target_pairs={{0,4},{4,0},{1,5},{5,1},{2,6},{6,2},{3,7},{7,3},{8,12},{12,8},{9,1... | collective-permute-start | bytes 1572872 | tf_op jit(solution)/shard_map/ppermute | solution.py:71
  215.6 23.8 %collective-permute-start.27 = (bf16[144,2048]{1,0:T(8,128)(2,1)S(1)}, bf16[144,2048]{1,0:T(8,128)(2,1)S(1)}, u32[]{:S(2)}, u32[]{:S(2)}) collective-permute-start(bf16[144,2048]{1,0:T(8,128)(2,1)S(1)} %collective-permute-done.23), channel_id=1, source_target_pairs={{0,2},{1,3},{2,0},{3,1},{4,6},{5,7},{6,4},{7,5},{8,10},{9,11},{10,... | collective-permute-start | bytes 1769480 | tf_op jit(solution)/shard_map/ppermute | solution.py:71
  305.7 50.3 %collective-permute-start.35 = (bf16[128,2048]{1,0:T(8,128)(2,1)}, bf16[128,2048]{1,0:T(8,128)(2,1)S(1)}, u32[]{:S(2)}, u32[]{:S(2)}) collective-permute-start(bf16[128,2048]{1,0:T(8,128)(2,1)} %get-tuple-element.122), channel_id=1, source_target_pairs={{0,2},{1,3},{2,0},{3,1},{4,6},{5,7},{6,4},{7,5},{8,10},{9,11},{10,... | collective-permute-start | bytes 1572872 | tf_op jit(solution)/shard_map/ppermute | solution.py:71
  307.9 32.9 %collective-permute-start.36 = (bf16[128,2048]{1,0:T(8,128)(2,1)}, bf16[128,2048]{1,0:T(8,128)(2,1)S(1)}, u32[]{:S(2)}, u32[]{:S(2)}) collective-permute-start(bf16[128,2048]{1,0:T(8,128)(2,1)} %get-tuple-element.123), channel_id=1, source_target_pairs={{0,2},{1,3},{2,0},{3,1},{4,6},{5,7},{6,4},{7,5},{8,10},{9,11},{10,... | collective-permute-start | bytes 1572872 | tf_op jit(solution)/shard_map/ppermute | solution.py:71
  309.2 60.3 %collective-permute-start.33 = (bf16[144,2048]{1,0:T(8,128)(2,1)S(1)}, bf16[144,2048]{1,0:T(8,128)(2,1)S(1)}, u32[]{:S(2)}, u32[]{:S(2)}) collective-permute-start(bf16[144,2048]{1,0:T(8,128)(2,1)S(1)} %get-tuple-element.121), channel_id=1, source_target_pairs={{0,4},{4,0},{1,5},{5,1},{2,6},{6,2},{3,7},{7,3},{8,12},{12,8},{9,1... | collective-permute-start | bytes 1769480 | tf_op jit(solution)/shard_map/ppermute | solution.py:71
  320.9 216.3 %reduce-scatter.7.cloned.1.call-start = ((), (), s32[]{:S(2)}) async-start(), calls=%async_computation.9 | async-start | bytes 5242880 | tf_op jit(solution)/shard_map/reduce_scatter | solution.py:692
  367.3 54.5 %collective-permute-start.42 = (bf16[2048,1024]{1,0:T(8,128)(2,1)}, bf16[2048,1024]{1,0:T(8,128)(2,1)}, u32[]{:S(2)}, u32[]{:S(2)}) collective-permute-start(bf16[2048,1024]{1,0:T(8,128)(2,1)} %convolution_convert_fusion.4), channel_id=1, source_target_pairs={{0,1},{1,0},{2,3},{3,2},{4,5},{5,4},{6,7},{7,6},{8,9},{9,8},{10,11... | collective-permute-start | bytes 12582920 | tf_op jit(solution)/shard_map/ppermute | solution.py:71
  369.7 52.1 %collective-permute-start.41 = (bf16[128,2048]{1,0:T(8,128)(2,1)}, bf16[128,2048]{1,0:T(8,128)(2,1)}, u32[]{:S(2)}, u32[]{:S(2)}) collective-permute-start(bf16[128,2048]{1,0:T(8,128)(2,1)} %get-tuple-element.118), channel_id=1, source_target_pairs={{0,2},{1,3},{2,0},{3,1},{4,6},{5,7},{6,4},{7,5},{8,10},{9,11},{10,... | collective-permute-start | bytes 1572872 | tf_op jit(solution)/shard_map/ppermute | solution.py:71
  371.8 24.9 %collective-permute-start.39 = (bf16[144,2048]{1,0:T(8,128)(2,1)S(1)}, bf16[144,2048]{1,0:T(8,128)(2,1)S(1)}, u32[]{:S(2)}, u32[]{:S(2)}) collective-permute-start(bf16[144,2048]{1,0:T(8,128)(2,1)S(1)} %get-tuple-element.117), channel_id=1, source_target_pairs={{0,4},{4,0},{1,5},{5,1},{2,6},{6,2},{3,7},{7,3},{8,12},{12,8},{9,1... | collective-permute-start | bytes 1769480 | tf_op jit(solution)/shard_map/ppermute | solution.py:71
  384.1 24.2 %collective-permute-start.43 = (bf16[128,2048]{1,0:T(8,128)(2,1)S(1)}, bf16[128,2048]{1,0:T(8,128)(2,1)S(1)}, u32[]{:S(2)}, u32[]{:S(2)}) collective-permute-start(bf16[128,2048]{1,0:T(8,128)(2,1)S(1)} %get-tuple-element.119), channel_id=1, source_target_pairs={{0,2},{1,3},{2,0},{3,1},{4,6},{5,7},{6,4},{7,5},{8,10},{9,11},{10,... | collective-permute-start | bytes 1572872 | tf_op jit(solution)/shard_map/ppermute | solution.py:71
  385.9 25.4 %collective-permute-start.38 = (bf16[144,2048]{1,0:T(8,128)(2,1)S(1)}, bf16[144,2048]{1,0:T(8,128)(2,1)}, u32[]{:S(2)}, u32[]{:S(2)}) collective-permute-start(bf16[144,2048]{1,0:T(8,128)(2,1)S(1)} %get-tuple-element.116), channel_id=1, source_target_pairs={{0,4},{4,0},{1,5},{5,1},{2,6},{6,2},{3,7},{7,3},{8,12},{12,8},{9,1... | collective-permute-start | bytes 1769480 | tf_op jit(solution)/shard_map/ppermute | solution.py:71
  396.9 23.4 %collective-permute-start.40 = (bf16[144,2048]{1,0:T(8,128)(2,1)S(1)}, bf16[144,2048]{1,0:T(8,128)(2,1)S(1)}, u32[]{:S(2)}, u32[]{:S(2)}) collective-permute-start(bf16[144,2048]{1,0:T(8,128)(2,1)S(1)} %add_convert_fusion.6), channel_id=1, source_target_pairs={{0,2},{1,3},{2,0},{3,1},{4,6},{5,7},{6,4},{7,5},{8,10},{9,11},{10,... | collective-permute-start | bytes 1769480 | tf_op jit(solution)/shard_map/ppermute | solution.py:71
  439.6 165.0 %reduce-scatter.9.cloned.1.call-start = ((), (), s32[]{:S(2)}) async-start(), calls=%async_computation.10 | async-start | bytes 3932160 | tf_op jit(solution)/shard_map/reduce_scatter | solution.py:720
  440.1 81.8 %collective-permute-start.55 = (bf16[1152,2048]{1,0:T(8,128)(2,1)}, bf16[1152,2048]{1,0:T(8,128)(2,1)}, u32[]{:S(2)}, u32[]{:S(2)}) collective-permute-start(bf16[1152,2048]{1,0:T(8,128)(2,1)} %constant_dynamic-update-slice_fusion), channel_id=1, source_target_pairs={{0,1},{1,0},{2,3},{3,2},{4,5},{5,4},{6,7},{7,6},{8,9},{9,8},{10,11... | collective-permute-start | bytes 14155784 | tf_op jit(solution)/shard_map/ppermute | solution.py:71
  448.0 25.6 %collective-permute-start.47 = (bf16[144,2048]{1,0:T(8,128)(2,1)S(1)}, bf16[144,2048]{1,0:T(8,128)(2,1)S(1)}, u32[]{:S(2)}, u32[]{:S(2)}) collective-permute-start(bf16[144,2048]{1,0:T(8,128)(2,1)S(1)} %slice.394), channel_id=1, source_target_pairs={{0,2},{1,3},{2,0},{3,1},{4,6},{5,7},{6,4},{7,5},{8,10},{9,11},{10,... | collective-permute-start | bytes 1769480 | tf_op jit(solution)/shard_map/ppermute | solution.py:71
  461.0 23.9 %collective-permute-start.50 = (bf16[128,2048]{1,0:T(8,128)(2,1)S(1)}, bf16[128,2048]{1,0:T(8,128)(2,1)S(1)}, u32[]{:S(2)}, u32[]{:S(2)}) collective-permute-start(bf16[128,2048]{1,0:T(8,128)(2,1)S(1)} %collective-permute-done.48), channel_id=1, source_target_pairs={{0,4},{4,0},{1,5},{5,1},{2,6},{6,2},{3,7},{7,3},{8,12},{12,8},{9,1... | collective-permute-start | bytes 1572872 | tf_op jit(solution)/shard_map/ppermute | solution.py:71
  493.0 27.8 %collective-permute-start.52 = (bf16[256,2048]{1,0:T(8,128)(2,1)S(1)}, bf16[256,2048]{1,0:T(8,128)(2,1)S(1)}, u32[]{:S(2)}, u32[]{:S(2)}) collective-permute-start(bf16[256,2048]{1,0:T(8,128)(2,1)S(1)} %copy-done.4), channel_id=1, source_target_pairs={{0,4},{4,0},{1,5},{5,1},{2,6},{6,2},{3,7},{7,3},{8,12},{12,8},{9,1... | collective-permute-start | bytes 3145736 | tf_op jit(solution)/shard_map/ppermute | solution.py:71
  494.3 26.5 %collective-permute-start.53 = (bf16[256,2048]{1,0:T(8,128)(2,1)S(1)}, bf16[256,2048]{1,0:T(8,128)(2,1)}, u32[]{:S(2)}, u32[]{:S(2)}) collective-permute-start(bf16[256,2048]{1,0:T(8,128)(2,1)S(1)} %copy-done.4), channel_id=1, source_target_pairs={{0,2},{1,3},{2,0},{3,1},{4,6},{5,7},{6,4},{7,5},{8,10},{9,11},{10,... | collective-permute-start | bytes 3145736 | tf_op jit(solution)/shard_map/ppermute | solution.py:71
  537.2 177.2 %reduce-scatter.11.cloned.1.call-start = ((), (), s32[]{:S(2)}) async-start(), calls=%async_computation.11 | async-start | bytes 1638400 | tf_op jit(solution)/shard_map/reduce_scatter | solution.py:787
  555.8 27.6 %collective-permute-start.56 = (bf16[144,2048]{1,0:T(8,128)(2,1)}, bf16[144,2048]{1,0:T(8,128)(2,1)}, u32[]{:S(2)}, u32[]{:S(2)}) collective-permute-start(bf16[144,2048]{1,0:T(8,128)(2,1)} %get-tuple-element.112), channel_id=1, source_target_pairs={{0,4},{4,0},{1,5},{5,1},{2,6},{6,2},{3,7},{7,3},{8,12},{12,8},{9,1... | collective-permute-start | bytes 1769480 | tf_op jit(solution)/shard_map/ppermute | solution.py:71
  556.9 26.5 %collective-permute-start.60 = (bf16[144,2048]{1,0:T(8,128)(2,1)S(1)}, bf16[144,2048]{1,0:T(8,128)(2,1)}, u32[]{:S(2)}, u32[]{:S(2)}) collective-permute-start(bf16[144,2048]{1,0:T(8,128)(2,1)S(1)} %get-tuple-element.113), channel_id=1, source_target_pairs={{0,2},{1,3},{2,0},{3,1},{4,6},{5,7},{6,4},{7,5},{8,10},{9,11},{10,... | collective-permute-start | bytes 1769480 | tf_op jit(solution)/shard_map/ppermute | solution.py:71
  561.3 30.0 %collective-permute-start.62 = (bf16[256,2048]{1,0:T(8,128)(2,1)}, bf16[256,2048]{1,0:T(8,128)(2,1)}, u32[]{:S(2)}, u32[]{:S(2)}) collective-permute-start(bf16[256,2048]{1,0:T(8,128)(2,1)} %convolution_convert_fusion.6), channel_id=1, source_target_pairs={{0,1},{1,0},{2,3},{3,2},{4,5},{5,4},{6,7},{7,6},{8,9},{9,8},{10,11... | collective-permute-start | bytes 3145736 | tf_op jit(solution)/shard_map/ppermute | solution.py:71
  607.1 146.9 %all-gather.15.cloned.1.call-start = ((), (), s32[]{:S(2)}) async-start(), calls=%async_computation.12 | async-start | bytes 9437184 | tf_op jit(solution)/shard_map/all_gather | solution.py:781
  607.9 23.0 %collective-permute-start.68 = (bf16[256,2048]{1,0:T(8,128)(2,1)S(1)}, bf16[256,2048]{1,0:T(8,128)(2,1)S(1)}, u32[]{:S(2)}, u32[]{:S(2)}) collective-permute-start(bf16[256,2048]{1,0:T(8,128)(2,1)S(1)} %copy-done.6), channel_id=1, source_target_pairs={{0,2},{1,3},{2,0},{3,1},{4,6},{5,7},{6,4},{7,5},{8,10},{9,11},{10,... | collective-permute-start | bytes 3145736 | tf_op jit(solution)/shard_map/ppermute | solution.py:71
  646.9 28.3 %collective-permute-start.66 = (bf16[512,768]{1,0:T(8,128)(2,1)S(1)}, bf16[512,768]{1,0:T(8,128)(2,1)S(1)}, u32[]{:S(2)}, u32[]{:S(2)}) collective-permute-start(bf16[512,768]{1,0:T(8,128)(2,1)S(1)} %copy-done.3), channel_id=1, source_target_pairs={{0,4},{4,0},{1,5},{5,1},{2,6},{6,2},{3,7},{7,3},{8,12},{12,8},{9,1... | collective-permute-start | bytes 2359304 | tf_op jit(solution)/shard_map/ppermute | solution.py:71
  646.9 28.9 %collective-permute-start.67 = (bf16[512,768]{1,0:T(8,128)(2,1)S(1)}, bf16[512,768]{1,0:T(8,128)(2,1)S(1)}, u32[]{:S(2)}, u32[]{:S(2)}) collective-permute-start(bf16[512,768]{1,0:T(8,128)(2,1)S(1)} %copy-done.3), channel_id=1, source_target_pairs={{0,2},{1,3},{2,0},{3,1},{4,6},{5,7},{6,4},{7,5},{8,10},{9,11},{10,... | collective-permute-start | bytes 2359304 | tf_op jit(solution)/shard_map/ppermute | solution.py:71
  677.0 37.4 %collective-permute-start.73 = (bf16[512,768]{1,0:T(8,128)(2,1)}, bf16[512,768]{1,0:T(8,128)(2,1)S(1)}, u32[]{:S(2)}, u32[]{:S(2)}) collective-permute-start(bf16[512,768]{1,0:T(8,128)(2,1)} %get-tuple-element.72.refs_1_), channel_id=1, source_target_pairs={{0,2},{1,3},{2,0},{3,1},{4,6},{5,7},{6,4},{7,5},{8,10},{9,11},{10,... | collective-permute-start | bytes 2359304 | tf_op jit(solution)/shard_map/ppermute | solution.py:71
  681.2 42.0 %collective-permute-start.81 = (bf16[512,768]{1,0:T(8,128)(2,1)S(1)}, bf16[512,768]{1,0:T(8,128)(2,1)S(1)}, u32[]{:S(2)}, u32[]{:S(2)}) collective-permute-start(bf16[512,768]{1,0:T(8,128)(2,1)S(1)} %copy-done.3), channel_id=1, source_target_pairs={{0,1},{1,0},{2,3},{3,2},{4,5},{5,4},{6,7},{7,6},{8,9},{9,8},{10,11... | collective-permute-start | bytes 2359304 | tf_op jit(solution)/shard_map/ppermute | solution.py:71
  682.7 38.3 %collective-permute-start.64 = (f32[16,2048]{1,0:T(8,128)S(1)}, f32[16,2048]{1,0:T(8,128)S(1)}, u32[]{:S(2)}, u32[]{:S(2)}) collective-permute-start(f32[16,2048]{1,0:T(8,128)S(1)} %get-tuple-element.128), channel_id=1, source_target_pairs={{0,2},{1,3},{2,0},{3,1},{4,6},{5,7},{6,4},{7,5},{8,10},{9,11},{10,... | collective-permute-start | bytes 393224 | tf_op jit(solution)/shard_map/ppermute | solution.py:71
  684.1 39.1 %collective-permute-start.65 = (f32[16,2048]{1,0:T(8,128)S(1)}, f32[16,2048]{1,0:T(8,128)S(1)}, u32[]{:S(2)}, u32[]{:S(2)}) collective-permute-start(f32[16,2048]{1,0:T(8,128)S(1)} %collective-permute-done.63), channel_id=1, source_target_pairs={{0,2},{1,3},{2,0},{3,1},{4,6},{5,7},{6,4},{7,5},{8,10},{9,11},{10,... | collective-permute-start | bytes 393224 | tf_op jit(solution)/shard_map/ppermute | solution.py:71
  (128 other events, 1915.8 us)
Sparse Core Ops, SparseCore 0:
  20.3 63.2 all-gather.6
  85.7 26.6 all-gather.8
  114.5 80.2 all-gather.10
  204.8 78.3 all-gather.12
  321.0 73.6 reduce-scatter.4
  439.7 73.2 reduce-scatter.6
  537.3 58.0 reduce-scatter.8
  607.3 28.6 reduce-scatter.10
  637.8 86.4 all-gather.14

commit v3 on v2

--- a/solution.py
+++ b/solution.py
@@ -134,10 +134,10 @@
                     if not self.bit(name, stage):
                         moves.append((side, name, held[side][self.step(name, stage)], stage))
             filled = None
-            if level < len(fills):
-                filled = fills[level](moves[-1][2])
             if before and level == 0:
                 moves = [(*move[:2], gate([move[2]], *before)[0], move[3]) if move[1] != (0, 0) else move for move in moves]
+            if level < len(fills):
+                filled = fills[level](moves[0][2])
             kept = [{}, {}]
             for number, (side, name, value, stage) in enumerate(moves):
                 moved = self.swap(value, stage)
@@ -158,16 +158,18 @@
             found[name] = self.swap(block, stage)
         return found
 
-    def complete(self, found, turned, before=()):
-        if before:
-            names = [name for name in found if name != (0, 0)]
-            held = gate([found[name] for name in names], *before)
-            found = {(0, 0): found[(0, 0)], **dict(zip(names, held))}
+    def extend(self, found, turned):
         for stage in self.slow[::-1] if turned else self.slow:
             for name, value in list(found.items()):
                 name = self.step(name, stage)
                 if name not in found:
                     found[name] = self.swap(value, stage)
+
+    def complete(self, found, turned, together=False):
+        names = [name for name in found if name != (0, 0)]
+        if together:
+            found = {(0, 0): found[(0, 0)], **dict(zip(names, gate([found[name] for name in names])))}
+        self.extend(found, turned)
         near = [found[name] for name in self.near]
         return [near + [self.swap(value) for value in near]]
 
@@ -662,33 +664,34 @@
     kept = []
 
     def upper_back(token):
-        kept.append(low(against(hold(cot_all, token), weight_down) * slope.astype(f32)))
+        kept.append(low(against(cot_all, weight_down) * slope.astype(f32)))
         return kept[0]
 
     def normed_back(token):
         return low(against(kept[0], weight_up))
 
     feed = low(dot(active, weight_down))
-    if kernels:
-        down_other = gate([down_other], feed[:16])[0]
     down_grad = low(across(active[:, :ff], cot_all) + down_other.astype(f32))
     down_mine = lax.psum_scatter(down_grad, "fsdp", scatter_dimension=0, tiled=True)
     feed, (upper_grad, partial) = plane.scatter(feed, (upper_back, normed_back))
     output = low(middle + (feed + bias_down))
     others = []
 
+    later = [upper_grad]
+
     def mate_grads(token):
-        others.append(plane.swap(low(across(normed_two, hold(upper_grad, token)[:, ff:]))))
+        if kernels:
+            later[0] = gate([upper_grad], token)[0]
+        others.append(plane.swap(low(across(normed_two, later[0][:, ff:]))))
         return others[0]
 
-    normed_two_grad, _ = plane.scatter(partial, (mate_grads,))
-    gain_back = gate([gain_two[None]], output)[0][0] if kernels else gain_two
+    normed_two_grad, _ = plane.scatter(partial, (mate_grads,), (feed,) if kernels else ())
+    up_other = gate([others[0]], down_mine)[0] if kernels else others[0]
+    up_grad = low(across(normed_two, later[0][:, :ff]) + up_other.astype(f32))
+    upper_grad = later[0]
+    gain_back = gate([gain_two[None]], up_grad[:16])[0][0] if kernels else gain_two
     middle_grad = cot_float + norm_input_grad(normed_two_grad, normal_two, inverse_two, gain_back)
     branch_grad = low(middle_grad)
-    up_other = gate([others[0]], branch_grad)[0] if kernels else others[0]
-    up_grad = low(across(normed_two, upper_grad[:, :ff]) + up_other.astype(f32))
-    if kernels:
-        up_grad = gate([up_grad], down_mine)[0]
     up_mine = lax.psum_scatter(up_grad, "fsdp", scatter_dimension=0, tiled=True)
     up_bias_grad = jnp.sum(upper_grad.astype(f32), axis=0)
     branch_all, _ = plane.gather(branch_grad)
@@ -699,7 +702,6 @@
     upstream = (upstream_near.reshape(shape), upstream_far.reshape(shape))
     fine = kernels and even and hidden % LANES == 0 and block * 2 == LANES and share % (2 * ROW_BLOCK) == 0
     if kernels:
-        info = gate([info], up_grad)[0]
         known = (info, projected, (mixed_near, mixed_far), upstream, log_totals, span_rows, heads)
         grads = attend_back_call(*known)
     else:
@@ -711,14 +713,19 @@
         grads = (grads[: spans // 2], grads[spans // 2 :])
     near, far = [g.reshape(count * piece_rows, 3 * width) for g in grads]
     if fine:
-        down_found = plane.whole(down_mine)
+        down_found = plane.whole(gate([down_mine], upstream_near)[0])
         near, far = gate([near, far], *[v for name, v in down_found.items() if name != (0, 0)])
     other = plane.swap(far)
     qkv_grad = low(across(normed, near) + across(plane.swap(normed), far))
     if fine:
         qkv_grad = gate([qkv_grad], up_mine)[0]
     qkv_mine = lax.psum_scatter(qkv_grad, "fsdp", scatter_dimension=0, tiled=True)
-    both = jnp.concatenate([near, gate([other], qkv_grad)[0] if kernels else other], axis=1)
+    if fine:
+        plane.extend(down_found, True)
+        other = gate([other], qkv_grad, down_found[plane.near[-1]])[0]
+    elif kernels:
+        other = gate([other], qkv_grad)[0]
+    both = jnp.concatenate([near, other], axis=1)
     partial = low(against(both, jnp.concatenate([weight_qkv, qkv_mate], axis=1)))
     def mate_out(token):
         others.append(low(across(attended[:, width:], hold(branch_all, token))))
@@ -776,7 +783,7 @@
     if fine:
         qkv_found = plane.whole(qkv_mine)
         down_all = place_rows(table, plane.complete(down_found, True))
-        sides = plane.complete(qkv_found, True, (down_all,))
+        sides = plane.complete(qkv_found, True, True)
         devices = jnp.arange(team, dtype=jnp.int32)
         up_full = lax.all_gather(gate([up_mine], qkv_mine)[0], PLANE, axis=0, tiled=False)
         up_all = place_columns(
@@ -786,7 +793,7 @@
         joined = jnp.concatenate([out_rows, vector], axis=1).reshape(-1, D)
         out_mine = lax.psum_scatter(joined, "fsdp", scatter_dimension=0, tiled=True)
         qkv_all = place_columns(functools.partial(place_heads_kernel, order), table, sides, share, 3 * D)
-        out_mine = gate([out_mine], sides[0][plane.half - 1])[0]
+        out_mine = gate([out_mine], down_all, *[v for name, v in qkv_found.items() if name != (0, 0)])[0]
         out_sides = plane.complete(plane.whole(out_mine), False)
         out_all = place_rows(table, out_sides, block)
         vectors = sum(rows[block:].astype(f32) for rows in out_sides[0])

time: 778 us -> 721 us (0.927)
  waiting for transfers between devices: 309 us -> 257 us
  matrix products: 166 us -> 155 us
    ppermute x85, waiting for transfers between devices: 290 us -> 230 us  [swap(): lax.ppermute(array, axis, [(i, i ^ bit) for i in range(self.sizes[axis])])]
    dot_general x5, matrix products: 52.8 us -> 43.8 us  [against(): lax.dot_general(left, right, (((1,), (1,)), ((), ())), preferred_element_...]
    unnamed x217 -> x203, local copies, waits for them, and re-layouts: 36.9 us -> 35.2 us
  transfers between devices with their start and end apart: 94 -> 94, of which waited for: 39 -> 34; matrix products, arithmetic and copies ran while one was open for 33% -> 37% of each run, Pallas kernels for 9% -> 10%
where the time goes in v3:
time: 721 us; the launch traced here: 714 us
  waiting for transfers between devices  257 us (36%)
  matrix products  155 us (21%)
  Pallas kernels  78 us (11%)
  starting transfers between devices  70.7 us (10%)
  local copies, waits for them, and re-layouts  67.8 us (9%)
  other arithmetic  55.2 us (8%)
  between operations  16.3 us (2%)
  blocking collectives  14.1 us (2%)
    ppermute x85, waiting for transfers between devices, swap(): lax.ppermute(array, axis, [(i, i ^ bit) for i in range(self.sizes[axis])])  230 us
    ppermute x85, starting transfers between devices, swap(): lax.ppermute(array, axis, [(i, i ^ bit) for i in range(self.sizes[axis])])  69 us
    dot_general x8, matrix products, across(): lax.dot_general(left, right, (((0,), (0,)), ((), ())), preferred_element_...  63.7 us
    dot_general x5, matrix products, dot(): return jnp.dot(left, right, preferred_element_type=f32)  47.5 us
    dot_general x5, matrix products, against(): lax.dot_general(left, right, (((1,), (1,)), ((), ())), preferred_element_...  43.8 us
    unnamed x203, local copies, waits for them, and re-layouts  35.2 us
    pallas_call x4, Pallas kernels, placed(): pl.pallas_call(kernel, out_shape=jax.ShapeDtypeStruct(shape, f32), grid_s...  29.5 us
    pallas_call x1, Pallas kernels, attend_back_call(): pl.pallas_call(functools.partial(attend_back_kernel, spans, span_rows), o...  26.5 us
  transfers between devices with their start and end apart: 94, of which 34 were waited for; matrix products, arithmetic and copies ran while one was open for 37% of the time, Pallas kernels for 10%

profile of v3, /device:TPU:0, one launch (start us, length us, event | category | flops | bytes accessed | tf_op | source)
XLA Modules:
  0.0 714.5 jit_solution(13391749261075877926)
XLA Ops:
  24.4 14.1 %all_gather.21 = bf16[192,128]{1,0:T(8,128)(2,1)S(1)} all-gather(bf16[48,128]{1,0:T(8,128)(2,1)S(1)} %bitcast.200), channel_id=1, replica_groups=mesh['fsdp'=4,'replica'=2,'ctx'=4] {'fsdp'}, dimensions={0}, use_global_device_ids=true | all-gather | bytes 61440 | tf_op jit(solution)/shard_map/all_gather | solution.py:582
  47.3 11.1 %collective-permute-done.9 = bf16[144,2048]{1,0:T(8,128)(2,1)S(1)} collective-permute-done((bf16[144,2048]{1,0:T(8,128)(2,1)S(1)}, bf16[144,2048]{1,0:T(8,128)(2,1)S(1)}, u32[]{:S(2)}, u32[]{:S(2)}) %collective-permute-start.9) | collective-permute-done | bytes 589856 | tf_op jit(solution)/shard_map/ppermute | solution.py:71
  62.3 10.3 %collective-permute-done.7 = bf16[144,2048]{1,0:T(8,128)(2,1)S(1)} collective-permute-done((bf16[144,2048]{1,0:T(8,128)(2,1)S(1)}, bf16[144,2048]{1,0:T(8,128)(2,1)S(1)}, u32[]{:S(2)}, u32[]{:S(2)}) %collective-permute-start.7) | collective-permute-done | bytes 589856 | tf_op jit(solution)/shard_map/ppermute | solution.py:71
  75.2 4.6 collective-permute-done.10
  85.2 8.4 %fusion.15 = bf16[1152,768]{1,0:T(8,128)(2,1)} fusion(bf16[1152,2048]{1,0:T(8,128)(2,1)} %constant_dynamic-update-slice_fusion, bf16[2048,768]{1,0:T(8,128)(2,1)} %all-gather.7.cloned.1.call-done, f32[768]{0:T(1024)S(1)} %copy-done.69, f32[768]{0:T(1024)S(1)} %reduce.5), kind=kOutput, calls=%fused_computation.38 | convolution fusion | flops 3626532864 | bytes 9639936 | tf_op jit(solution)/shard_map/dot_general | solution.py:30
  93.6 8.4 %fusion.16 = bf16[1152,768]{1,0:T(8,128)(2,1)} fusion(bf16[1152,2048]{1,0:T(8,128)(2,1)} %constant_dynamic-update-slice_fusion, bf16[2048,768]{1,0:T(8,128)(2,1)} %collective-permute-done.12, f32[768]{0:T(1024)S(1)} %reduce.6, f32[768]{0:T(1024)S(1)} %copy-done.69), kind=kOutput, calls=%fused_computation.39 | convolution fusion | flops 3626532864 | bytes 9639936 | tf_op jit(solution)/shard_map/dot_general | solution.py:30
  114.9 22.0 %attend.1 = (bf16[2,2,272,256]{3,2,1,0:T(8,128)(2,1)}, bf16[2,2,272,256]{3,2,1,0:T(8,128)(2,1)}, f32[2,2,2,1152]{3,2,1,0:T(2,128)}) custom-call(s32[3]{0:T(128)} %pad_add_fusion.info, bf16[2,2,288,768]{3,2,1,0:T(8,128)(2,1)} %bitcast.202, bf16[2,2,288,768]{3,2,1,0:T(8,128)(2,1)} %collective-permute-done.13.qf.kf.vf, bf16[2,2,288,768]{3,2,1,0:T(8,128)(2,1)} %bitcast.203, ...), custom_call_target="tpu_custom_call" | custom-call | flops 24000000000 | bytes 8000000 | tf_op jit(solution)/shard_map/attend/pallas_call | solution.py:388
  152.8 8.9 %collective-permute-done.20 = bf16[128,2048]{1,0:T(8,128)(2,1)S(1)} collective-permute-done((bf16[128,2048]{1,0:T(8,128)(2,1)S(1)}, bf16[128,2048]{1,0:T(8,128)(2,1)S(1)}, u32[]{:S(2)}, u32[]{:S(2)}) %collective-permute-start.20) | collective-permute-done | bytes 524320 | tf_op jit(solution)/shard_map/ppermute | solution.py:71
  167.1 5.9 collective-permute-done.19
  173.0 14.5 %collective-permute-done.21 = bf16[128,2048]{1,0:T(8,128)(2,1)} collective-permute-done((bf16[128,2048]{1,0:T(8,128)(2,1)}, bf16[128,2048]{1,0:T(8,128)(2,1)}, u32[]{:S(2)}, u32[]{:S(2)}) %collective-permute-start.21) | collective-permute-done | bytes 524320 | tf_op jit(solution)/shard_map/ppermute | solution.py:71
  205.8 9.3 %collective-permute-done.26 = bf16[128,2048]{1,0:T(8,128)(2,1)S(1)} collective-permute-done((bf16[128,2048]{1,0:T(8,128)(2,1)S(1)}, bf16[128,2048]{1,0:T(8,128)(2,1)S(1)}, u32[]{:S(2)}, u32[]{:S(2)}) %collective-permute-start.26) | collective-permute-done | bytes 524320 | tf_op jit(solution)/shard_map/ppermute | solution.py:71
  218.1 8.1 %collective-permute-done.24 = bf16[128,2048]{1,0:T(8,128)(2,1)} collective-permute-done((bf16[128,2048]{1,0:T(8,128)(2,1)S(1)}, bf16[128,2048]{1,0:T(8,128)(2,1)}, u32[]{:S(2)}, u32[]{:S(2)}) %collective-permute-start.24) | collective-permute-done | bytes 524320 | tf_op jit(solution)/shard_map/ppermute | solution.py:71
  229.9 9.5 %collective-permute-done.27 = bf16[144,2048]{1,0:T(8,128)(2,1)S(1)} collective-permute-done((bf16[144,2048]{1,0:T(8,128)(2,1)S(1)}, bf16[144,2048]{1,0:T(8,128)(2,1)S(1)}, u32[]{:S(2)}, u32[]{:S(2)}) %collective-permute-start.27) | collective-permute-done | bytes 589856 | tf_op jit(solution)/shard_map/ppermute | solution.py:71
  241.2 15.0 %multiply_convert_fusion = (bf16[1088,2048]{1,0:T(8,128)(2,1)S(1)}, f32[1088,2048]{1,0:T(8,128)}) fusion(f32[2048]{0:T(1024)S(1)} %pad_maximum_fusion.14, bf16[1088,2048]{1,0:T(8,128)(2,1)} %constant_dynamic-update-slice_fusion.15, bf16[2048,1024]{1,0:T(8,128)(2,1)} %collective-permute-done.29, bf16[2048,1024]{1,0:T(8,128)(2,1)S(1)} %copy-done.32), kind=kOutput, calls=%fused_computation.11 | convolution fusion | flops 9156952064 | bytes 26222592 | tf_op jit(solution)/shard_map/dot_general | solution.py:30
  256.2 11.2 %convolution_convert_fusion.5 = bf16[1024,2048]{1,0:T(8,128)(2,1)} fusion(bf16[1088,2048]{1,0:T(8,128)(2,1)} %constant_dynamic-update-slice_fusion.7.refs_1_, bf16[1088,2048]{1,0:T(8,128)(2,1)S(1)} %get-tuple-element.174), kind=kOutput, calls=%fused_computation.32 | convolution fusion | flops 4565499904 | bytes 10878976 | tf_op jit(solution)/shard_map/dot_general | solution.py:34
  267.4 15.8 %all-gather.13.cloned.1.call-done.refs_0_ = bf16[1024,2048]{1,0:T(8,128)(2,1)} async-done(((bf16[256,2048]{1,0:T(8,128)(2,1)}), bf16[1024,2048]{1,0:T(8,128)(2,1)}) %all-gather.13.cloned.1.call-update) | async-done | bytes 4194320 | tf_op jit(solution)/shard_map/all_gather | solution.py:597
  283.2 10.2 %add_convert_fusion.1 = bf16[1024,2048]{1,0:T(8,128)(2,1)} fusion(bf16[1024,2048]{1,0:T(8,128)(2,1)} %collective-permute-done.30.refs_1_, bf16[1088,2048]{1,0:T(8,128)(2,1)} %constant_dynamic-update-slice_fusion.7.refs_1_, bf16[1088,2048]{1,0:T(8,128)(2,1)} %copy-done.70), kind=kOutput, calls=%fused_computation.17 | convolution fusion | flops 4569694208 | bytes 15073280 | tf_op jit(solution)/shard_map/dot_general | solution.py:34
  293.7 13.2 %convolution_convert_fusion.1 = bf16[1088,2048]{1,0:T(8,128)(2,1)S(1)} fusion(bf16[1088,2048]{1,0:T(8,128)(2,1)} %copy-done.70, bf16[1024,2048]{1,0:T(8,128)(2,1)} %collective-permute-done.31, bf16[1024,2048]{1,0:T(8,128)(2,1)} %gate.18), kind=kOutput, calls=%fused_computation.20 | convolution fusion | flops 9145810944 | bytes 17301504 | tf_op jit(solution)/shard_map/dot_general | solution.py:30
  312.2 16.6 %fusion.6.refs_0_ = bf16[1088,2048]{1,0:T(8,128)(2,1)S(1)} fusion(bf16[1088,2048]{1,0:T(8,128)(2,1)} %constant_dynamic-update-slice_fusion.7.refs_1_, bf16[1024,2048]{1,0:T(8,128)(2,1)} %collective-permute-done.31, bf16[1024,2048]{1,0:T(8,128)(2,1)} %gate.18, f32[1088,2048]{1,0:T(8,128)} %get-tuple-element.175), kind=kOutput, calls=%fused_computation.18 | convolution fusion | flops 9170321408 | bytes 26214400 | tf_op jit(solution)/shard_map/dot_general | solution.py:38
  328.9 5.1 collective-permute-done.36
  336.7 12.2 %convolution_convert_fusion = bf16[1088,2048]{1,0:T(8,128)(2,1)S(1)} fusion(bf16[1088,2048]{1,0:T(8,128)(2,1)S(1)} %fusion.6.refs_0_, bf16[2048,1024]{1,0:T(8,128)(2,1)} %collective-permute-done.29, bf16[2048,1024]{1,0:T(8,128)(2,1)} %gate.17), kind=kOutput, calls=%fused_computation.19 | convolution fusion | flops 9145810944 | bytes 17301504 | tf_op jit(solution)/shard_map/dot_general | solution.py:38
  354.4 11.0 %collective-permute-done.34 = bf16[144,2048]{1,0:T(8,128)(2,1)S(1)} collective-permute-done((bf16[144,2048]{1,0:T(8,128)(2,1)S(1)}, bf16[144,2048]{1,0:T(8,128)(2,1)S(1)}, u32[]{:S(2)}, u32[]{:S(2)}) %collective-permute-start.34) | collective-permute-done | bytes 589856 | tf_op jit(solution)/shard_map/ppermute | solution.py:71
  368.5 9.6 %convolution_convert_fusion.4 = bf16[2048,1024]{1,0:T(8,128)(2,1)} fusion(bf16[1088,2048]{1,0:T(8,128)(2,1)} %constant_dynamic-update-slice_fusion.15, bf16[1088,2048]{1,0:T(8,128)(2,1)} %gate.20), kind=kOutput, calls=%fused_computation.31 | convolution fusion | flops 4565499904 | bytes 10878976 | tf_op jit(solution)/shard_map/dot_general | solution.py:34
  384.0 10.3 %collective-permute-done.39 = bf16[144,2048]{1,0:T(8,128)(2,1)S(1)} collective-permute-done((bf16[144,2048]{1,0:T(8,128)(2,1)S(1)}, bf16[144,2048]{1,0:T(8,128)(2,1)S(1)}, u32[]{:S(2)}, u32[]{:S(2)}) %collective-permute-start.39) | collective-permute-done | bytes 589856 | tf_op jit(solution)/shard_map/ppermute | solution.py:71
  400.6 6.0 collective-permute-done.38
  407.2 4.8 collective-permute-done.40
  413.7 7.8 %collective-permute-done.41 = bf16[128,2048]{1,0:T(8,128)(2,1)} collective-permute-done((bf16[128,2048]{1,0:T(8,128)(2,1)}, bf16[128,2048]{1,0:T(8,128)(2,1)}, u32[]{:S(2)}, u32[]{:S(2)}) %collective-permute-start.41) | collective-permute-done | bytes 524320 | tf_op jit(solution)/shard_map/ppermute | solution.py:71
  421.5 10.2 %add_convert_fusion = bf16[2048,1024]{1,0:T(8,128)(2,1)} fusion(bf16[2048,1024]{1,0:T(8,128)(2,1)} %gate.22, bf16[1088,2048]{1,0:T(8,128)(2,1)} %constant_dynamic-update-slice_fusion.15, bf16[1088,2048]{1,0:T(8,128)(2,1)} %gate.20), kind=kOutput, calls=%fused_computation.16 | convolution fusion | flops 4569694208 | bytes 15073280 | tf_op jit(solution)/shard_map/dot_general | solution.py:34
  447.1 9.9 %collective-permute-done.48 = bf16[128,2048]{1,0:T(8,128)(2,1)S(1)} collective-permute-done((bf16[128,2048]{1,0:T(8,128)(2,1)S(1)}, bf16[128,2048]{1,0:T(8,128)(2,1)S(1)}, u32[]{:S(2)}, u32[]{:S(2)}) %collective-permute-start.48) | collective-permute-done | bytes 524320 | tf_op jit(solution)/shard_map/ppermute | solution.py:71
  460.2 8.2 %collective-permute-done.46 = bf16[128,2048]{1,0:T(8,128)(2,1)} collective-permute-done((bf16[128,2048]{1,0:T(8,128)(2,1)S(1)}, bf16[128,2048]{1,0:T(8,128)(2,1)}, u32[]{:S(2)}, u32[]{:S(2)}) %collective-permute-start.46) | collective-permute-done | bytes 524320 | tf_op jit(solution)/shard_map/ppermute | solution.py:71
  469.8 9.3 %collective-permute-done.49 = bf16[144,2048]{1,0:T(8,128)(2,1)S(1)} collective-permute-done((bf16[144,2048]{1,0:T(8,128)(2,1)S(1)}, bf16[144,2048]{1,0:T(8,128)(2,1)S(1)}, u32[]{:S(2)}, u32[]{:S(2)}) %collective-permute-start.49) | collective-permute-done | bytes 589856 | tf_op jit(solution)/shard_map/ppermute | solution.py:71
  487.3 26.5 %attend_back.1 = (bf16[2,2,288,768]{3,2,1,0:T(8,128)(2,1)}, bf16[2,2,288,768]{3,2,1,0:T(8,128)(2,1)}) custom-call(s32[3]{0:T(128)} %pad_add_fusion.info, bf16[2,2,288,768]{3,2,1,0:T(8,128)(2,1)} %bitcast.205, bf16[2,2,288,768]{3,2,1,0:T(8,128)(2,1)} %collective-permute-done.13.qf.kf.vf, bf16[2,2,288,768]{3,2,1,0:T(8,128)(2,1)} %bitcast.206, ...), custom_call_target="tpu_custom_call" | custom-call | flops 30000001024 | bytes 16000000 | tf_op jit(solution)/shard_map/attend_back/pallas_call | solution.py:414
  515.4 6.9 fusion.68
  522.3 8.3 %add_convert_fusion.2.refs_0_ = bf16[2048,768]{1,0:T(8,128)(2,1)} fusion(f32[2048,768]{1,0:T(8,128)S(1)} %fusion.68, bf16[1152,2048]{1,0:T(8,128)(2,1)} %constant_dynamic-update-slice_fusion, bf16[1152,768]{1,0:T(8,128)(2,1)S(1)} %copy-done.24), kind=kOutput, calls=%fused_computation.26 | convolution fusion | flops 3627024384 | bytes 15925248 | tf_op jit(solution)/shard_map/dot_general | solution.py:34
  533.6 7.1 collective-permute-done.56.refs_2_.refs_3_
  540.7 11.4 %convert_reduce_fusion = (f32[2048]{0:T(1024)S(1)}, f32[2048]{0:T(1024)S(1)}, bf16[1152,2048]{1,0:T(8,128)(2,1)S(1)}) fusion(bf16[1152,2048]{1,0:T(8,128)(2,1)} %constant_dynamic-update-slice_fusion, bf16[2048,768]{1,0:T(8,128)(2,1)} %collective-permute-done.12, bf16[2048,768]{1,0:T(8,128)(2,1)} %all-gather.7.cloned.1.call-done, ...), kind=kOutput, calls=%fused_computation.1 | convolution fusion | flops 7281569792 | bytes 19283968 | tf_op jit(solution)/shard_map/dot_general | solution.py:38
  558.5 11.1 %collective-permute-done.58 = bf16[144,2048]{1,0:T(8,128)(2,1)S(1)} collective-permute-done((bf16[144,2048]{1,0:T(8,128)(2,1)S(1)}, bf16[144,2048]{1,0:T(8,128)(2,1)S(1)}, u32[]{:S(2)}, u32[]{:S(2)}) %collective-permute-start.58) | collective-permute-done | bytes 589856 | tf_op jit(solution)/shard_map/ppermute | solution.py:71
  571.9 9.2 %collective-permute-done.57 = bf16[144,2048]{1,0:T(8,128)(2,1)} collective-permute-done((bf16[144,2048]{1,0:T(8,128)(2,1)}, bf16[144,2048]{1,0:T(8,128)(2,1)}, u32[]{:S(2)}, u32[]{:S(2)}) %collective-permute-start.57) | collective-permute-done | bytes 589856 | tf_op jit(solution)/shard_map/ppermute | solution.py:71
  588.0 4.9 fusion.22.refs_0_
  592.9 6.3 collective-permute-done.62
  604.5 9.5 %collective-permute-done.60 = bf16[144,2048]{1,0:T(8,128)(2,1)} collective-permute-done((bf16[144,2048]{1,0:T(8,128)(2,1)}, bf16[144,2048]{1,0:T(8,128)(2,1)}, u32[]{:S(2)}, u32[]{:S(2)}) %collective-permute-start.60) | collective-permute-done | bytes 589856 | tf_op jit(solution)/shard_map/ppermute | solution.py:71
  620.2 8.9 %place.4.refs_1_ = f32[2048,2048]{1,0:T(8,128)} custom-call(s32[8]{0:T(128)S(1)} %xor_add_fusion.table, bf16[256,2048]{1,0:T(8,128)(2,1)S(1)} %copy-done.3, bf16[256,2048]{1,0:T(8,128)(2,1)} %collective-permute-done.52.refs_2_.refs_1_, bf16[256,2048]{1,0:T(8,128)(2,1)S(1)} %copy-done.6, bf16[256,2048]{1,0:T(8,128)(2,1)} %collective-permute-done.56.refs_2_.refs_3_, ...), custom_call_target="tpu_custom_call" | custom-call | bytes 25165824 | tf_op jit(solution)/shard_map/place/pallas_call | solution.py:479
  638.6 10.8 %collective-permute-done.74.refs_2_ = bf16[80,2048]{1,0:T(8,128)(2,1)S(1)} collective-permute-done((bf16[80,2048]{1,0:T(8,128)(2,1)}, bf16[80,2048]{1,0:T(8,128)(2,1)S(1)}, u32[]{:S(2)}, u32[]{:S(2)}) %collective-permute-start.74) | collective-permute-done | bytes 327712 | tf_op jit(solution)/shard_map/ppermute | solution.py:71
  660.7 13.4 %collective-permute-done.80.refs_3_ = bf16[512,768]{1,0:T(8,128)(2,1)S(1)} collective-permute-done((bf16[512,768]{1,0:T(8,128)(2,1)}, bf16[512,768]{1,0:T(8,128)(2,1)S(1)}, u32[]{:S(2)}, u32[]{:S(2)}) %collective-permute-start.80) | collective-permute-done | bytes 786464 | tf_op jit(solution)/shard_map/ppermute | solution.py:71
  675.9 4.1 place.6
  680.7 9.4 %place.5 = f32[512,6144]{1,0:T(8,128)} custom-call(s32[8]{0:T(128)S(1)} %xor_add_fusion.table, bf16[512,768]{1,0:T(8,128)(2,1)} %reduce-scatter.9.cloned.1.call-done.refs_1_.refs_0_, bf16[512,768]{1,0:T(8,128)(2,1)} %get-tuple-element.68.refs_1_, bf16[512,768]{1,0:T(8,128)(2,1)} %get-tuple-element.69.refs_2_, ...), custom_call_target="tpu_custom_call" | custom-call | bytes 18874368 | tf_op jit(solution)/shard_map/place/pallas_call | solution.py:479
  690.1 7.1 all-gather.15.cloned.1.call-done
  700.6 7.1 place.7
  (514 shorter events, 214.6 us)
Async XLA Ops:
  7.2 76.4 %all-gather.7.cloned.1.call-start = ((), (), s32[]{:S(2)}) async-start(), calls=%async_computation.4 | async-start | bytes 3932160 | tf_op jit(solution)/shard_map/all_gather | solution.py:578
  9.3 30.8 %collective-permute-start.1 = (bf16[144,2048]{1,0:T(8,128)(2,1)}, bf16[144,2048]{1,0:T(8,128)(2,1)}, u32[]{:S(2)}, u32[]{:S(2)}) collective-permute-start(bf16[144,2048]{1,0:T(8,128)(2,1)} %slice_bitcast_fusion), channel_id=1, source_target_pairs={{0,2},{1,3},{2,0},{3,1},{4,6},{5,7},{6,4},{7,5},{8,10},{9,11},{10,... | collective-permute-start | bytes 1769480 | tf_op jit(solution)/shard_map/ppermute | solution.py:71
  12.3 27.8 %collective-permute-start = (bf16[144,2048]{1,0:T(8,128)(2,1)}, bf16[144,2048]{1,0:T(8,128)(2,1)}, u32[]{:S(2)}, u32[]{:S(2)}) collective-permute-start(bf16[144,2048]{1,0:T(8,128)(2,1)} %slice_bitcast_fusion), channel_id=1, source_target_pairs={{0,4},{4,0},{1,5},{5,1},{2,6},{6,2},{3,7},{7,3},{8,12},{12,8},{9,1... | collective-permute-start | bytes 1769480 | tf_op jit(solution)/shard_map/ppermute | solution.py:71
  20.1 94.7 %all-gather.9.cloned.1.call-start = ((), (), s32[]{:S(2)}) async-start(), calls=%async_computation.5 | async-start | bytes 1310720 | tf_op jit(solution)/shard_map/all_gather | solution.py:591
  45.2 27.4 %collective-permute-start.7 = (bf16[144,2048]{1,0:T(8,128)(2,1)S(1)}, bf16[144,2048]{1,0:T(8,128)(2,1)S(1)}, u32[]{:S(2)}, u32[]{:S(2)}) collective-permute-start(bf16[144,2048]{1,0:T(8,128)(2,1)S(1)} %get-tuple-element.127), channel_id=1, source_target_pairs={{0,4},{4,0},{1,5},{5,1},{2,6},{6,2},{3,7},{7,3},{8,12},{12,8},{9,1... | collective-permute-start | bytes 1769480 | tf_op jit(solution)/shard_map/ppermute | solution.py:71
  45.7 27.8 %collective-permute-start.8 = (bf16[144,2048]{1,0:T(8,128)(2,1)S(1)}, bf16[144,2048]{1,0:T(8,128)(2,1)S(1)}, u32[]{:S(2)}, u32[]{:S(2)}) collective-permute-start(bf16[144,2048]{1,0:T(8,128)(2,1)S(1)} %get-tuple-element.128), channel_id=1, source_target_pairs={{0,2},{1,3},{2,0},{3,1},{4,6},{5,7},{6,4},{7,5},{8,10},{9,11},{10,... | collective-permute-start | bytes 1769480 | tf_op jit(solution)/shard_map/ppermute | solution.py:71
  58.5 22.3 %collective-permute-start.11 = (bf16[144,2048]{1,0:T(8,128)(2,1)S(1)}, bf16[144,2048]{1,0:T(8,128)(2,1)S(1)}, u32[]{:S(2)}, u32[]{:S(2)}) collective-permute-start(bf16[144,2048]{1,0:T(8,128)(2,1)S(1)} %collective-permute-done.9), channel_id=1, source_target_pairs={{0,4},{4,0},{1,5},{5,1},{2,6},{6,2},{3,7},{7,3},{8,12},{12,8},{9,1... | collective-permute-start | bytes 1769480 | tf_op jit(solution)/shard_map/ppermute | solution.py:71
  84.3 110.5 %all-gather.11.cloned.1.call-start = ((), (), s32[]{:S(2)}) async-start(), calls=%async_computation.6 | async-start | bytes 5242880 | tf_op jit(solution)/shard_map/all_gather | solution.py:596
  106.4 176.8 %all-gather.13.cloned.1.call-start = ((), (), s32[]{:S(2)}) async-start(), calls=%async_computation.7 | async-start | bytes 5242880 | tf_op jit(solution)/shard_map/all_gather | solution.py:597
  110.9 26.0 %collective-permute-start.4 = (bf16[128,2048]{1,0:T(8,128)(2,1)}, bf16[128,2048]{1,0:T(8,128)(2,1)S(1)}, u32[]{:S(2)}, u32[]{:S(2)}) collective-permute-start(bf16[128,2048]{1,0:T(8,128)(2,1)} %collective-permute-done.2), channel_id=1, source_target_pairs={{0,4},{4,0},{1,5},{5,1},{2,6},{6,2},{3,7},{7,3},{8,12},{12,8},{9,1... | collective-permute-start | bytes 1572872 | tf_op jit(solution)/shard_map/ppermute | solution.py:71
  111.4 38.4 %collective-permute-start.22 = (bf16[144,2048]{1,0:T(8,128)(2,1)}, bf16[144,2048]{1,0:T(8,128)(2,1)S(1)}, u32[]{:S(2)}, u32[]{:S(2)}) collective-permute-start(bf16[144,2048]{1,0:T(8,128)(2,1)} %collective-permute-done), channel_id=1, source_target_pairs={{0,2},{1,3},{2,0},{3,1},{4,6},{5,7},{6,4},{7,5},{8,10},{9,11},{10,... | collective-permute-start | bytes 1769480 | tf_op jit(solution)/shard_map/ppermute | solution.py:71
  114.9 28.5 %collective-permute-start.15 = (bf16[256,2048]{1,0:T(8,128)(2,1)}, bf16[256,2048]{1,0:T(8,128)(2,1)S(1)}, u32[]{:S(2)}, u32[]{:S(2)}) collective-permute-start(bf16[256,2048]{1,0:T(8,128)(2,1)} %all-gather.9.cloned.1.call-done), channel_id=1, source_target_pairs={{0,1},{1,0},{2,3},{3,2},{4,5},{5,4},{6,7},{7,6},{8,9},{9,8},{10,11... | collective-permute-start | bytes 3145736 | tf_op jit(solution)/shard_map/ppermute | solution.py:71
  150.7 22.3 %collective-permute-start.19 = (bf16[128,2048]{1,0:T(8,128)(2,1)}, bf16[128,2048]{1,0:T(8,128)(2,1)}, u32[]{:S(2)}, u32[]{:S(2)}) collective-permute-start(bf16[128,2048]{1,0:T(8,128)(2,1)} %get-tuple-element.122), channel_id=1, source_target_pairs={{0,2},{1,3},{2,0},{3,1},{4,6},{5,7},{6,4},{7,5},{8,10},{9,11},{10,... | collective-permute-start | bytes 1572872 | tf_op jit(solution)/shard_map/ppermute | solution.py:71
  152.2 36.9 %collective-permute-start.16 = (bf16[144,2048]{1,0:T(8,128)(2,1)}, bf16[144,2048]{1,0:T(8,128)(2,1)S(1)}, u32[]{:S(2)}, u32[]{:S(2)}) collective-permute-start(bf16[144,2048]{1,0:T(8,128)(2,1)} %get-tuple-element.120), channel_id=1, source_target_pairs={{0,4},{4,0},{1,5},{5,1},{2,6},{6,2},{3,7},{7,3},{8,12},{12,8},{9,1... | collective-permute-start | bytes 1769480 | tf_op jit(solution)/shard_map/ppermute | solution.py:71
  162.6 24.9 %collective-permute-start.21 = (bf16[128,2048]{1,0:T(8,128)(2,1)}, bf16[128,2048]{1,0:T(8,128)(2,1)}, u32[]{:S(2)}, u32[]{:S(2)}) collective-permute-start(bf16[128,2048]{1,0:T(8,128)(2,1)} %add_convert_fusion.11), channel_id=1, source_target_pairs={{0,4},{4,0},{1,5},{5,1},{2,6},{6,2},{3,7},{7,3},{8,12},{12,8},{9,1... | collective-permute-start | bytes 1572872 | tf_op jit(solution)/shard_map/ppermute | solution.py:71
  164.7 24.4 %collective-permute-start.18 = (bf16[144,2048]{1,0:T(8,128)(2,1)S(1)}, bf16[144,2048]{1,0:T(8,128)(2,1)}, u32[]{:S(2)}, u32[]{:S(2)}) collective-permute-start(bf16[144,2048]{1,0:T(8,128)(2,1)S(1)} %add_convert_fusion.8), channel_id=1, source_target_pairs={{0,2},{1,3},{2,0},{3,1},{4,6},{5,7},{6,4},{7,5},{8,10},{9,11},{10,... | collective-permute-start | bytes 1769480 | tf_op jit(solution)/shard_map/ppermute | solution.py:71
  194.8 46.3 %collective-permute-start.29 = (bf16[2048,1024]{1,0:T(8,128)(2,1)}, bf16[2048,1024]{1,0:T(8,128)(2,1)}, u32[]{:S(2)}, u32[]{:S(2)}) collective-permute-start(bf16[2048,1024]{1,0:T(8,128)(2,1)} %gate.17), channel_id=1, source_target_pairs={{0,1},{1,0},{2,3},{3,2},{4,5},{5,4},{6,7},{7,6},{8,9},{9,8},{10,11... | collective-permute-start | bytes 12582920 | tf_op jit(solution)/shard_map/ppermute | solution.py:71
  201.8 24.4 %collective-permute-start.24 = (bf16[128,2048]{1,0:T(8,128)(2,1)S(1)}, bf16[128,2048]{1,0:T(8,128)(2,1)}, u32[]{:S(2)}, u32[]{:S(2)}) collective-permute-start(bf16[128,2048]{1,0:T(8,128)(2,1)S(1)} %slice.380), channel_id=1, source_target_pairs={{0,4},{4,0},{1,5},{5,1},{2,6},{6,2},{3,7},{7,3},{8,12},{12,8},{9,1... | collective-permute-start | bytes 1572872 | tf_op jit(solution)/shard_map/ppermute | solution.py:71
  204.7 216.8 %reduce-scatter.5.cloned.1.call-start = ((), (), s32[]{:S(2)}) async-start(), calls=%async_computation.8 | async-start | bytes 5242880 | tf_op jit(solution)/shard_map/reduce_scatter | solution.py:675
  205.2 23.0 %collective-permute-start.25 = (bf16[144,2048]{1,0:T(8,128)(2,1)S(1)}, bf16[144,2048]{1,0:T(8,128)(2,1)S(1)}, u32[]{:S(2)}, u32[]{:S(2)}) collective-permute-start(bf16[144,2048]{1,0:T(8,128)(2,1)S(1)} %slice.379), channel_id=1, source_target_pairs={{0,2},{1,3},{2,0},{3,1},{4,6},{5,7},{6,4},{7,5},{8,10},{9,11},{10,... | collective-permute-start | bytes 1769480 | tf_op jit(solution)/shard_map/ppermute | solution.py:71
  215.1 25.2 %collective-permute-start.28 = (bf16[128,2048]{1,0:T(8,128)(2,1)S(1)}, bf16[128,2048]{1,0:T(8,128)(2,1)S(1)}, u32[]{:S(2)}, u32[]{:S(2)}) collective-permute-start(bf16[128,2048]{1,0:T(8,128)(2,1)S(1)} %collective-permute-done.26), channel_id=1, source_target_pairs={{0,4},{4,0},{1,5},{5,1},{2,6},{6,2},{3,7},{7,3},{8,12},{12,8},{9,1... | collective-permute-start | bytes 1572872 | tf_op jit(solution)/shard_map/ppermute | solution.py:71
  215.6 23.8 %collective-permute-start.27 = (bf16[144,2048]{1,0:T(8,128)(2,1)S(1)}, bf16[144,2048]{1,0:T(8,128)(2,1)S(1)}, u32[]{:S(2)}, u32[]{:S(2)}) collective-permute-start(bf16[144,2048]{1,0:T(8,128)(2,1)S(1)} %collective-permute-done.23), channel_id=1, source_target_pairs={{0,2},{1,3},{2,0},{3,1},{4,6},{5,7},{6,4},{7,5},{8,10},{9,11},{10,... | collective-permute-start | bytes 1769480 | tf_op jit(solution)/shard_map/ppermute | solution.py:71
  293.4 237.1 %reduce-scatter.7.cloned.1.call-start = ((), (), s32[]{:S(2)}) async-start(), calls=%async_computation.9 | async-start | bytes 5242880 | tf_op jit(solution)/shard_map/reduce_scatter | solution.py:695
  308.1 40.8 %collective-permute-start.35 = (bf16[128,2048]{1,0:T(8,128)(2,1)}, bf16[128,2048]{1,0:T(8,128)(2,1)S(1)}, u32[]{:S(2)}, u32[]{:S(2)}) collective-permute-start(bf16[128,2048]{1,0:T(8,128)(2,1)} %get-tuple-element.118), channel_id=1, source_target_pairs={{0,2},{1,3},{2,0},{3,1},{4,6},{5,7},{6,4},{7,5},{8,10},{9,11},{10,... | collective-permute-start | bytes 1572872 | tf_op jit(solution)/shard_map/ppermute | solution.py:71
  309.7 24.3 %collective-permute-start.36 = (bf16[128,2048]{1,0:T(8,128)(2,1)}, bf16[128,2048]{1,0:T(8,128)(2,1)S(1)}, u32[]{:S(2)}, u32[]{:S(2)}) collective-permute-start(bf16[128,2048]{1,0:T(8,128)(2,1)} %get-tuple-element.119), channel_id=1, source_target_pairs={{0,2},{1,3},{2,0},{3,1},{4,6},{5,7},{6,4},{7,5},{8,10},{9,11},{10,... | collective-permute-start | bytes 1572872 | tf_op jit(solution)/shard_map/ppermute | solution.py:71
  310.2 44.2 %collective-permute-start.32 = (bf16[144,2048]{1,0:T(8,128)(2,1)S(1)}, bf16[144,2048]{1,0:T(8,128)(2,1)S(1)}, u32[]{:S(2)}, u32[]{:S(2)}) collective-permute-start(bf16[144,2048]{1,0:T(8,128)(2,1)S(1)} %get-tuple-element.116), channel_id=1, source_target_pairs={{0,4},{4,0},{1,5},{5,1},{2,6},{6,2},{3,7},{7,3},{8,12},{12,8},{9,1... | collective-permute-start | bytes 1769480 | tf_op jit(solution)/shard_map/ppermute | solution.py:71
  311.7 37.2 %collective-permute-start.33 = (bf16[144,2048]{1,0:T(8,128)(2,1)S(1)}, bf16[144,2048]{1,0:T(8,128)(2,1)S(1)}, u32[]{:S(2)}, u32[]{:S(2)}) collective-permute-start(bf16[144,2048]{1,0:T(8,128)(2,1)S(1)} %get-tuple-element.117), channel_id=1, source_target_pairs={{0,4},{4,0},{1,5},{5,1},{2,6},{6,2},{3,7},{7,3},{8,12},{12,8},{9,1... | collective-permute-start | bytes 1769480 | tf_op jit(solution)/shard_map/ppermute | solution.py:71
  378.1 43.4 %collective-permute-start.42 = (bf16[2048,1024]{1,0:T(8,128)(2,1)}, bf16[2048,1024]{1,0:T(8,128)(2,1)}, u32[]{:S(2)}, u32[]{:S(2)}) collective-permute-start(bf16[2048,1024]{1,0:T(8,128)(2,1)} %convolution_convert_fusion.4), channel_id=1, source_target_pairs={{0,1},{1,0},{2,3},{3,2},{4,5},{5,4},{6,7},{7,6},{8,9},{9,8},{10,11... | collective-permute-start | bytes 12582920 | tf_op jit(solution)/shard_map/ppermute | solution.py:71
  378.8 27.8 %collective-permute-start.38 = (bf16[144,2048]{1,0:T(8,128)(2,1)S(1)}, bf16[144,2048]{1,0:T(8,128)(2,1)}, u32[]{:S(2)}, u32[]{:S(2)}) collective-permute-start(bf16[144,2048]{1,0:T(8,128)(2,1)S(1)} %get-tuple-element.112), channel_id=1, source_target_pairs={{0,4},{4,0},{1,5},{5,1},{2,6},{6,2},{3,7},{7,3},{8,12},{12,8},{9,1... | collective-permute-start | bytes 1769480 | tf_op jit(solution)/shard_map/ppermute | solution.py:71
  397.9 117.5 %collective-permute-start.55 = (bf16[1152,2048]{1,0:T(8,128)(2,1)}, bf16[1152,2048]{1,0:T(8,128)(2,1)}, u32[]{:S(2)}, u32[]{:S(2)}) collective-permute-start(bf16[1152,2048]{1,0:T(8,128)(2,1)} %constant_dynamic-update-slice_fusion), channel_id=1, source_target_pairs={{0,1},{1,0},{2,3},{3,2},{4,5},{5,4},{6,7},{7,6},{8,9},{9,8},{10,11... | collective-permute-start | bytes 14155784 | tf_op jit(solution)/shard_map/ppermute | solution.py:71
  397.9 23.6 %collective-permute-start.41 = (bf16[128,2048]{1,0:T(8,128)(2,1)}, bf16[128,2048]{1,0:T(8,128)(2,1)}, u32[]{:S(2)}, u32[]{:S(2)}) collective-permute-start(bf16[128,2048]{1,0:T(8,128)(2,1)} %get-tuple-element.114), channel_id=1, source_target_pairs={{0,2},{1,3},{2,0},{3,1},{4,6},{5,7},{6,4},{7,5},{8,10},{9,11},{10,... | collective-permute-start | bytes 1572872 | tf_op jit(solution)/shard_map/ppermute | solution.py:71
  406.6 26.9 %collective-permute-start.44 = (bf16[128,2048]{1,0:T(8,128)(2,1)}, bf16[128,2048]{1,0:T(8,128)(2,1)}, u32[]{:S(2)}, u32[]{:S(2)}) collective-permute-start(bf16[128,2048]{1,0:T(8,128)(2,1)} %add_convert_fusion.9), channel_id=1, source_target_pairs={{0,4},{4,0},{1,5},{5,1},{2,6},{6,2},{3,7},{7,3},{8,12},{12,8},{9,1... | collective-permute-start | bytes 1572872 | tf_op jit(solution)/shard_map/ppermute | solution.py:71
  431.7 167.5 %reduce-scatter.9.cloned.1.call-start = ((), (), s32[]{:S(2)}) async-start(), calls=%async_computation.10 | async-start | bytes 3932160 | tf_op jit(solution)/shard_map/reduce_scatter | solution.py:722
  443.8 24.7 %collective-permute-start.46 = (bf16[128,2048]{1,0:T(8,128)(2,1)S(1)}, bf16[128,2048]{1,0:T(8,128)(2,1)}, u32[]{:S(2)}, u32[]{:S(2)}) collective-permute-start(bf16[128,2048]{1,0:T(8,128)(2,1)S(1)} %slice.397), channel_id=1, source_target_pairs={{0,4},{4,0},{1,5},{5,1},{2,6},{6,2},{3,7},{7,3},{8,12},{12,8},{9,1... | collective-permute-start | bytes 1572872 | tf_op jit(solution)/shard_map/ppermute | solution.py:71
  445.4 24.4 %collective-permute-start.47 = (bf16[144,2048]{1,0:T(8,128)(2,1)S(1)}, bf16[144,2048]{1,0:T(8,128)(2,1)S(1)}, u32[]{:S(2)}, u32[]{:S(2)}) collective-permute-start(bf16[144,2048]{1,0:T(8,128)(2,1)S(1)} %slice.396), channel_id=1, source_target_pairs={{0,2},{1,3},{2,0},{3,1},{4,6},{5,7},{6,4},{7,5},{8,10},{9,11},{10,... | collective-permute-start | bytes 1769480 | tf_op jit(solution)/shard_map/ppermute | solution.py:71
  457.1 22.1 %collective-permute-start.50 = (bf16[128,2048]{1,0:T(8,128)(2,1)S(1)}, bf16[128,2048]{1,0:T(8,128)(2,1)S(1)}, u32[]{:S(2)}, u32[]{:S(2)}) collective-permute-start(bf16[128,2048]{1,0:T(8,128)(2,1)S(1)} %collective-permute-done.48), channel_id=1, source_target_pairs={{0,4},{4,0},{1,5},{5,1},{2,6},{6,2},{3,7},{7,3},{8,12},{12,8},{9,1... | collective-permute-start | bytes 1572872 | tf_op jit(solution)/shard_map/ppermute | solution.py:71
  483.5 30.3 %collective-permute-start.53 = (bf16[256,2048]{1,0:T(8,128)(2,1)}, bf16[256,2048]{1,0:T(8,128)(2,1)S(1)}, u32[]{:S(2)}, u32[]{:S(2)}) collective-permute-start(bf16[256,2048]{1,0:T(8,128)(2,1)} %gate.24.refs_0_), channel_id=1, source_target_pairs={{0,2},{1,3},{2,0},{3,1},{4,6},{5,7},{6,4},{7,5},{8,10},{9,11},{10,... | collective-permute-start | bytes 3145736 | tf_op jit(solution)/shard_map/ppermute | solution.py:71
  485.2 28.7 %collective-permute-start.52 = (bf16[256,2048]{1,0:T(8,128)(2,1)}, bf16[256,2048]{1,0:T(8,128)(2,1)}, u32[]{:S(2)}, u32[]{:S(2)}) collective-permute-start(bf16[256,2048]{1,0:T(8,128)(2,1)} %gate.24.refs_0_), channel_id=1, source_target_pairs={{0,4},{4,0},{1,5},{5,1},{2,6},{6,2},{3,7},{7,3},{8,12},{12,8},{9,1... | collective-permute-start | bytes 3145736 | tf_op jit(solution)/shard_map/ppermute | solution.py:71
  514.8 25.9 %collective-permute-start.54 = (bf16[1152,768]{1,0:T(8,128)(2,1)}, bf16[1152,768]{1,0:T(8,128)(2,1)}, u32[]{:S(2)}, u32[]{:S(2)}) collective-permute-start(bf16[1152,768]{1,0:T(8,128)(2,1)} %get-tuple-element.63), channel_id=1, source_target_pairs={{0,1},{1,0},{2,3},{3,2},{4,5},{5,4},{6,7},{7,6},{8,9},{9,8},{10,11... | collective-permute-start | bytes 5308424 | tf_op jit(solution)/shard_map/ppermute | solution.py:71
  514.8 25.9 %collective-permute-start.56 = (bf16[256,2048]{1,0:T(8,128)(2,1)}, bf16[256,2048]{1,0:T(8,128)(2,1)}, u32[]{:S(2)}, u32[]{:S(2)}) collective-permute-start(bf16[256,2048]{1,0:T(8,128)(2,1)} %collective-permute-done.52.refs_2_.refs_1_), channel_id=1, source_target_pairs={{0,2},{1,3},{2,0},{3,1},{4,6},{5,7},{6,4},{7,5},{8,10},{9,11},{10,... | collective-permute-start | bytes 3145736 | tf_op jit(solution)/shard_map/ppermute | solution.py:71
  530.6 101.4 %reduce-scatter.11.cloned.1.call-start = ((), (), s32[]{:S(2)}) async-start(), calls=%async_computation.11 | async-start | bytes 1638400 | tf_op jit(solution)/shard_map/reduce_scatter | solution.py:794
  554.0 27.1 %collective-permute-start.57 = (bf16[144,2048]{1,0:T(8,128)(2,1)}, bf16[144,2048]{1,0:T(8,128)(2,1)}, u32[]{:S(2)}, u32[]{:S(2)}) collective-permute-start(bf16[144,2048]{1,0:T(8,128)(2,1)} %get-tuple-element.108), channel_id=1, source_target_pairs={{0,4},{4,0},{1,5},{5,1},{2,6},{6,2},{3,7},{7,3},{8,12},{12,8},{9,1... | collective-permute-start | bytes 1769480 | tf_op jit(solution)/shard_map/ppermute | solution.py:71
  555.5 25.6 %collective-permute-start.61 = (bf16[144,2048]{1,0:T(8,128)(2,1)S(1)}, bf16[144,2048]{1,0:T(8,128)(2,1)}, u32[]{:S(2)}, u32[]{:S(2)}) collective-permute-start(bf16[144,2048]{1,0:T(8,128)(2,1)S(1)} %get-tuple-element.109), channel_id=1, source_target_pairs={{0,2},{1,3},{2,0},{3,1},{4,6},{5,7},{6,4},{7,5},{8,10},{9,11},{10,... | collective-permute-start | bytes 1769480 | tf_op jit(solution)/shard_map/ppermute | solution.py:71
  558.5 29.5 %collective-permute-start.63 = (bf16[256,2048]{1,0:T(8,128)(2,1)}, bf16[256,2048]{1,0:T(8,128)(2,1)S(1)}, u32[]{:S(2)}, u32[]{:S(2)}) collective-permute-start(bf16[256,2048]{1,0:T(8,128)(2,1)} %convolution_convert_fusion.6), channel_id=1, source_target_pairs={{0,1},{1,0},{2,3},{3,2},{4,5},{5,4},{6,7},{7,6},{8,9},{9,8},{10,11... | collective-permute-start | bytes 3145736 | tf_op jit(solution)/shard_map/ppermute | solution.py:71
  601.9 95.3 %all-gather.15.cloned.1.call-start = ((), (), s32[]{:S(2)}) async-start(), calls=%async_computation.12 | async-start | bytes 9437184 | tf_op jit(solution)/shard_map/all_gather | solution.py:788
  637.6 36.5 %collective-permute-start.80 = (bf16[512,768]{1,0:T(8,128)(2,1)}, bf16[512,768]{1,0:T(8,128)(2,1)S(1)}, u32[]{:S(2)}, u32[]{:S(2)}) collective-permute-start(bf16[512,768]{1,0:T(8,128)(2,1)} %get-tuple-element.68.refs_1_), channel_id=1, source_target_pairs={{0,2},{1,3},{2,0},{3,1},{4,6},{5,7},{6,4},{7,5},{8,10},{9,11},{10,... | collective-permute-start | bytes 2359304 | tf_op jit(solution)/shard_map/ppermute | solution.py:71
  655.7 24.9 %collective-permute-start.81 = (bf16[512,768]{1,0:T(8,128)(2,1)}, bf16[512,768]{1,0:T(8,128)(2,1)S(1)}, u32[]{:S(2)}, u32[]{:S(2)}) collective-permute-start(bf16[512,768]{1,0:T(8,128)(2,1)} %reduce-scatter.9.cloned.1.call-done.refs_1_.refs_0_), channel_id=1, source_target_pairs={{0,1},{1,0},{2,3},{3,2},{4,5},{5,4},{6,7},{7,6},{8,9},{9,8},{10,11... | collective-permute-start | bytes 2359304 | tf_op jit(solution)/shard_map/ppermute | solution.py:71
  656.1 24.6 %collective-permute-start.82 = (bf16[512,768]{1,0:T(8,128)(2,1)}, bf16[512,768]{1,0:T(8,128)(2,1)S(1)}, u32[]{:S(2)}, u32[]{:S(2)}) collective-permute-start(bf16[512,768]{1,0:T(8,128)(2,1)} %get-tuple-element.68.refs_1_), channel_id=1, source_target_pairs={{0,1},{1,0},{2,3},{3,2},{4,5},{5,4},{6,7},{7,6},{8,9},{9,8},{10,11... | collective-permute-start | bytes 2359304 | tf_op jit(solution)/shard_map/ppermute | solution.py:71
  (121 other events, 1557.7 us)
Sparse Core Ops, SparseCore 0:
  20.3 63.2 all-gather.6
  85.7 26.6 all-gather.8
  114.5 80.2 all-gather.10
  204.8 78.3 all-gather.12
  293.5 75.4 reduce-scatter.4
  431.8 74.3 reduce-scatter.6
  530.7 58.7 reduce-scatter.8
  601.9 28.7 reduce-scatter.10
  632.6 64.5 all-gather.14

commit v4 on v3

--- a/solution.py
+++ b/solution.py
@@ -136,7 +136,7 @@
             filled = None
             if before and level == 0:
                 moves = [(*move[:2], gate([move[2]], *before)[0], move[3]) if move[1] != (0, 0) else move for move in moves]
-            if level < len(fills):
+            if level < len(fills) and fills[level] is not None:
                 filled = fills[level](moves[0][2])
             kept = [{}, {}]
             for number, (side, name, value, stage) in enumerate(moves):
@@ -685,7 +685,7 @@
         others.append(plane.swap(low(across(normed_two, later[0][:, ff:]))))
         return others[0]
 
-    normed_two_grad, _ = plane.scatter(partial, (mate_grads,), (feed,) if kernels else ())
+    normed_two_grad, _ = plane.scatter(partial, (None, mate_grads), (feed,) if kernels else ())
     up_other = gate([others[0]], down_mine)[0] if kernels else others[0]
     up_grad = low(across(normed_two, later[0][:, :ff]) + up_other.astype(f32))
     upper_grad = later[0]

time: 721 us -> 727 us (level)
    unnamed x203 -> x205, local copies, waits for them, and re-layouts: 35.2 us -> 35.2 us
  transfers between devices with their start and end apart: 94 -> 94, of which waited for: 34 -> 33; matrix products, arithmetic and copies ran while one was open for 37% -> 37% of each run, Pallas kernels for 10% -> 10%
where the time goes in v4:
time: 727 us; the launch traced here: 720 us
  waiting for transfers between devices  263 us (36%)
  matrix products  155 us (21%)
  Pallas kernels  78 us (11%)
  starting transfers between devices  69.5 us (10%)
  local copies, waits for them, and re-layouts  67.8 us (9%)
  other arithmetic  56.1 us (8%)
  between operations  16.3 us (2%)
  blocking collectives  14.1 us (2%)
    ppermute x85, waiting for transfers between devices, swap(): lax.ppermute(array, axis, [(i, i ^ bit) for i in range(self.sizes[axis])])  236 us
    ppermute x85, starting transfers between devices, swap(): lax.ppermute(array, axis, [(i, i ^ bit) for i in range(self.sizes[axis])])  67.7 us
    dot_general x8, matrix products, across(): lax.dot_general(left, right, (((0,), (0,)), ((), ())), preferred_element_...  63.7 us
    dot_general x5, matrix products, dot(): return jnp.dot(left, right, preferred_element_type=f32)  47.5 us
    dot_general x5, matrix products, against(): lax.dot_general(left, right, (((1,), (1,)), ((), ())), preferred_element_...  43.8 us
    unnamed x205, local copies, waits for them, and re-layouts  35.2 us
    pallas_call x4, Pallas kernels, placed(): pl.pallas_call(kernel, out_shape=jax.ShapeDtypeStruct(shape, f32), grid_s...  29.5 us
    pallas_call x1, Pallas kernels, attend_back_call(): pl.pallas_call(functools.partial(attend_back_kernel, spans, span_rows), o...  26.5 us
  transfers between devices with their start and end apart: 94, of which 33 were waited for; matrix products, arithmetic and copies ran while one was open for 37% of the time, Pallas kernels for 10%

profile of v4, /device:TPU:0, one launch (start us, length us, event | category | flops | bytes accessed | tf_op | source)
XLA Modules:
  0.0 719.9 jit_solution(10842272965771258863)
XLA Ops:
  24.4 14.1 %all_gather.21 = bf16[192,128]{1,0:T(8,128)(2,1)S(1)} all-gather(bf16[48,128]{1,0:T(8,128)(2,1)S(1)} %bitcast.200), channel_id=1, replica_groups=mesh['fsdp'=4,'replica'=2,'ctx'=4] {'fsdp'}, dimensions={0}, use_global_device_ids=true | all-gather | bytes 61440 | tf_op jit(solution)/shard_map/all_gather | solution.py:582
  47.3 11.1 %collective-permute-done.9 = bf16[144,2048]{1,0:T(8,128)(2,1)S(1)} collective-permute-done((bf16[144,2048]{1,0:T(8,128)(2,1)S(1)}, bf16[144,2048]{1,0:T(8,128)(2,1)S(1)}, u32[]{:S(2)}, u32[]{:S(2)}) %collective-permute-start.9) | collective-permute-done | bytes 589856 | tf_op jit(solution)/shard_map/ppermute | solution.py:71
  62.3 10.3 %collective-permute-done.7 = bf16[144,2048]{1,0:T(8,128)(2,1)S(1)} collective-permute-done((bf16[144,2048]{1,0:T(8,128)(2,1)S(1)}, bf16[144,2048]{1,0:T(8,128)(2,1)S(1)}, u32[]{:S(2)}, u32[]{:S(2)}) %collective-permute-start.7) | collective-permute-done | bytes 589856 | tf_op jit(solution)/shard_map/ppermute | solution.py:71
  75.2 4.6 collective-permute-done.10
  85.2 8.4 %fusion.15 = bf16[1152,768]{1,0:T(8,128)(2,1)} fusion(bf16[1152,2048]{1,0:T(8,128)(2,1)} %constant_dynamic-update-slice_fusion, bf16[2048,768]{1,0:T(8,128)(2,1)} %all-gather.7.cloned.1.call-done, f32[768]{0:T(1024)S(1)} %copy-done.70, f32[768]{0:T(1024)S(1)} %reduce.5), kind=kOutput, calls=%fused_computation.38 | convolution fusion | flops 3626532864 | bytes 9639936 | tf_op jit(solution)/shard_map/dot_general | solution.py:30
  93.6 8.4 %fusion.16 = bf16[1152,768]{1,0:T(8,128)(2,1)} fusion(bf16[1152,2048]{1,0:T(8,128)(2,1)} %constant_dynamic-update-slice_fusion, bf16[2048,768]{1,0:T(8,128)(2,1)} %collective-permute-done.12, f32[768]{0:T(1024)S(1)} %reduce.6, f32[768]{0:T(1024)S(1)} %copy-done.70), kind=kOutput, calls=%fused_computation.39 | convolution fusion | flops 3626532864 | bytes 9639936 | tf_op jit(solution)/shard_map/dot_general | solution.py:30
  114.9 22.0 %attend.1 = (bf16[2,2,272,256]{3,2,1,0:T(8,128)(2,1)}, bf16[2,2,272,256]{3,2,1,0:T(8,128)(2,1)}, f32[2,2,2,1152]{3,2,1,0:T(2,128)}) custom-call(s32[3]{0:T(128)} %pad_add_fusion.info, bf16[2,2,288,768]{3,2,1,0:T(8,128)(2,1)} %bitcast.202, bf16[2,2,288,768]{3,2,1,0:T(8,128)(2,1)} %collective-permute-done.13.qf.kf.vf, bf16[2,2,288,768]{3,2,1,0:T(8,128)(2,1)} %bitcast.203, ...), custom_call_target="tpu_custom_call" | custom-call | flops 24000000000 | bytes 8000000 | tf_op jit(solution)/shard_map/attend/pallas_call | solution.py:388
  152.8 8.9 %collective-permute-done.20 = bf16[128,2048]{1,0:T(8,128)(2,1)S(1)} collective-permute-done((bf16[128,2048]{1,0:T(8,128)(2,1)S(1)}, bf16[128,2048]{1,0:T(8,128)(2,1)S(1)}, u32[]{:S(2)}, u32[]{:S(2)}) %collective-permute-start.20) | collective-permute-done | bytes 524320 | tf_op jit(solution)/shard_map/ppermute | solution.py:71
  167.2 5.9 collective-permute-done.19
  173.0 14.5 %collective-permute-done.21 = bf16[128,2048]{1,0:T(8,128)(2,1)} collective-permute-done((bf16[128,2048]{1,0:T(8,128)(2,1)}, bf16[128,2048]{1,0:T(8,128)(2,1)}, u32[]{:S(2)}, u32[]{:S(2)}) %collective-permute-start.21) | collective-permute-done | bytes 524320 | tf_op jit(solution)/shard_map/ppermute | solution.py:71
  205.7 9.3 %collective-permute-done.26 = bf16[128,2048]{1,0:T(8,128)(2,1)S(1)} collective-permute-done((bf16[128,2048]{1,0:T(8,128)(2,1)S(1)}, bf16[128,2048]{1,0:T(8,128)(2,1)S(1)}, u32[]{:S(2)}, u32[]{:S(2)}) %collective-permute-start.26) | collective-permute-done | bytes 524320 | tf_op jit(solution)/shard_map/ppermute | solution.py:71
  218.0 8.1 %collective-permute-done.24 = bf16[128,2048]{1,0:T(8,128)(2,1)} collective-permute-done((bf16[128,2048]{1,0:T(8,128)(2,1)S(1)}, bf16[128,2048]{1,0:T(8,128)(2,1)}, u32[]{:S(2)}, u32[]{:S(2)}) %collective-permute-start.24) | collective-permute-done | bytes 524320 | tf_op jit(solution)/shard_map/ppermute | solution.py:71
  229.8 9.5 %collective-permute-done.27 = bf16[144,2048]{1,0:T(8,128)(2,1)S(1)} collective-permute-done((bf16[144,2048]{1,0:T(8,128)(2,1)S(1)}, bf16[144,2048]{1,0:T(8,128)(2,1)S(1)}, u32[]{:S(2)}, u32[]{:S(2)}) %collective-permute-start.27) | collective-permute-done | bytes 589856 | tf_op jit(solution)/shard_map/ppermute | solution.py:71
  241.1 15.0 %multiply_convert_fusion = (bf16[1088,2048]{1,0:T(8,128)(2,1)S(1)}, f32[1088,2048]{1,0:T(8,128)}) fusion(f32[2048]{0:T(1024)S(1)} %pad_maximum_fusion.14, bf16[1088,2048]{1,0:T(8,128)(2,1)} %constant_dynamic-update-slice_fusion.15, bf16[2048,1024]{1,0:T(8,128)(2,1)} %collective-permute-done.29, bf16[2048,1024]{1,0:T(8,128)(2,1)S(1)} %copy-done.31), kind=kOutput, calls=%fused_computation.11 | convolution fusion | flops 9156952064 | bytes 26222592 | tf_op jit(solution)/shard_map/dot_general | solution.py:30
  256.2 11.2 %convolution_convert_fusion.5 = bf16[1024,2048]{1,0:T(8,128)(2,1)} fusion(bf16[1088,2048]{1,0:T(8,128)(2,1)} %constant_dynamic-update-slice_fusion.7.refs_1_, bf16[1088,2048]{1,0:T(8,128)(2,1)S(1)} %get-tuple-element.174), kind=kOutput, calls=%fused_computation.32 | convolution fusion | flops 4565499904 | bytes 10878976 | tf_op jit(solution)/shard_map/dot_general | solution.py:34
  267.3 15.8 %all-gather.13.cloned.1.call-done.refs_0_ = bf16[1024,2048]{1,0:T(8,128)(2,1)} async-done(((bf16[256,2048]{1,0:T(8,128)(2,1)}), bf16[1024,2048]{1,0:T(8,128)(2,1)}) %all-gather.13.cloned.1.call-update) | async-done | bytes 4194320 | tf_op jit(solution)/shard_map/all_gather | solution.py:597
  283.2 10.2 %add_convert_fusion.1 = bf16[1024,2048]{1,0:T(8,128)(2,1)} fusion(bf16[1024,2048]{1,0:T(8,128)(2,1)} %collective-permute-done.30.refs_1_, bf16[1088,2048]{1,0:T(8,128)(2,1)} %constant_dynamic-update-slice_fusion.7.refs_1_, bf16[1088,2048]{1,0:T(8,128)(2,1)} %copy-done.71), kind=kOutput, calls=%fused_computation.17 | convolution fusion | flops 4569694208 | bytes 15073280 | tf_op jit(solution)/shard_map/dot_general | solution.py:34
  293.6 13.2 %convolution_convert_fusion.1 = bf16[1088,2048]{1,0:T(8,128)(2,1)S(1)} fusion(bf16[1088,2048]{1,0:T(8,128)(2,1)} %copy-done.71, bf16[1024,2048]{1,0:T(8,128)(2,1)} %collective-permute-done.31, bf16[1024,2048]{1,0:T(8,128)(2,1)} %gate.18), kind=kOutput, calls=%fused_computation.20 | convolution fusion | flops 9145810944 | bytes 17301504 | tf_op jit(solution)/shard_map/dot_general | solution.py:30
  312.2 16.6 %fusion.6.refs_0_ = bf16[1088,2048]{1,0:T(8,128)(2,1)S(1)} fusion(bf16[1088,2048]{1,0:T(8,128)(2,1)} %constant_dynamic-update-slice_fusion.7.refs_1_, bf16[1024,2048]{1,0:T(8,128)(2,1)} %collective-permute-done.31, bf16[1024,2048]{1,0:T(8,128)(2,1)} %gate.18, f32[1088,2048]{1,0:T(8,128)} %get-tuple-element.175), kind=kOutput, calls=%fused_computation.18 | convolution fusion | flops 9170321408 | bytes 26214400 | tf_op jit(solution)/shard_map/dot_general | solution.py:38
  328.8 5.2 collective-permute-done.36
  336.9 12.2 %convolution_convert_fusion = bf16[1088,2048]{1,0:T(8,128)(2,1)S(1)} fusion(bf16[1088,2048]{1,0:T(8,128)(2,1)S(1)} %fusion.6.refs_0_, bf16[2048,1024]{1,0:T(8,128)(2,1)} %collective-permute-done.29, bf16[2048,1024]{1,0:T(8,128)(2,1)} %gate.17), kind=kOutput, calls=%fused_computation.19 | convolution fusion | flops 9145810944 | bytes 17301504 | tf_op jit(solution)/shard_map/dot_general | solution.py:38
  354.7 10.9 %collective-permute-done.34 = bf16[144,2048]{1,0:T(8,128)(2,1)S(1)} collective-permute-done((bf16[144,2048]{1,0:T(8,128)(2,1)S(1)}, bf16[144,2048]{1,0:T(8,128)(2,1)S(1)}, u32[]{:S(2)}, u32[]{:S(2)}) %collective-permute-start.34) | collective-permute-done | bytes 589856 | tf_op jit(solution)/shard_map/ppermute | solution.py:71
  369.2 13.5 %collective-permute-done.39 = bf16[144,2048]{1,0:T(8,128)(2,1)S(1)} collective-permute-done((bf16[144,2048]{1,0:T(8,128)(2,1)}, bf16[144,2048]{1,0:T(8,128)(2,1)S(1)}, u32[]{:S(2)}, u32[]{:S(2)}) %collective-permute-start.39) | collective-permute-done | bytes 589856 | tf_op jit(solution)/shard_map/ppermute | solution.py:71
  384.7 9.5 %convolution_convert_fusion.4 = bf16[2048,1024]{1,0:T(8,128)(2,1)} fusion(bf16[1088,2048]{1,0:T(8,128)(2,1)} %constant_dynamic-update-slice_fusion.15, bf16[1088,2048]{1,0:T(8,128)(2,1)} %gate.21), kind=kOutput, calls=%fused_computation.31 | convolution fusion | flops 4565499904 | bytes 10878976 | tf_op jit(solution)/shard_map/dot_general | solution.py:34
  399.3 12.4 %collective-permute-done.42 = bf16[128,2048]{1,0:T(8,128)(2,1)S(1)} collective-permute-done((bf16[128,2048]{1,0:T(8,128)(2,1)}, bf16[128,2048]{1,0:T(8,128)(2,1)S(1)}, u32[]{:S(2)}, u32[]{:S(2)}) %collective-permute-start.42) | collective-permute-done | bytes 524320 | tf_op jit(solution)/shard_map/ppermute | solution.py:71
  416.6 7.8 %collective-permute-done.40 = bf16[144,2048]{1,0:T(8,128)(2,1)} collective-permute-done((bf16[144,2048]{1,0:T(8,128)(2,1)S(1)}, bf16[144,2048]{1,0:T(8,128)(2,1)}, u32[]{:S(2)}, u32[]{:S(2)}) %collective-permute-start.40) | collective-permute-done | bytes 589856 | tf_op jit(solution)/shard_map/ppermute | solution.py:71
  426.8 10.2 %add_convert_fusion = bf16[2048,1024]{1,0:T(8,128)(2,1)} fusion(bf16[2048,1024]{1,0:T(8,128)(2,1)} %gate.22, bf16[1088,2048]{1,0:T(8,128)(2,1)} %constant_dynamic-update-slice_fusion.15, bf16[1088,2048]{1,0:T(8,128)(2,1)} %gate.21), kind=kOutput, calls=%fused_computation.16 | convolution fusion | flops 4569694208 | bytes 15073280 | tf_op jit(solution)/shard_map/dot_general | solution.py:34
  452.5 9.8 %collective-permute-done.48 = bf16[128,2048]{1,0:T(8,128)(2,1)S(1)} collective-permute-done((bf16[128,2048]{1,0:T(8,128)(2,1)S(1)}, bf16[128,2048]{1,0:T(8,128)(2,1)S(1)}, u32[]{:S(2)}, u32[]{:S(2)}) %collective-permute-start.48) | collective-permute-done | bytes 524320 | tf_op jit(solution)/shard_map/ppermute | solution.py:71
  465.6 8.2 %collective-permute-done.46 = bf16[128,2048]{1,0:T(8,128)(2,1)} collective-permute-done((bf16[128,2048]{1,0:T(8,128)(2,1)S(1)}, bf16[128,2048]{1,0:T(8,128)(2,1)}, u32[]{:S(2)}, u32[]{:S(2)}) %collective-permute-start.46) | collective-permute-done | bytes 524320 | tf_op jit(solution)/shard_map/ppermute | solution.py:71
  475.0 9.4 %collective-permute-done.49 = bf16[144,2048]{1,0:T(8,128)(2,1)S(1)} collective-permute-done((bf16[144,2048]{1,0:T(8,128)(2,1)S(1)}, bf16[144,2048]{1,0:T(8,128)(2,1)S(1)}, u32[]{:S(2)}, u32[]{:S(2)}) %collective-permute-start.49) | collective-permute-done | bytes 589856 | tf_op jit(solution)/shard_map/ppermute | solution.py:71
  492.8 26.5 %attend_back.1 = (bf16[2,2,288,768]{3,2,1,0:T(8,128)(2,1)}, bf16[2,2,288,768]{3,2,1,0:T(8,128)(2,1)}) custom-call(s32[3]{0:T(128)} %pad_add_fusion.info, bf16[2,2,288,768]{3,2,1,0:T(8,128)(2,1)} %bitcast.205, bf16[2,2,288,768]{3,2,1,0:T(8,128)(2,1)} %collective-permute-done.13.qf.kf.vf, bf16[2,2,288,768]{3,2,1,0:T(8,128)(2,1)} %bitcast.206, ...), custom_call_target="tpu_custom_call" | custom-call | flops 30000001024 | bytes 16000000 | tf_op jit(solution)/shard_map/attend_back/pallas_call | solution.py:414
  520.7 6.9 fusion.68
  527.7 8.4 %add_convert_fusion.2.refs_0_ = bf16[2048,768]{1,0:T(8,128)(2,1)} fusion(f32[2048,768]{1,0:T(8,128)S(1)} %fusion.68, bf16[1152,2048]{1,0:T(8,128)(2,1)} %constant_dynamic-update-slice_fusion, bf16[1152,768]{1,0:T(8,128)(2,1)S(1)} %copy-done.24), kind=kOutput, calls=%fused_computation.26 | convolution fusion | flops 3627024384 | bytes 15925248 | tf_op jit(solution)/shard_map/dot_general | solution.py:34
  539.1 7.0 collective-permute-done.56.refs_2_.refs_3_
  546.1 11.4 %convert_reduce_fusion = (f32[2048]{0:T(1024)S(1)}, f32[2048]{0:T(1024)S(1)}, bf16[1152,2048]{1,0:T(8,128)(2,1)S(1)}) fusion(bf16[1152,2048]{1,0:T(8,128)(2,1)} %constant_dynamic-update-slice_fusion, bf16[2048,768]{1,0:T(8,128)(2,1)} %collective-permute-done.12, bf16[2048,768]{1,0:T(8,128)(2,1)} %all-gather.7.cloned.1.call-done, ...), kind=kOutput, calls=%fused_computation.1 | convolution fusion | flops 7281569792 | bytes 19283968 | tf_op jit(solution)/shard_map/dot_general | solution.py:38
  563.9 11.1 %collective-permute-done.58 = bf16[144,2048]{1,0:T(8,128)(2,1)S(1)} collective-permute-done((bf16[144,2048]{1,0:T(8,128)(2,1)S(1)}, bf16[144,2048]{1,0:T(8,128)(2,1)S(1)}, u32[]{:S(2)}, u32[]{:S(2)}) %collective-permute-start.58) | collective-permute-done | bytes 589856 | tf_op jit(solution)/shard_map/ppermute | solution.py:71
  577.2 9.3 %collective-permute-done.57 = bf16[144,2048]{1,0:T(8,128)(2,1)} collective-permute-done((bf16[144,2048]{1,0:T(8,128)(2,1)}, bf16[144,2048]{1,0:T(8,128)(2,1)}, u32[]{:S(2)}, u32[]{:S(2)}) %collective-permute-start.57) | collective-permute-done | bytes 589856 | tf_op jit(solution)/shard_map/ppermute | solution.py:71
  593.4 4.8 fusion.22.refs_0_
  598.2 6.4 collective-permute-done.62
  609.8 9.6 %collective-permute-done.60 = bf16[144,2048]{1,0:T(8,128)(2,1)} collective-permute-done((bf16[144,2048]{1,0:T(8,128)(2,1)}, bf16[144,2048]{1,0:T(8,128)(2,1)}, u32[]{:S(2)}, u32[]{:S(2)}) %collective-permute-start.60) | collective-permute-done | bytes 589856 | tf_op jit(solution)/shard_map/ppermute | solution.py:71
  625.6 8.9 %place.4.refs_1_ = f32[2048,2048]{1,0:T(8,128)} custom-call(s32[8]{0:T(128)S(1)} %xor_add_fusion.table, bf16[256,2048]{1,0:T(8,128)(2,1)S(1)} %copy-done.3, bf16[256,2048]{1,0:T(8,128)(2,1)} %collective-permute-done.52.refs_2_.refs_1_, bf16[256,2048]{1,0:T(8,128)(2,1)S(1)} %copy-done.6, bf16[256,2048]{1,0:T(8,128)(2,1)} %collective-permute-done.56.refs_2_.refs_3_, ...), custom_call_target="tpu_custom_call" | custom-call | bytes 25165824 | tf_op jit(solution)/shard_map/place/pallas_call | solution.py:479
  643.9 11.0 %collective-permute-done.74.refs_2_ = bf16[80,2048]{1,0:T(8,128)(2,1)S(1)} collective-permute-done((bf16[80,2048]{1,0:T(8,128)(2,1)}, bf16[80,2048]{1,0:T(8,128)(2,1)S(1)}, u32[]{:S(2)}, u32[]{:S(2)}) %collective-permute-start.74) | collective-permute-done | bytes 327712 | tf_op jit(solution)/shard_map/ppermute | solution.py:71
  661.4 4.2 collective-permute-done.75.refs_3_
  666.1 13.5 %collective-permute-done.80.refs_3_ = bf16[512,768]{1,0:T(8,128)(2,1)S(1)} collective-permute-done((bf16[512,768]{1,0:T(8,128)(2,1)}, bf16[512,768]{1,0:T(8,128)(2,1)S(1)}, u32[]{:S(2)}, u32[]{:S(2)}) %collective-permute-start.80) | collective-permute-done | bytes 786464 | tf_op jit(solution)/shard_map/ppermute | solution.py:71
  681.4 4.1 place.6
  686.2 9.4 %place.5 = f32[512,6144]{1,0:T(8,128)} custom-call(s32[8]{0:T(128)S(1)} %xor_add_fusion.table, bf16[512,768]{1,0:T(8,128)(2,1)} %reduce-scatter.9.cloned.1.call-done.refs_1_.refs_0_, bf16[512,768]{1,0:T(8,128)(2,1)} %get-tuple-element.68.refs_1_, bf16[512,768]{1,0:T(8,128)(2,1)} %get-tuple-element.69.refs_2_, ...), custom_call_target="tpu_custom_call" | custom-call | bytes 18874368 | tf_op jit(solution)/shard_map/place/pallas_call | solution.py:479
  695.5 7.1 all-gather.15.cloned.1.call-done
  706.0 7.1 place.7
  (516 shorter events, 210.6 us)
Async XLA Ops:
  7.2 76.3 %all-gather.7.cloned.1.call-start = ((), (), s32[]{:S(2)}) async-start(), calls=%async_computation.4 | async-start | bytes 3932160 | tf_op jit(solution)/shard_map/all_gather | solution.py:578
  9.3 30.8 %collective-permute-start.1 = (bf16[144,2048]{1,0:T(8,128)(2,1)}, bf16[144,2048]{1,0:T(8,128)(2,1)}, u32[]{:S(2)}, u32[]{:S(2)}) collective-permute-start(bf16[144,2048]{1,0:T(8,128)(2,1)} %slice_bitcast_fusion), channel_id=1, source_target_pairs={{0,2},{1,3},{2,0},{3,1},{4,6},{5,7},{6,4},{7,5},{8,10},{9,11},{10,... | collective-permute-start | bytes 1769480 | tf_op jit(solution)/shard_map/ppermute | solution.py:71
  12.3 27.8 %collective-permute-start = (bf16[144,2048]{1,0:T(8,128)(2,1)}, bf16[144,2048]{1,0:T(8,128)(2,1)}, u32[]{:S(2)}, u32[]{:S(2)}) collective-permute-start(bf16[144,2048]{1,0:T(8,128)(2,1)} %slice_bitcast_fusion), channel_id=1, source_target_pairs={{0,4},{4,0},{1,5},{5,1},{2,6},{6,2},{3,7},{7,3},{8,12},{12,8},{9,1... | collective-permute-start | bytes 1769480 | tf_op jit(solution)/shard_map/ppermute | solution.py:71
  20.1 94.8 %all-gather.9.cloned.1.call-start = ((), (), s32[]{:S(2)}) async-start(), calls=%async_computation.5 | async-start | bytes 1310720 | tf_op jit(solution)/shard_map/all_gather | solution.py:591
  45.2 27.4 %collective-permute-start.7 = (bf16[144,2048]{1,0:T(8,128)(2,1)S(1)}, bf16[144,2048]{1,0:T(8,128)(2,1)S(1)}, u32[]{:S(2)}, u32[]{:S(2)}) collective-permute-start(bf16[144,2048]{1,0:T(8,128)(2,1)S(1)} %get-tuple-element.127), channel_id=1, source_target_pairs={{0,4},{4,0},{1,5},{5,1},{2,6},{6,2},{3,7},{7,3},{8,12},{12,8},{9,1... | collective-permute-start | bytes 1769480 | tf_op jit(solution)/shard_map/ppermute | solution.py:71
  45.7 27.7 %collective-permute-start.8 = (bf16[144,2048]{1,0:T(8,128)(2,1)S(1)}, bf16[144,2048]{1,0:T(8,128)(2,1)S(1)}, u32[]{:S(2)}, u32[]{:S(2)}) collective-permute-start(bf16[144,2048]{1,0:T(8,128)(2,1)S(1)} %get-tuple-element.128), channel_id=1, source_target_pairs={{0,2},{1,3},{2,0},{3,1},{4,6},{5,7},{6,4},{7,5},{8,10},{9,11},{10,... | collective-permute-start | bytes 1769480 | tf_op jit(solution)/shard_map/ppermute | solution.py:71
  58.4 22.3 %collective-permute-start.11 = (bf16[144,2048]{1,0:T(8,128)(2,1)S(1)}, bf16[144,2048]{1,0:T(8,128)(2,1)S(1)}, u32[]{:S(2)}, u32[]{:S(2)}) collective-permute-start(bf16[144,2048]{1,0:T(8,128)(2,1)S(1)} %collective-permute-done.9), channel_id=1, source_target_pairs={{0,4},{4,0},{1,5},{5,1},{2,6},{6,2},{3,7},{7,3},{8,12},{12,8},{9,1... | collective-permute-start | bytes 1769480 | tf_op jit(solution)/shard_map/ppermute | solution.py:71
  84.3 110.5 %all-gather.11.cloned.1.call-start = ((), (), s32[]{:S(2)}) async-start(), calls=%async_computation.6 | async-start | bytes 5242880 | tf_op jit(solution)/shard_map/all_gather | solution.py:596
  106.4 176.8 %all-gather.13.cloned.1.call-start = ((), (), s32[]{:S(2)}) async-start(), calls=%async_computation.7 | async-start | bytes 5242880 | tf_op jit(solution)/shard_map/all_gather | solution.py:597
  110.9 26.0 %collective-permute-start.4 = (bf16[128,2048]{1,0:T(8,128)(2,1)}, bf16[128,2048]{1,0:T(8,128)(2,1)S(1)}, u32[]{:S(2)}, u32[]{:S(2)}) collective-permute-start(bf16[128,2048]{1,0:T(8,128)(2,1)} %collective-permute-done.2), channel_id=1, source_target_pairs={{0,4},{4,0},{1,5},{5,1},{2,6},{6,2},{3,7},{7,3},{8,12},{12,8},{9,1... | collective-permute-start | bytes 1572872 | tf_op jit(solution)/shard_map/ppermute | solution.py:71
  111.5 38.4 %collective-permute-start.22 = (bf16[144,2048]{1,0:T(8,128)(2,1)}, bf16[144,2048]{1,0:T(8,128)(2,1)S(1)}, u32[]{:S(2)}, u32[]{:S(2)}) collective-permute-start(bf16[144,2048]{1,0:T(8,128)(2,1)} %collective-permute-done), channel_id=1, source_target_pairs={{0,2},{1,3},{2,0},{3,1},{4,6},{5,7},{6,4},{7,5},{8,10},{9,11},{10,... | collective-permute-start | bytes 1769480 | tf_op jit(solution)/shard_map/ppermute | solution.py:71
  114.9 28.5 %collective-permute-start.15 = (bf16[256,2048]{1,0:T(8,128)(2,1)}, bf16[256,2048]{1,0:T(8,128)(2,1)S(1)}, u32[]{:S(2)}, u32[]{:S(2)}) collective-permute-start(bf16[256,2048]{1,0:T(8,128)(2,1)} %all-gather.9.cloned.1.call-done), channel_id=1, source_target_pairs={{0,1},{1,0},{2,3},{3,2},{4,5},{5,4},{6,7},{7,6},{8,9},{9,8},{10,11... | collective-permute-start | bytes 3145736 | tf_op jit(solution)/shard_map/ppermute | solution.py:71
  150.7 22.3 %collective-permute-start.19 = (bf16[128,2048]{1,0:T(8,128)(2,1)}, bf16[128,2048]{1,0:T(8,128)(2,1)}, u32[]{:S(2)}, u32[]{:S(2)}) collective-permute-start(bf16[128,2048]{1,0:T(8,128)(2,1)} %get-tuple-element.122), channel_id=1, source_target_pairs={{0,2},{1,3},{2,0},{3,1},{4,6},{5,7},{6,4},{7,5},{8,10},{9,11},{10,... | collective-permute-start | bytes 1572872 | tf_op jit(solution)/shard_map/ppermute | solution.py:71
  152.2 36.9 %collective-permute-start.16 = (bf16[144,2048]{1,0:T(8,128)(2,1)}, bf16[144,2048]{1,0:T(8,128)(2,1)S(1)}, u32[]{:S(2)}, u32[]{:S(2)}) collective-permute-start(bf16[144,2048]{1,0:T(8,128)(2,1)} %get-tuple-element.120), channel_id=1, source_target_pairs={{0,4},{4,0},{1,5},{5,1},{2,6},{6,2},{3,7},{7,3},{8,12},{12,8},{9,1... | collective-permute-start | bytes 1769480 | tf_op jit(solution)/shard_map/ppermute | solution.py:71
  162.6 24.9 %collective-permute-start.21 = (bf16[128,2048]{1,0:T(8,128)(2,1)}, bf16[128,2048]{1,0:T(8,128)(2,1)}, u32[]{:S(2)}, u32[]{:S(2)}) collective-permute-start(bf16[128,2048]{1,0:T(8,128)(2,1)} %add_convert_fusion.11), channel_id=1, source_target_pairs={{0,4},{4,0},{1,5},{5,1},{2,6},{6,2},{3,7},{7,3},{8,12},{12,8},{9,1... | collective-permute-start | bytes 1572872 | tf_op jit(solution)/shard_map/ppermute | solution.py:71
  164.8 24.4 %collective-permute-start.18 = (bf16[144,2048]{1,0:T(8,128)(2,1)S(1)}, bf16[144,2048]{1,0:T(8,128)(2,1)}, u32[]{:S(2)}, u32[]{:S(2)}) collective-permute-start(bf16[144,2048]{1,0:T(8,128)(2,1)S(1)} %add_convert_fusion.8), channel_id=1, source_target_pairs={{0,2},{1,3},{2,0},{3,1},{4,6},{5,7},{6,4},{7,5},{8,10},{9,11},{10,... | collective-permute-start | bytes 1769480 | tf_op jit(solution)/shard_map/ppermute | solution.py:71
  194.8 46.3 %collective-permute-start.29 = (bf16[2048,1024]{1,0:T(8,128)(2,1)}, bf16[2048,1024]{1,0:T(8,128)(2,1)}, u32[]{:S(2)}, u32[]{:S(2)}) collective-permute-start(bf16[2048,1024]{1,0:T(8,128)(2,1)} %gate.17), channel_id=1, source_target_pairs={{0,1},{1,0},{2,3},{3,2},{4,5},{5,4},{6,7},{7,6},{8,9},{9,8},{10,11... | collective-permute-start | bytes 12582920 | tf_op jit(solution)/shard_map/ppermute | solution.py:71
  201.8 24.4 %collective-permute-start.24 = (bf16[128,2048]{1,0:T(8,128)(2,1)S(1)}, bf16[128,2048]{1,0:T(8,128)(2,1)}, u32[]{:S(2)}, u32[]{:S(2)}) collective-permute-start(bf16[128,2048]{1,0:T(8,128)(2,1)S(1)} %slice.380), channel_id=1, source_target_pairs={{0,4},{4,0},{1,5},{5,1},{2,6},{6,2},{3,7},{7,3},{8,12},{12,8},{9,1... | collective-permute-start | bytes 1572872 | tf_op jit(solution)/shard_map/ppermute | solution.py:71
  204.6 222.2 %reduce-scatter.5.cloned.1.call-start = ((), (), s32[]{:S(2)}) async-start(), calls=%async_computation.8 | async-start | bytes 5242880 | tf_op jit(solution)/shard_map/reduce_scatter | solution.py:675
  205.1 23.0 %collective-permute-start.25 = (bf16[144,2048]{1,0:T(8,128)(2,1)S(1)}, bf16[144,2048]{1,0:T(8,128)(2,1)S(1)}, u32[]{:S(2)}, u32[]{:S(2)}) collective-permute-start(bf16[144,2048]{1,0:T(8,128)(2,1)S(1)} %slice.379), channel_id=1, source_target_pairs={{0,2},{1,3},{2,0},{3,1},{4,6},{5,7},{6,4},{7,5},{8,10},{9,11},{10,... | collective-permute-start | bytes 1769480 | tf_op jit(solution)/shard_map/ppermute | solution.py:71
  215.1 25.2 %collective-permute-start.28 = (bf16[128,2048]{1,0:T(8,128)(2,1)S(1)}, bf16[128,2048]{1,0:T(8,128)(2,1)S(1)}, u32[]{:S(2)}, u32[]{:S(2)}) collective-permute-start(bf16[128,2048]{1,0:T(8,128)(2,1)S(1)} %collective-permute-done.26), channel_id=1, source_target_pairs={{0,4},{4,0},{1,5},{5,1},{2,6},{6,2},{3,7},{7,3},{8,12},{12,8},{9,1... | collective-permute-start | bytes 1572872 | tf_op jit(solution)/shard_map/ppermute | solution.py:71
  215.6 23.8 %collective-permute-start.27 = (bf16[144,2048]{1,0:T(8,128)(2,1)S(1)}, bf16[144,2048]{1,0:T(8,128)(2,1)S(1)}, u32[]{:S(2)}, u32[]{:S(2)}) collective-permute-start(bf16[144,2048]{1,0:T(8,128)(2,1)S(1)} %collective-permute-done.23), channel_id=1, source_target_pairs={{0,2},{1,3},{2,0},{3,1},{4,6},{5,7},{6,4},{7,5},{8,10},{9,11},{10,... | collective-permute-start | bytes 1769480 | tf_op jit(solution)/shard_map/ppermute | solution.py:71
  293.4 242.6 %reduce-scatter.7.cloned.1.call-start = ((), (), s32[]{:S(2)}) async-start(), calls=%async_computation.9 | async-start | bytes 5242880 | tf_op jit(solution)/shard_map/reduce_scatter | solution.py:695
  308.1 41.1 %collective-permute-start.35 = (bf16[128,2048]{1,0:T(8,128)(2,1)}, bf16[128,2048]{1,0:T(8,128)(2,1)S(1)}, u32[]{:S(2)}, u32[]{:S(2)}) collective-permute-start(bf16[128,2048]{1,0:T(8,128)(2,1)} %get-tuple-element.118), channel_id=1, source_target_pairs={{0,2},{1,3},{2,0},{3,1},{4,6},{5,7},{6,4},{7,5},{8,10},{9,11},{10,... | collective-permute-start | bytes 1572872 | tf_op jit(solution)/shard_map/ppermute | solution.py:71
  309.7 24.4 %collective-permute-start.36 = (bf16[128,2048]{1,0:T(8,128)(2,1)}, bf16[128,2048]{1,0:T(8,128)(2,1)}, u32[]{:S(2)}, u32[]{:S(2)}) collective-permute-start(bf16[128,2048]{1,0:T(8,128)(2,1)} %get-tuple-element.119), channel_id=1, source_target_pairs={{0,2},{1,3},{2,0},{3,1},{4,6},{5,7},{6,4},{7,5},{8,10},{9,11},{10,... | collective-permute-start | bytes 1572872 | tf_op jit(solution)/shard_map/ppermute | solution.py:71
  310.2 44.5 %collective-permute-start.32 = (bf16[144,2048]{1,0:T(8,128)(2,1)S(1)}, bf16[144,2048]{1,0:T(8,128)(2,1)S(1)}, u32[]{:S(2)}, u32[]{:S(2)}) collective-permute-start(bf16[144,2048]{1,0:T(8,128)(2,1)S(1)} %get-tuple-element.116), channel_id=1, source_target_pairs={{0,4},{4,0},{1,5},{5,1},{2,6},{6,2},{3,7},{7,3},{8,12},{12,8},{9,1... | collective-permute-start | bytes 1769480 | tf_op jit(solution)/shard_map/ppermute | solution.py:71
  311.7 37.5 %collective-permute-start.33 = (bf16[144,2048]{1,0:T(8,128)(2,1)S(1)}, bf16[144,2048]{1,0:T(8,128)(2,1)S(1)}, u32[]{:S(2)}, u32[]{:S(2)}) collective-permute-start(bf16[144,2048]{1,0:T(8,128)(2,1)S(1)} %get-tuple-element.117), channel_id=1, source_target_pairs={{0,4},{4,0},{1,5},{5,1},{2,6},{6,2},{3,7},{7,3},{8,12},{12,8},{9,1... | collective-permute-start | bytes 1769480 | tf_op jit(solution)/shard_map/ppermute | solution.py:71
  394.2 32.6 %collective-permute-start.44 = (bf16[2048,1024]{1,0:T(8,128)(2,1)}, bf16[2048,1024]{1,0:T(8,128)(2,1)}, u32[]{:S(2)}, u32[]{:S(2)}) collective-permute-start(bf16[2048,1024]{1,0:T(8,128)(2,1)} %convolution_convert_fusion.4), channel_id=1, source_target_pairs={{0,1},{1,0},{2,3},{3,2},{4,5},{5,4},{6,7},{7,6},{8,9},{9,8},{10,11... | collective-permute-start | bytes 12582920 | tf_op jit(solution)/shard_map/ppermute | solution.py:71
  398.8 25.6 %collective-permute-start.40 = (bf16[144,2048]{1,0:T(8,128)(2,1)S(1)}, bf16[144,2048]{1,0:T(8,128)(2,1)}, u32[]{:S(2)}, u32[]{:S(2)}) collective-permute-start(bf16[144,2048]{1,0:T(8,128)(2,1)S(1)} %copy-done.34), channel_id=1, source_target_pairs={{0,2},{1,3},{2,0},{3,1},{4,6},{5,7},{6,4},{7,5},{8,10},{9,11},{10,... | collective-permute-start | bytes 1769480 | tf_op jit(solution)/shard_map/ppermute | solution.py:71
  415.0 105.7 %collective-permute-start.55 = (bf16[1152,2048]{1,0:T(8,128)(2,1)}, bf16[1152,2048]{1,0:T(8,128)(2,1)}, u32[]{:S(2)}, u32[]{:S(2)}) collective-permute-start(bf16[1152,2048]{1,0:T(8,128)(2,1)} %constant_dynamic-update-slice_fusion), channel_id=1, source_target_pairs={{0,1},{1,0},{2,3},{3,2},{4,5},{5,4},{6,7},{7,6},{8,9},{9,8},{10,11... | collective-permute-start | bytes 14155784 | tf_op jit(solution)/shard_map/ppermute | solution.py:71
  415.0 23.8 %collective-permute-start.41 = (bf16[128,2048]{1,0:T(8,128)(2,1)}, bf16[128,2048]{1,0:T(8,128)(2,1)}, u32[]{:S(2)}, u32[]{:S(2)}) collective-permute-start(bf16[128,2048]{1,0:T(8,128)(2,1)} %get-tuple-element.114), channel_id=1, source_target_pairs={{0,2},{1,3},{2,0},{3,1},{4,6},{5,7},{6,4},{7,5},{8,10},{9,11},{10,... | collective-permute-start | bytes 1572872 | tf_op jit(solution)/shard_map/ppermute | solution.py:71
  437.0 167.6 %reduce-scatter.9.cloned.1.call-start = ((), (), s32[]{:S(2)}) async-start(), calls=%async_computation.10 | async-start | bytes 3932160 | tf_op jit(solution)/shard_map/reduce_scatter | solution.py:722
  448.9 24.9 %collective-permute-start.46 = (bf16[128,2048]{1,0:T(8,128)(2,1)S(1)}, bf16[128,2048]{1,0:T(8,128)(2,1)}, u32[]{:S(2)}, u32[]{:S(2)}) collective-permute-start(bf16[128,2048]{1,0:T(8,128)(2,1)S(1)} %slice.397), channel_id=1, source_target_pairs={{0,4},{4,0},{1,5},{5,1},{2,6},{6,2},{3,7},{7,3},{8,12},{12,8},{9,1... | collective-permute-start | bytes 1572872 | tf_op jit(solution)/shard_map/ppermute | solution.py:71
  450.7 24.2 %collective-permute-start.47 = (bf16[144,2048]{1,0:T(8,128)(2,1)S(1)}, bf16[144,2048]{1,0:T(8,128)(2,1)S(1)}, u32[]{:S(2)}, u32[]{:S(2)}) collective-permute-start(bf16[144,2048]{1,0:T(8,128)(2,1)S(1)} %slice.396), channel_id=1, source_target_pairs={{0,2},{1,3},{2,0},{3,1},{4,6},{5,7},{6,4},{7,5},{8,10},{9,11},{10,... | collective-permute-start | bytes 1769480 | tf_op jit(solution)/shard_map/ppermute | solution.py:71
  462.3 22.2 %collective-permute-start.50 = (bf16[128,2048]{1,0:T(8,128)(2,1)S(1)}, bf16[128,2048]{1,0:T(8,128)(2,1)S(1)}, u32[]{:S(2)}, u32[]{:S(2)}) collective-permute-start(bf16[128,2048]{1,0:T(8,128)(2,1)S(1)} %collective-permute-done.48), channel_id=1, source_target_pairs={{0,4},{4,0},{1,5},{5,1},{2,6},{6,2},{3,7},{7,3},{8,12},{12,8},{9,1... | collective-permute-start | bytes 1572872 | tf_op jit(solution)/shard_map/ppermute | solution.py:71
  488.8 30.4 %collective-permute-start.53 = (bf16[256,2048]{1,0:T(8,128)(2,1)}, bf16[256,2048]{1,0:T(8,128)(2,1)S(1)}, u32[]{:S(2)}, u32[]{:S(2)}) collective-permute-start(bf16[256,2048]{1,0:T(8,128)(2,1)} %gate.24.refs_0_), channel_id=1, source_target_pairs={{0,2},{1,3},{2,0},{3,1},{4,6},{5,7},{6,4},{7,5},{8,10},{9,11},{10,... | collective-permute-start | bytes 3145736 | tf_op jit(solution)/shard_map/ppermute | solution.py:71
  490.6 28.7 %collective-permute-start.52 = (bf16[256,2048]{1,0:T(8,128)(2,1)}, bf16[256,2048]{1,0:T(8,128)(2,1)}, u32[]{:S(2)}, u32[]{:S(2)}) collective-permute-start(bf16[256,2048]{1,0:T(8,128)(2,1)} %gate.24.refs_0_), channel_id=1, source_target_pairs={{0,4},{4,0},{1,5},{5,1},{2,6},{6,2},{3,7},{7,3},{8,12},{12,8},{9,1... | collective-permute-start | bytes 3145736 | tf_op jit(solution)/shard_map/ppermute | solution.py:71
  520.2 25.9 %collective-permute-start.54 = (bf16[1152,768]{1,0:T(8,128)(2,1)}, bf16[1152,768]{1,0:T(8,128)(2,1)}, u32[]{:S(2)}, u32[]{:S(2)}) collective-permute-start(bf16[1152,768]{1,0:T(8,128)(2,1)} %get-tuple-element.63), channel_id=1, source_target_pairs={{0,1},{1,0},{2,3},{3,2},{4,5},{5,4},{6,7},{7,6},{8,9},{9,8},{10,11... | collective-permute-start | bytes 5308424 | tf_op jit(solution)/shard_map/ppermute | solution.py:71
  520.2 25.9 %collective-permute-start.56 = (bf16[256,2048]{1,0:T(8,128)(2,1)}, bf16[256,2048]{1,0:T(8,128)(2,1)}, u32[]{:S(2)}, u32[]{:S(2)}) collective-permute-start(bf16[256,2048]{1,0:T(8,128)(2,1)} %collective-permute-done.52.refs_2_.refs_1_), channel_id=1, source_target_pairs={{0,2},{1,3},{2,0},{3,1},{4,6},{5,7},{6,4},{7,5},{8,10},{9,11},{10,... | collective-permute-start | bytes 3145736 | tf_op jit(solution)/shard_map/ppermute | solution.py:71
  536.0 101.1 %reduce-scatter.11.cloned.1.call-start = ((), (), s32[]{:S(2)}) async-start(), calls=%async_computation.11 | async-start | bytes 1638400 | tf_op jit(solution)/shard_map/reduce_scatter | solution.py:794
  559.4 27.1 %collective-permute-start.57 = (bf16[144,2048]{1,0:T(8,128)(2,1)}, bf16[144,2048]{1,0:T(8,128)(2,1)}, u32[]{:S(2)}, u32[]{:S(2)}) collective-permute-start(bf16[144,2048]{1,0:T(8,128)(2,1)} %get-tuple-element.108), channel_id=1, source_target_pairs={{0,4},{4,0},{1,5},{5,1},{2,6},{6,2},{3,7},{7,3},{8,12},{12,8},{9,1... | collective-permute-start | bytes 1769480 | tf_op jit(solution)/shard_map/ppermute | solution.py:71
  560.9 25.6 %collective-permute-start.61 = (bf16[144,2048]{1,0:T(8,128)(2,1)S(1)}, bf16[144,2048]{1,0:T(8,128)(2,1)}, u32[]{:S(2)}, u32[]{:S(2)}) collective-permute-start(bf16[144,2048]{1,0:T(8,128)(2,1)S(1)} %get-tuple-element.109), channel_id=1, source_target_pairs={{0,2},{1,3},{2,0},{3,1},{4,6},{5,7},{6,4},{7,5},{8,10},{9,11},{10,... | collective-permute-start | bytes 1769480 | tf_op jit(solution)/shard_map/ppermute | solution.py:71
  563.9 29.5 %collective-permute-start.63 = (bf16[256,2048]{1,0:T(8,128)(2,1)}, bf16[256,2048]{1,0:T(8,128)(2,1)S(1)}, u32[]{:S(2)}, u32[]{:S(2)}) collective-permute-start(bf16[256,2048]{1,0:T(8,128)(2,1)} %convolution_convert_fusion.6), channel_id=1, source_target_pairs={{0,1},{1,0},{2,3},{3,2},{4,5},{5,4},{6,7},{7,6},{8,9},{9,8},{10,11... | collective-permute-start | bytes 3145736 | tf_op jit(solution)/shard_map/ppermute | solution.py:71
  607.3 95.3 %all-gather.15.cloned.1.call-start = ((), (), s32[]{:S(2)}) async-start(), calls=%async_computation.12 | async-start | bytes 9437184 | tf_op jit(solution)/shard_map/all_gather | solution.py:788
  643.1 36.5 %collective-permute-start.80 = (bf16[512,768]{1,0:T(8,128)(2,1)}, bf16[512,768]{1,0:T(8,128)(2,1)S(1)}, u32[]{:S(2)}, u32[]{:S(2)}) collective-permute-start(bf16[512,768]{1,0:T(8,128)(2,1)} %get-tuple-element.68.refs_1_), channel_id=1, source_target_pairs={{0,2},{1,3},{2,0},{3,1},{4,6},{5,7},{6,4},{7,5},{8,10},{9,11},{10,... | collective-permute-start | bytes 2359304 | tf_op jit(solution)/shard_map/ppermute | solution.py:71
  660.8 25.3 %collective-permute-start.81 = (bf16[512,768]{1,0:T(8,128)(2,1)}, bf16[512,768]{1,0:T(8,128)(2,1)S(1)}, u32[]{:S(2)}, u32[]{:S(2)}) collective-permute-start(bf16[512,768]{1,0:T(8,128)(2,1)} %reduce-scatter.9.cloned.1.call-done.refs_1_.refs_0_), channel_id=1, source_target_pairs={{0,1},{1,0},{2,3},{3,2},{4,5},{5,4},{6,7},{7,6},{8,9},{9,8},{10,11... | collective-permute-start | bytes 2359304 | tf_op jit(solution)/shard_map/ppermute | solution.py:71
  661.1 25.0 %collective-permute-start.82 = (bf16[512,768]{1,0:T(8,128)(2,1)}, bf16[512,768]{1,0:T(8,128)(2,1)S(1)}, u32[]{:S(2)}, u32[]{:S(2)}) collective-permute-start(bf16[512,768]{1,0:T(8,128)(2,1)} %get-tuple-element.68.refs_1_), channel_id=1, source_target_pairs={{0,1},{1,0},{2,3},{3,2},{4,5},{5,4},{6,7},{7,6},{8,9},{9,8},{10,11... | collective-permute-start | bytes 2359304 | tf_op jit(solution)/shard_map/ppermute | solution.py:71
  665.6 20.6 %collective-permute-start.83 = (bf16[512,768]{1,0:T(8,128)(2,1)}, bf16[512,768]{1,0:T(8,128)(2,1)S(1)}, u32[]{:S(2)}, u32[]{:S(2)}) collective-permute-start(bf16[512,768]{1,0:T(8,128)(2,1)} %get-tuple-element.69.refs_2_), channel_id=1, source_target_pairs={{0,1},{1,0},{2,3},{3,2},{4,5},{5,4},{6,7},{7,6},{8,9},{9,8},{10,11... | collective-permute-start | bytes 2359304 | tf_op jit(solution)/shard_map/ppermute | solution.py:71
  (122 other events, 1550.7 us)
Sparse Core Ops, SparseCore 0:
  20.2 63.2 all-gather.6
  85.7 26.6 all-gather.8
  114.5 80.2 all-gather.10
  204.8 78.3 all-gather.12
  293.5 75.4 reduce-scatter.4
  437.1 74.4 reduce-scatter.6
  536.2 58.7 reduce-scatter.8
  607.3 28.7 reduce-scatter.10
  638.0 64.5 all-gather.14
